TPU v7x, 768 devices: a whole 4x8x12 slice. The times are simulated.
768 devices in a mesh: ctx: 24 (over z, x_hi), tp: 32 (over x_lo, y, core).
Axes of the slice: x: 4 (x_hi: 2, x_lo: 2; x = x_hi * 2 + x_lo), y: 8, z: 12, core: 2. Of those that a mesh axis runs over, the one named last changes fastest.
Arguments:
- tokens: bfloat16 [6144, 4096], P('ctx', 'tp'), may hold values from -6 to 6
- cotangent: bfloat16 [6144, 4096], P('ctx', 'tp'), may hold values from -6 to 6
- in_weight: bfloat16 [4096, 3, 4096], P(None, None, 'tp'), may hold values from -0.09375 to 0.09375
- filter_taps: float32 [128, 4096], P(None, 'tp'), may hold values from -0.5 to 0.5
- out_weight: bfloat16 [4096, 4096], P('tp'), may hold values from -0.09375 to 0.09375
- segment_ids: int32 [6144], replicated, may hold values from 0 to 47, never falling along the last dimension, each value on 1 to 512 neighbouring positions
Outputs:
- block_out: bfloat16 [6144, 4096], P('ctx', 'tp')
- input_grad: bfloat16 [6144, 4096], P('ctx', 'tp')
Inputs may be any that keep to these rules, and one draw needn't show every extreme that they name: `segment_ids`: never falls along the sequence; every number 0 to 47 names one contig of 1 to 512 positions, and at least one contig has exactly 512.
All inputs are finite; a program needn't handle non-finite values.
Results may differ from a plain program's by a relative error of at most 0.024.
Values may be sent and summed in bfloat16 or wider, within the bound.
No kernel may reach another device: no remote copies, remote signals or barrier semaphores. Data moves between devices by JAX's collectives and lax.ppermute only.
A program may use at most 32 MiB of HBM per device.

v0:
```python
import jax
import jax.numpy as jnp
from jax import lax
from jax.sharding import PartitionSpec as P


def side_by_side(arrays, axis, dim, along):
    both = jnp.concatenate(arrays, axis=along)
    result, at, outs = (lax.all_gather(both, axis, axis=dim, tiled=True), 0, [])
    for a in arrays:
        outs.append(lax.slice_in_dim(result, at, at + a.shape[along], axis=along))
        at += a.shape[along]
    return tuple(outs)


def passed_along(block, axis, distance):
    devices = range(lax.axis_size(axis))
    route = [(i - distance, i) for i in devices if i - distance in devices]
    return lax.ppermute(block, axis, route)


def split_up(shard, dim, size):
    dims = shard.shape
    blocks = shard.reshape(*dims[:dim], size, dims[dim] // size, *dims[dim + 1 :])
    return jnp.moveaxis(blocks, dim, 0)


def summed_on_arrival(shard, axis, dim):
    blocks = split_up(shard, dim, lax.axis_size(axis))
    arrived = lax.all_to_all(blocks, axis, split_axis=0, concat_axis=0, tiled=True)
    return arrived.astype(jnp.float32).sum(axis=0)


def shards(tokens, cotangent, in_weight, filter_taps, out_weight, segment_ids):
    width = in_weight.shape[0]
    chans = in_weight.shape[2]
    rows = tokens.shape[0]
    taps = filter_taps.shape[0]
    margin = taps - 1
    w_in = in_weight.reshape(width, 3 * chans)
    full_rows, full_grad = side_by_side((tokens, cotangent), "tp", 1, 0)
    projected = jnp.dot(full_rows, w_in, preferred_element_type=jnp.float32).astype(jnp.bfloat16)
    mix = (
        projected[:, chans : 2 * chans].astype(jnp.float32)
        * projected[:, 2 * chans :].astype(jnp.float32)
    ).astype(jnp.bfloat16)
    prior_mix = passed_along(mix[rows - margin :], "ctx", 1)
    query = projected[:, :chans].astype(jnp.float32)
    key_part = projected[:, chans : 2 * chans].astype(jnp.float32)
    value_part = projected[:, 2 * chans :].astype(jnp.float32)
    base = lax.axis_index("ctx") * rows
    positions = base + jnp.arange(rows + margin, dtype=jnp.int32)
    seg_padded = jnp.concatenate([segment_ids, jnp.broadcast_to(segment_ids[-1:], (margin,))])
    seg_here = lax.dynamic_slice_in_dim(seg_padded, base, rows + margin)
    first = jnp.sum((segment_ids[None, :] < seg_here[:, None]).astype(jnp.int32), axis=1)
    reach_all = positions - first
    reach_here = reach_all[:rows]
    extended = jnp.concatenate([prior_mix, mix], 0).astype(jnp.float32)
    conv = jnp.zeros((rows, chans), jnp.float32)
    for shift_by in range(taps):
        piece = extended[margin - shift_by : margin - shift_by + rows]
        keep = (shift_by <= reach_here)[:, None].astype(jnp.float32)
        conv = conv + filter_taps[shift_by][None, :] * piece * keep
    gated = (query * conv).astype(jnp.bfloat16)
    out_term = jnp.dot(gated, out_weight, preferred_element_type=jnp.float32)
    out_sum = summed_on_arrival(out_term.astype(jnp.bfloat16), "tp", 1)
    dgated = lax.dot_general(
        full_grad, out_weight, (((1,), (1,)), ((), ())), preferred_element_type=jnp.float32
    )
    dquery = dgated * conv
    dconv = (dgated * query).astype(jnp.bfloat16)
    after = passed_along(dconv[:margin], "ctx", -1)
    ext_grad = jnp.concatenate([dconv, after], 0).astype(jnp.float32)
    dmix = jnp.zeros((rows, chans), jnp.float32)
    for shift_by in range(taps):
        piece = ext_grad[shift_by : shift_by + rows]
        keep = (shift_by <= reach_all[shift_by : shift_by + rows])[:, None].astype(jnp.float32)
        dmix = dmix + filter_taps[shift_by][None, :] * piece * keep
    dproj = jnp.concatenate([dquery, dmix * value_part, dmix * key_part], axis=1).astype(
        jnp.bfloat16
    )
    grad_term = lax.dot_general(
        dproj, w_in, (((1,), (1,)), ((), ())), preferred_element_type=jnp.float32
    )
    grad_sum = summed_on_arrival(grad_term.astype(jnp.bfloat16), "tp", 1)
    return (out_sum.astype(jnp.bfloat16), grad_sum.astype(jnp.bfloat16))


def solution(mesh):
    placed = (
        P("ctx", "tp"),
        P("ctx", "tp"),
        P(None, None, "tp"),
        P(None, "tp"),
        P("tp", None),
        P(),
    )
    return jax.shard_map(
        shards,
        mesh=mesh,
        in_specs=placed,
        out_specs=(P("ctx", "tp"), P("ctx", "tp")),
        check_vma=False,
    )
```

profile of v0, /device:TPU:12, one launch (start us, length us, event | category | flops | bytes accessed | tf_op | source)
XLA Modules:
  0.0 252.1 jit_solution(12664683371864543525)
XLA Ops:
  7.2 1.6 pad_maximum_fusion
  8.9 4.8 %copy.12 = bf16[4096,3,128]{0,2,1:T(8,128)(2,1)} copy(bf16[4096,3,128]{2,0,1:T(8,128)(2,1)} %param.8) | data formatting | bytes 6291456 | tf_op args[2]
  13.7 0.6 slice.1698
  14.3 0.7 pad_dynamic-slice_fusion
  15.0 1.3 convert_reduce_fusion
  16.5 0.1 compare_convert_fusion.95
  16.6 0.1 compare_convert_fusion.126
  16.7 0.1 compare_convert_fusion.125
  16.8 0.1 compare_convert_fusion.124
  16.9 0.1 compare_convert_fusion.123
  17.0 0.1 compare_convert_fusion.122
  17.3 77.5 %all-gather.2.cloned.1.call-done = bf16[512,4096]{1,0:T(8,128)(2,1)} async-done(((bf16[512,128]{1,0:T(8,128)(2,1)}), bf16[512,4096]{1,0:T(8,128)(2,1)}) %all-gather.2.cloned.1.call-update) | async-done | bytes 4194320 | tf_op jit(solution)/shard_map/all_gather | solution.py:9
  94.7 3.9 %fusion.6 = bf16[256,384]{1,0:T(8,128)(2,1)S(1)} fusion(bf16[4096,384]{0,1:T(8,128)(2,1)} %bitcast.278, bf16[512,4096]{1,0:T(8,128)(2,1)} %all-gather.2.cloned.1.call-done), kind=kOutput, calls=%fused_computation.11 | convolution fusion | flops 805404672 | bytes 5439488 | tf_op jit(solution)/shard_map/dot_general | solution.py:42
  98.7 0.7 fusion.15
  99.4 2.3 collective-permute-start.1
  101.8 5.9 %collective-permute-done.1 = bf16[127,128]{1,0:T(8,128)(2,1)S(1)} collective-permute-done((bf16[127,128]{1,0:T(8,128)(2,1)S(1)}, bf16[127,128]{1,0:T(8,128)(2,1)S(1)}, u32[]{:S(2)}, u32[]{:S(2)}) %collective-permute-start.1) | collective-permute-done | bytes 32544 | tf_op jit(solution)/shard_map/ppermute | solution.py:19
  107.7 1.7 fusion.212
  109.4 5.0 %fusion.18 = (bf16[256,128]{1,0:T(8,128)(2,1)S(1)}, f32[256,128]{1,0:T(8,128)S(1)}) fusion(bf16[256,384]{1,0:T(8,128)(2,1)S(1)} %fusion.6, f32[256]{0:T(256)S(1)} %get-tuple-element.137, f32[383,128]{1,0:T(8,128)S(1)} %maximum_convert_fusion.1, f32[128]{0:T(128)S(1)} %get-tuple-element.134, f32[256]{0:T(256)S(1)} %get-tuple-element.138, ...), kind=kLoop, calls=%fused_computation.26 | loop fusion | flops 9535488 | bytes 13123584 | tf_op jit(solution)/shard_map/convert.3
  114.5 2.5 collective-permute-start
  117.0 4.8 %collective-permute-done = bf16[127,128]{1,0:T(8,128)(2,1)S(1)} collective-permute-done((bf16[127,128]{1,0:T(8,128)(2,1)S(1)}, bf16[127,128]{1,0:T(8,128)(2,1)S(1)}, u32[]{:S(2)}, u32[]{:S(2)}) %collective-permute-start) | collective-permute-done | bytes 32544 | tf_op jit(solution)/shard_map/ppermute | solution.py:19
  121.8 1.7 fusion.467
  123.6 5.0 %multiply_convert_fusion = (bf16[256,128]{1,0:T(8,128)(2,1)S(1)}, f32[256,128]{1,0:T(8,128)S(1)}) fusion(f32[256,128]{1,0:T(8,128)S(1)} %get-tuple-element.392, f32[256]{0:T(256)S(1)} %get-tuple-element.390, f32[383,128]{1,0:T(8,128)S(1)} %maximum_convert_fusion, f32[128]{0:T(128)S(1)} %get-tuple-element.134, f32[256]{0:T(256)S(1)} %get-tuple-element.389, ...), kind=kLoop, calls=%fused_computation.794 | loop fusion | flops 9502720 | bytes 13189120 | tf_op jit(solution)/shard_map/convert.2
  128.6 0.7 fusion.5
  129.3 1.9 copy.20
  131.2 4.9 %all-to-all-start = ((bf16[32,256,128]{2,1,0:T(8,128)(2,1)}), bf16[32,256,128]{2,1,0:T(8,128)(2,1)S(1)}, u32[]{:S(2)}, u32[]{:S(2)}) async-start(bf16[32,256,128]{2,1,0:T(8,128)(2,1)} %bitcast.280), calls=%async_computation | async-start | bytes 4194304 | tf_op jit(solution)/shard_map/all_to_all | solution.py:30
  136.2 3.1 %fusion.4 = bf16[32,32,8,128]{3,2,1,0:T(8,128)(2,1)S(1)} fusion(bf16[4096,384]{0,1:T(8,128)(2,1)} %bitcast.279, bf16[256,128]{1,0:T(8,128)(2,1)S(1)} %get-tuple-element.6, bf16[256,128]{1,0:T(8,128)(2,1)S(1)} %get-tuple-element.4, bf16[256,128]{1,0:T(8,128)(2,1)S(1)} %get-tuple-element.2), kind=kOutput, calls=%fused_computation.9 | convolution fusion | flops 806944768 | bytes 5439488 | tf_op jit(solution)/shard_map/dot_general | solution.py:82
  139.3 1.9 copy.19
  141.2 46.4 %all-to-all-done = bf16[32,256,128]{2,1,0:T(8,128)(2,1)S(1)} async-done(((bf16[32,256,128]{2,1,0:T(8,128)(2,1)}), bf16[32,256,128]{2,1,0:T(8,128)(2,1)S(1)}, u32[]{:S(2)}, u32[]{:S(2)}) %all-to-all-start) | async-done | bytes 2097184 | tf_op jit(solution)/shard_map/all_to_all | solution.py:30
  187.6 4.5 %all-to-all-start.1 = ((bf16[32,256,128]{2,1,0:T(8,128)(2,1)}), bf16[32,256,128]{2,1,0:T(8,128)(2,1)}, u32[]{:S(2)}, u32[]{:S(2)}) async-start(bf16[32,256,128]{2,1,0:T(8,128)(2,1)} %bitcast.281), calls=%async_computation.1 | async-start | bytes 4194304 | tf_op jit(solution)/shard_map/all_to_all | solution.py:30
  192.2 0.9 reduce_sum.34
  193.1 49.6 %all-to-all-done.1 = bf16[32,256,128]{2,1,0:T(8,128)(2,1)} async-done(((bf16[32,256,128]{2,1,0:T(8,128)(2,1)}), bf16[32,256,128]{2,1,0:T(8,128)(2,1)}, u32[]{:S(2)}, u32[]{:S(2)}) %all-to-all-start.1) | async-done | bytes 2097184 | tf_op jit(solution)/shard_map/all_to_all | solution.py:30
  242.7 2.5 %reduce_sum.35 = bf16[256,128]{1,0:T(8,128)(2,1)} reduce(bf16[32,256,128]{2,1,0:T(8,128)(2,1)} %all-to-all-done.1, bf16[]{:T(256)} %constant.269.clone.1), dimensions={0}, to_apply=%region_2.0 | reduce | flops 1015808 | bytes 2162690 | tf_op jit(solution)/shard_map/reduce_sum | solution.py:31
  (31 shorter events, 0.4 us)
Async XLA Ops:
  7.2 91.5 %copy-start = (bf16[128,4096]{1,0:T(8,128)(2,1)S(1)}, bf16[128,4096]{1,0:T(8,128)(2,1)}, u32[]{:S(2)}) copy-start(bf16[128,4096]{1,0:T(8,128)(2,1)} %param.10) | copy-start | bytes 3145732
  7.2 87.6 %all-gather.2.cloned.1.call-start = ((), (), s32[]{:S(2)}) async-start(), calls=%async_computation.2 | async-start | bytes 4325376 | tf_op jit(solution)/shard_map/all_gather | solution.py:9
  8.9 4.8 %copy-start.1 = (s32[6144]{0:T(1024)S(1)}, s32[6144]{0:T(1024)}, u32[]{:S(2)}) copy-start(s32[6144]{0:T(1024)} %param.11) | copy-start | bytes 73732
  8.9 7.4 %copy-start.2 = (f32[128,128]{1,0:T(8,128)S(1)}, f32[128,128]{1,0:T(8,128)}, u32[]{:S(2)}) copy-start(f32[128,128]{1,0:T(8,128)} %param.9) | copy-start | bytes 196612
  94.7 4.0 %copy-start.3 = (bf16[512,4096]{1,0:T(8,128)(2,1)S(1)}, bf16[512,4096]{1,0:T(8,128)(2,1)}, u32[]{:S(2)}) copy-start(bf16[512,4096]{1,0:T(8,128)(2,1)} %all-gather.2.cloned.1.call-done) | copy-start | bytes 12582916
  99.4 8.2 %collective-permute-start.1 = (bf16[127,128]{1,0:T(8,128)(2,1)S(1)}, bf16[127,128]{1,0:T(8,128)(2,1)S(1)}, u32[]{:S(2)}, u32[]{:S(2)}) collective-permute-start(bf16[127,128]{1,0:T(8,128)(2,1)S(1)} %slice.2345), channel_id=1, source_target_pairs={{32,0},{64,32},{96,64},{128,96},{160,128},{192,160},{224,192},{256... | collective-permute-start | bytes 97544 | tf_op jit(solution)/shard_map/ppermute | solution.py:19
  114.5 7.3 %collective-permute-start = (bf16[127,128]{1,0:T(8,128)(2,1)S(1)}, bf16[127,128]{1,0:T(8,128)(2,1)S(1)}, u32[]{:S(2)}, u32[]{:S(2)}) collective-permute-start(bf16[127,128]{1,0:T(8,128)(2,1)S(1)} %slice.2215), channel_id=1, source_target_pairs={{0,32},{32,64},{64,96},{96,128},{128,160},{160,192},{192,224},{224... | collective-permute-start | bytes 97544 | tf_op jit(solution)/shard_map/ppermute | solution.py:19
  131.2 56.4 %all-to-all-start = ((bf16[32,256,128]{2,1,0:T(8,128)(2,1)}), bf16[32,256,128]{2,1,0:T(8,128)(2,1)S(1)}, u32[]{:S(2)}, u32[]{:S(2)}) async-start(bf16[32,256,128]{2,1,0:T(8,128)(2,1)} %bitcast.280), calls=%async_computation | async-start | bytes 4194304 | tf_op jit(solution)/shard_map/all_to_all | solution.py:30
  187.6 55.1 %all-to-all-start.1 = ((bf16[32,256,128]{2,1,0:T(8,128)(2,1)}), bf16[32,256,128]{2,1,0:T(8,128)(2,1)}, u32[]{:S(2)}, u32[]{:S(2)}) async-start(bf16[32,256,128]{2,1,0:T(8,128)(2,1)} %bitcast.281), calls=%async_computation.1 | async-start | bytes 4194304 | tf_op jit(solution)/shard_map/all_to_all | solution.py:30
Sparse Core Ops, SparseCore 0:
  10.3 84.3 all-gather.1
where the time goes:
time: 253 us; the launch traced here: 252 us
  waiting for transfers between devices  184 us (73%)
  other arithmetic  20.6 us (8%)
  starting transfers between devices  14.4 us (6%)
  between operations  14.4 us (6%)
  local copies, waits for them, and re-layouts  10 us (4%)
  matrix products  8.51 us (3%)
    all_to_all x2, waiting for transfers between devices, summed_on_arrival(): lax.all_to_all(blocks, axis, split_axis=0, concat_axis=0, tiled=True)  96 us
    all_gather x1, waiting for transfers between devices, side_by_side(): result, at, outs = (lax.all_gather(both, axis, axis=dim, tiled=True), 0, [])  77.5 us
    ppermute x2, waiting for transfers between devices, passed_along(): return lax.ppermute(block, axis, route)  10.6 us
    another operation x3, other arithmetic  10 us
    all_to_all x2, starting transfers between devices, summed_on_arrival(): lax.all_to_all(blocks, axis, split_axis=0, concat_axis=0, tiled=True)  9.49 us
  transfers between devices with their start and end apart: 5, of which 5 were waited for; matrix products, arithmetic and copies ran while one was open for 6% of the time, Pallas kernels for 0%

commit v1 on v0

v1 whole, which is shorter than its diff:
```python
import jax
import jax.numpy as jnp
from jax import lax
from jax.experimental import pallas as pl
from jax.experimental.pallas import tpu as pltpu
from jax.sharding import Mesh
from jax.sharding import PartitionSpec as P

X, Y, CORE = 2, 8, 2
SWAP = [(0, 1), (1, 0)]
LANES = 128
STRIP = 64
INTERPRET = False
BF, F32 = jnp.bfloat16, jnp.float32


def f32(a):
    return a.astype(F32)


def call(kernel, name, outs, scratch, flops, nbytes, *args):
    return pl.pallas_call(
        kernel,
        out_shape=[jax.ShapeDtypeStruct(s, d) for s, d in outs],
        in_specs=[pl.BlockSpec(memory_space=pltpu.SMEM)]
        + [pl.BlockSpec(memory_space=pltpu.VMEM)] * (len(args) - 1),
        out_specs=[pl.BlockSpec(memory_space=pltpu.VMEM)] * len(outs),
        scratch_shapes=scratch,
        cost_estimate=pl.CostEstimate(flops=flops, bytes_accessed=nbytes, transcendentals=0),
        compiler_params=pltpu.CompilerParams(vmem_limit_bytes=48 << 20),
        name=name,
        interpret=INTERPRET,
    )(*args)


def offset(pos, far, other, j):
    x = 1 - pos[0] if far else pos[0]
    core = 1 - pos[1] if other else pos[1]
    return pl.multiple_of(((x * Y + j) * CORE + core) * LANES, LANES)


def lay_out(pos, parts, whole):
    for at, part in enumerate(parts):
        for j in range(Y):
            whole[:, pl.ds(offset(pos, at // 2, at % 2, j), LANES)] = part[j]


def project(pos, t0, t1, t2, t3, w, q, k, v, mix, tail, whole):
    lay_out(pos, (t0, t1, t2, t3), whole)
    rhs = jnp.concatenate([w[0], w[1], w[2]], axis=1)
    proj = jnp.dot(whole[...], rhs, preferred_element_type=F32).astype(BF)
    q[...] = proj[:, :LANES]
    k[...] = proj[:, LANES : 2 * LANES]
    v[...] = proj[:, 2 * LANES :]
    product = (f32(proj[:, LANES : 2 * LANES]) * f32(proj[:, 2 * LANES :])).astype(BF)
    mix[...] = product
    tail[...] = product[-tail.shape[0] :]


def convolve(ext, limit, taps, shifted, back, result):
    total = ext.shape[0]
    for b in range(8):
        by = (total - b) % total if back else b
        shifted[b] = pltpu.roll(ext, by, 0) if by else ext
    n_taps = taps.shape[0]

    def strip(i, carry):
        at = pl.multiple_of(i * STRIP, STRIP)
        lim = limit[pl.ds(at, STRIP), :]

        def eight(a, acc):
            if back:
                start = pl.multiple_of(at + 8 * a, 8)
            else:
                start = pl.multiple_of(at + n_taps - 8 * a, 8)
            for b in range(8):
                s = 8 * a + b
                piece = shifted[b, pl.ds(start, STRIP), :]
                acc = acc + jnp.where(lim >= s, piece, 0.0) * taps[pl.ds(s, 1), :]
            return acc

        acc = lax.fori_loop(0, n_taps // 8, eight, jnp.zeros((STRIP, LANES), F32))
        result[pl.ds(at, STRIP), :] = acc
        return carry

    lax.fori_loop(0, limit.shape[0] // STRIP, strip, 0)


def forward(pos, prior, mix, q, reach, taps, w, conv, o0, o1, o2, o3, shifted):
    ext = jnp.concatenate([f32(prior[...]), f32(mix[...])], axis=0)
    convolve(ext, reach, taps, shifted, False, conv)
    gated = (f32(q[...]) * conv[...]).astype(BF)
    for far in range(2):
        own, other = (o0, o1) if far == 0 else (o2, o3)
        for j in range(Y):
            rhs = jnp.concatenate(
                [w[:, pl.ds(offset(pos, far, o, j), LANES)] for o in range(2)], axis=1
            )
            term = jnp.dot(gated, rhs, preferred_element_type=F32).astype(BF)
            own[j] = term[:, :LANES]
            other[j] = term[:, LANES:]


def back_gate(pos, c0, c1, c2, c3, w, q, conv, dq, dconv, head, whole):
    lay_out(pos, (c0, c1, c2, c3), whole)
    dgated = lax.dot_general(
        whole[...], w[...], (((1,), (1,)), ((), ())), preferred_element_type=F32
    )
    dq[...] = (dgated * conv[...]).astype(BF)
    d = (dgated * f32(q[...])).astype(BF)
    dconv[...] = d
    head[...] = d[: head.shape[0]]


def back_project(pos, dconv, after, k, v, dq, rem, taps, w, g0, g1, g2, g3, shifted, dmix):
    ext = jnp.concatenate([f32(dconv[...]), f32(after[...])], axis=0)
    convolve(ext, rem, taps, shifted, True, dmix)
    dk = (dmix[...] * f32(v[...])).astype(BF)
    dv = (dmix[...] * f32(k[...])).astype(BF)
    dproj = jnp.concatenate([dq[...], dk, dv], axis=1)
    for far in range(2):
        own, other = (g0, g1) if far == 0 else (g2, g3)
        for j in range(Y):
            rhs = jnp.concatenate(
                [
                    jnp.concatenate(
                        [w[b, pl.ds(offset(pos, far, o, j), LANES), :] for b in range(3)], axis=1
                    )
                    for o in range(2)
                ],
                axis=0,
            )
            term = lax.dot_general(
                dproj, rhs, (((1,), (1,)), ((), ())), preferred_element_type=F32
            ).astype(BF)
            own[j] = term[:, :LANES]
            other[j] = term[:, LANES:]


def passed_along(block, distance):
    devices = range(lax.axis_size("ctx"))
    route = [(i - distance, i) for i in devices if i - distance in devices]
    return lax.ppermute(block, "ctx", route)


def spread_y(block):
    copies = jnp.broadcast_to(block[None], (Y,) + block.shape)
    return lax.all_to_all(copies, "y", split_axis=0, concat_axis=0, tiled=True)


def quarters(own):
    far = lax.ppermute(own, "x", SWAP)
    return own, lax.ppermute(own, "core", SWAP), far, lax.ppermute(far, "core", SWAP)


def summed(own_own, own_other, far_own, far_other):
    got = lax.ppermute(far_other, "core", SWAP)
    sent = (f32(far_own) + f32(got)).astype(BF)
    near = lax.ppermute(own_other, "core", SWAP)
    got = lax.ppermute(sent, "x", SWAP)
    half = (f32(own_own) + f32(near) + f32(got)).astype(BF)
    arrived = lax.all_to_all(half, "y", split_axis=0, concat_axis=0, tiled=True)
    return f32(arrived).sum(axis=0).astype(BF)


def shards(tokens, cotangent, in_weight, filter_taps, out_weight, segment_ids):
    width, _, chans = in_weight.shape
    rows = tokens.shape[0]
    taps = filter_taps.shape[0]
    w3 = in_weight.transpose(1, 0, 2)
    pos = jnp.stack([lax.axis_index("x"), lax.axis_index("core")]).astype(jnp.int32)
    t_quarters = quarters(spread_y(tokens))
    c_quarters = quarters(spread_y(cotangent))

    base = lax.axis_index("ctx") * rows
    positions = base + jnp.arange(rows, dtype=jnp.int32)
    seg_here = lax.dynamic_slice_in_dim(segment_ids, base, rows)
    first = jnp.sum((segment_ids[None, :] < seg_here[:, None]).astype(jnp.int32), axis=1)
    end = jnp.sum((segment_ids[None, :] <= seg_here[:, None]).astype(jnp.int32), axis=1)
    reach = jnp.broadcast_to((positions - first)[:, None], (rows, chans))
    rem = jnp.broadcast_to((end - 1 - positions)[:, None], (rows, chans))

    block, edge, quarter = (rows, chans), (taps, chans), (Y, rows, LANES)
    whole = [pltpu.VMEM((rows, width), BF)]
    shifted = [pltpu.VMEM((8, rows + taps, chans), F32)]
    macs = rows * width * chans
    small = rows * width * 2
    q, k, v, mix, tail = call(
        project, "project", [(block, BF)] * 4 + [(edge, BF)], whole,
        6 * macs, small + width * chans * 6, pos, *t_quarters, w3,
    )
    prior = passed_along(tail, 1)
    conv, *terms = call(
        forward, "forward", [(block, F32)] + [(quarter, BF)] * 4, shifted,
        2 * macs, 4 * small, pos, prior, mix, q, reach, filter_taps, out_weight,
    )
    block_out = summed(*terms)
    dq, dconv, head = call(
        back_gate, "back_gate", [(block, BF)] * 2 + [(edge, BF)], whole,
        2 * macs, small + width * chans * 2, pos, *c_quarters, out_weight, q, conv,
    )
    after = passed_along(head, -1)
    terms = call(
        back_project, "back_project", [(quarter, BF)] * 4,
        shifted + [pltpu.VMEM(block, F32)],
        6 * macs, 4 * small, pos, dconv, after, k, v, dq, rem, filter_taps, w3,
    )
    return block_out, summed(*terms)


def solution(mesh):
    fine = Mesh(
        mesh.devices.reshape(mesh.shape["ctx"], X, Y, CORE), ("ctx", "x", "y", "core")
    )
    tp = ("x", "y", "core")
    placed = (P("ctx", tp), P("ctx", tp), P(None, None, tp), P(None, tp), P(tp, None), P())
    return jax.shard_map(
        shards,
        mesh=fine,
        in_specs=placed,
        out_specs=(P("ctx", tp), P("ctx", tp)),
        check_vma=False,
    )
```

time: 253 us -> 149 us (0.59)
  the two profiles are of different devices: /device:TPU:12 before, /device:TPU:512 now
where the time goes in v1:
time: 149 us; the launch traced here: 148 us
  starting transfers between devices  56.4 us (38%)
  waiting for transfers between devices  40.2 us (27%)
  blocking collectives  24.5 us (16%)
  Pallas kernels  14.5 us (10%)
  local copies, waits for them, and re-layouts  5.68 us (4%)
  other arithmetic  5.3 us (4%)
    all_to_all x1, blocking collectives, spread_y(): return lax.all_to_all(copies, 'y', split_axis=0, concat_axis=0, tiled=True)  24.5 us
    all_to_all x2, waiting for transfers between devices, summed(): arrived = lax.all_to_all(half, 'y', split_axis=0, concat_axis=0, tiled=True)  15.9 us
    pallas_call x4, Pallas kernels, call(): pl.pallas_call(kernel, out_shape=[jax.ShapeDtypeStruct(s, d) for s, d in...  14.5 us
    ppermute x2, waiting for transfers between devices, summed(): got = lax.ppermute(sent, 'x', SWAP)  14.4 us
    all_to_all x2, starting transfers between devices, summed(): arrived = lax.all_to_all(half, 'y', split_axis=0, concat_axis=0, tiled=True)  12.7 us
    ppermute x2, starting transfers between devices, passed_along(): return lax.ppermute(block, 'ctx', route)  11.1 us
    ppermute x2, waiting for transfers between devices, quarters(): far = lax.ppermute(own, 'x', SWAP)  9.89 us
    ppermute x2, starting transfers between devices, quarters(): far = lax.ppermute(own, 'x', SWAP)  6.92 us
  transfers between devices with their start and end apart: 17, of which 6 were waited for; matrix products, arithmetic and copies ran while one was open for 3% of the time, Pallas kernels for 10%

profile of v1, /device:TPU:512, one launch (start us, length us, event | category | flops | bytes accessed | tf_op | source)
XLA Modules:
  0.0 147.6 jit_solution(6693654190361471556)
XLA Ops:
  0.6 1.1 broadcast_in_dim.8
  1.7 24.5 %all_to_all.20.t0 = bf16[8,256,128]{2,1,0:T(8,128)(2,1)} all-to-all(bf16[8,256,128]{2,1,0:T(8,128)(2,1)S(1)} %broadcast_in_dim.8), channel_id=1, replica_groups=mesh['ctx'=24,'x'=2,'y'=8,'core'=2] {'y'}, dimensions={0} | all-to-all | bytes 1048576 | tf_op jit(solution)/shard_map/all_to_all | solution.py:148
  26.2 1.7 %broadcast_in_dim.10 = bf16[8,256,128]{2,1,0:T(8,128)(2,1)} broadcast(bf16[256,128]{1,0:T(8,128)(2,1)} %param.7), dimensions={1,2} | broadcast | bytes 589824 | tf_op jit(solution)/shard_map/broadcast_in_dim | solution.py:147
  27.9 4.3 %all-to-all-start.2 = ((bf16[8,256,128]{2,1,0:T(8,128)(2,1)}), bf16[8,256,128]{2,1,0:T(8,128)(2,1)}, u32[]{:S(2)}, u32[]{:S(2)}) async-start(bf16[8,256,128]{2,1,0:T(8,128)(2,1)} %broadcast_in_dim.10), calls=%async_computation.2 | async-start | bytes 1048576 | tf_op jit(solution)/shard_map/all_to_all | solution.py:148
  32.2 3.4 %collective-permute-start.1 = (bf16[8,256,128]{2,1,0:T(8,128)(2,1)}, bf16[8,256,128]{2,1,0:T(8,128)(2,1)}, u32[]{:S(2)}, u32[]{:S(2)}) collective-permute-start(bf16[8,256,128]{2,1,0:T(8,128)(2,1)} %all_to_all.20.t0), channel_id=1, source_target_pairs={{0,16},{16,0},{1,17},{17,1},{2,18},{18,2},{3,19},{19,3},{4,20},{20... | collective-permute-start | bytes 1572872 | tf_op jit(solution)/shard_map/ppermute | solution.py:152
  35.6 1.9 %collective-permute-start = (bf16[8,256,128]{2,1,0:T(8,128)(2,1)}, bf16[8,256,128]{2,1,0:T(8,128)(2,1)}, u32[]{:S(2)}, u32[]{:S(2)}) collective-permute-start(bf16[8,256,128]{2,1,0:T(8,128)(2,1)} %all_to_all.20.t0), channel_id=1, source_target_pairs={{0,1},{1,0},{2,3},{3,2},{4,5},{5,4},{6,7},{7,6},{8,9},{9,8},{10,11... | collective-permute-start | bytes 1572872 | tf_op jit(solution)/shard_map/ppermute | solution.py:153
  37.5 8.9 %collective-permute-done.1.t2 = bf16[8,256,128]{2,1,0:T(8,128)(2,1)} collective-permute-done((bf16[8,256,128]{2,1,0:T(8,128)(2,1)}, bf16[8,256,128]{2,1,0:T(8,128)(2,1)}, u32[]{:S(2)}, u32[]{:S(2)}) %collective-permute-start.1) | collective-permute-done | bytes 524320 | tf_op jit(solution)/shard_map/ppermute | solution.py:152
  46.4 1.9 %collective-permute-start.2 = (bf16[8,256,128]{2,1,0:T(8,128)(2,1)}, bf16[8,256,128]{2,1,0:T(8,128)(2,1)}, u32[]{:S(2)}, u32[]{:S(2)}) collective-permute-start(bf16[8,256,128]{2,1,0:T(8,128)(2,1)} %collective-permute-done.1.t2), channel_id=1, source_target_pairs={{0,1},{1,0},{2,3},{3,2},{4,5},{5,4},{6,7},{7,6},{8,9},{9,8},{10,11... | collective-permute-start | bytes 1572872 | tf_op jit(solution)/shard_map/ppermute | solution.py:153
  48.5 3.5 %collective-permute-start.8 = (bf16[8,256,128]{2,1,0:T(8,128)(2,1)}, bf16[8,256,128]{2,1,0:T(8,128)(2,1)S(1)}, u32[]{:S(2)}, u32[]{:S(2)}) collective-permute-start(bf16[8,256,128]{2,1,0:T(8,128)(2,1)} %all-to-all-done.2.c0), channel_id=1, source_target_pairs={{0,16},{16,0},{1,17},{17,1},{2,18},{18,2},{3,19},{19,3},{4,20},{20... | collective-permute-start | bytes 1572872 | tf_op jit(solution)/shard_map/ppermute | solution.py:152
  52.1 1.5 %convert_reduce_fusion = (s32[256]{0:T(256)S(1)}, s32[256]{0:T(256)S(1)}) fusion(s32[6144]{0:T(1024)S(1)} %copy-done.8, s32[256]{0:T(256)S(1)} %dynamic_slice.3), kind=kLoop, calls=%fused_computation | loop fusion | flops 9436672 | bytes 27648 | tf_op jit(solution)/shard_map/reduce_sum | solution.py:179
  53.6 1.0 copy-done.2
  54.6 3.2 %project.1 = (bf16[256,128]{1,0:T(8,128)(2,1)S(1)}, bf16[256,128]{1,0:T(8,128)(2,1)S(1)}, bf16[256,128]{1,0:T(8,128)(2,1)S(1)}, bf16[256,128]{1,0:T(8,128)(2,1)S(1)}, bf16[128,128]{1,0:T(8,128)(2,1)S(1)}) custom-call(s32[2]{0:T(128)S(1)} %pad_add_fusion.pos, bf16[8,256,128]{2,1,0:T(8,128)(2,1)S(1)} %copy-done.2, ...), custom_call_target="tpu_custom_call" | custom-call | flops 805306368 | bytes 5242880 | tf_op jit(solution)/shard_map/project/pallas_call | solution.py:22
  57.8 4.6 %collective-permute-start.3 = (bf16[128,128]{1,0:T(8,128)(2,1)S(1)}, bf16[128,128]{1,0:T(8,128)(2,1)S(1)}, u32[]{:S(2)}, u32[]{:S(2)}) collective-permute-start(bf16[128,128]{1,0:T(8,128)(2,1)S(1)} %get-tuple-element.19), channel_id=1, source_target_pairs={{0,32},{32,64},{64,96},{96,128},{128,160},{160,192},{192,224},{224... | collective-permute-start | bytes 98312 | tf_op jit(solution)/shard_map/ppermute | solution.py:143
  62.5 1.9 %collective-permute-start.7 = (bf16[8,256,128]{2,1,0:T(8,128)(2,1)}, bf16[8,256,128]{2,1,0:T(8,128)(2,1)S(1)}, u32[]{:S(2)}, u32[]{:S(2)}) collective-permute-start(bf16[8,256,128]{2,1,0:T(8,128)(2,1)} %all-to-all-done.2.c0), channel_id=1, source_target_pairs={{0,1},{1,0},{2,3},{3,2},{4,5},{5,4},{6,7},{7,6},{8,9},{9,8},{10,11... | collective-permute-start | bytes 1572872 | tf_op jit(solution)/shard_map/ppermute | solution.py:153
  64.4 1.0 collective-permute-done.8.c2
  65.4 1.9 %collective-permute-start.9 = (bf16[8,256,128]{2,1,0:T(8,128)(2,1)S(1)}, bf16[8,256,128]{2,1,0:T(8,128)(2,1)S(1)}, u32[]{:S(2)}, u32[]{:S(2)}) collective-permute-start(bf16[8,256,128]{2,1,0:T(8,128)(2,1)S(1)} %collective-permute-done.8.c2), channel_id=1, source_target_pairs={{0,1},{1,0},{2,3},{3,2},{4,5},{5,4},{6,7},{7,6},{8,9},{9,8},{10,11... | collective-permute-start | bytes 1572872 | tf_op jit(solution)/shard_map/ppermute | solution.py:153
  67.5 3.8 %forward.1 = (f32[256,128]{1,0:T(8,128)S(1)}, bf16[8,256,128]{2,1,0:T(8,128)(2,1)S(1)}, bf16[8,256,128]{2,1,0:T(8,128)(2,1)S(1)}, bf16[8,256,128]{2,1,0:T(8,128)(2,1)S(1)}, bf16[8,256,128]{2,1,0:T(8,128)(2,1)S(1)}) custom-call(s32[2]{0:T(128)S(1)} %pad_add_fusion.pos, bf16[128,128]{1,0:T(8,128)(2,1)S(1)} %collective-permute-done.3.prior, ...), custom_call_target="tpu_custom_call" | custom-call | flops 268435456 | bytes 8388608 | tf_op jit(solution)/shard_map/forward/pallas_call | solution.py:22
  71.3 2.4 %collective-permute-start.5 = (bf16[8,256,128]{2,1,0:T(8,128)(2,1)S(1)}, bf16[8,256,128]{2,1,0:T(8,128)(2,1)S(1)}, u32[]{:S(2)}, u32[]{:S(2)}) collective-permute-start(bf16[8,256,128]{2,1,0:T(8,128)(2,1)S(1)} %get-tuple-element.25), channel_id=1, source_target_pairs={{0,1},{1,0},{2,3},{3,2},{4,5},{5,4},{6,7},{7,6},{8,9},{9,8},{10,11... | collective-permute-start | bytes 1572872 | tf_op jit(solution)/shard_map/ppermute | solution.py:157
  73.7 1.9 %collective-permute-start.4 = (bf16[8,256,128]{2,1,0:T(8,128)(2,1)S(1)}, bf16[8,256,128]{2,1,0:T(8,128)(2,1)S(1)}, u32[]{:S(2)}, u32[]{:S(2)}) collective-permute-start(bf16[8,256,128]{2,1,0:T(8,128)(2,1)S(1)} %get-tuple-element.23), channel_id=1, source_target_pairs={{0,1},{1,0},{2,3},{3,2},{4,5},{5,4},{6,7},{7,6},{8,9},{9,8},{10,11... | collective-permute-start | bytes 1572872 | tf_op jit(solution)/shard_map/ppermute | solution.py:159
  75.6 2.3 %back_gate.1 = (bf16[256,128]{1,0:T(8,128)(2,1)S(1)}, bf16[256,128]{1,0:T(8,128)(2,1)S(1)}, bf16[128,128]{1,0:T(8,128)(2,1)S(1)}) custom-call(s32[2]{0:T(128)S(1)} %pad_add_fusion.pos, bf16[8,256,128]{2,1,0:T(8,128)(2,1)} %all-to-all-done.2.c0, bf16[8,256,128]{2,1,0:T(8,128)(2,1)S(1)} %collective-permute-done.7.c1, ...), custom_call_target="tpu_custom_call" | custom-call | flops 268435456 | bytes 3145728 | tf_op jit(solution)/shard_map/back_gate/pallas_call | solution.py:22
  78.0 6.5 %collective-permute-start.10 = (bf16[128,128]{1,0:T(8,128)(2,1)S(1)}, bf16[128,128]{1,0:T(8,128)(2,1)S(1)}, u32[]{:S(2)}, u32[]{:S(2)}) collective-permute-start(bf16[128,128]{1,0:T(8,128)(2,1)S(1)} %get-tuple-element.28), channel_id=1, source_target_pairs={{32,0},{64,32},{96,64},{128,96},{160,128},{192,160},{224,192},{256... | collective-permute-start | bytes 98312 | tf_op jit(solution)/shard_map/ppermute | solution.py:143
  84.6 2.5 %collective-permute-start.6 = (bf16[8,256,128]{2,1,0:T(8,128)(2,1)S(1)}, bf16[8,256,128]{2,1,0:T(8,128)(2,1)S(1)}, u32[]{:S(2)}, u32[]{:S(2)}) collective-permute-start(bf16[8,256,128]{2,1,0:T(8,128)(2,1)S(1)} %add_convert_fusion.3), channel_id=1, source_target_pairs={{0,16},{16,0},{1,17},{17,1},{2,18},{18,2},{3,19},{19,3},{4,20},{20... | collective-permute-start | bytes 1572872 | tf_op jit(solution)/shard_map/ppermute | solution.py:160
  87.2 5.2 %back_project.1 = (bf16[8,256,128]{2,1,0:T(8,128)(2,1)S(1)}, bf16[8,256,128]{2,1,0:T(8,128)(2,1)}, bf16[8,256,128]{2,1,0:T(8,128)(2,1)S(1)}, bf16[8,256,128]{2,1,0:T(8,128)(2,1)}) custom-call(s32[2]{0:T(128)S(1)} %pad_add_fusion.pos, bf16[256,128]{1,0:T(8,128)(2,1)S(1)} %get-tuple-element.27.dconv, bf16[128,128]{1,0:T(8,128)(2,1)S(1)} %collective-permute-done.10.after, ...), custom_call_target="tpu_custom_call" | custom-call | flops 805306368 | bytes 8388608 | tf_op jit(solution)/shard_map/back_project/pallas_call | solution.py:22
  94.0 2.0 %collective-permute-start.12 = (bf16[8,256,128]{2,1,0:T(8,128)(2,1)}, bf16[8,256,128]{2,1,0:T(8,128)(2,1)S(1)}, u32[]{:S(2)}, u32[]{:S(2)}) collective-permute-start(bf16[8,256,128]{2,1,0:T(8,128)(2,1)} %get-tuple-element.35), channel_id=1, source_target_pairs={{0,1},{1,0},{2,3},{3,2},{4,5},{5,4},{6,7},{7,6},{8,9},{9,8},{10,11... | collective-permute-start | bytes 1572872 | tf_op jit(solution)/shard_map/ppermute | solution.py:157
  96.0 2.4 %collective-permute-start.11 = (bf16[8,256,128]{2,1,0:T(8,128)(2,1)}, bf16[8,256,128]{2,1,0:T(8,128)(2,1)S(1)}, u32[]{:S(2)}, u32[]{:S(2)}) collective-permute-start(bf16[8,256,128]{2,1,0:T(8,128)(2,1)} %get-tuple-element.33), channel_id=1, source_target_pairs={{0,1},{1,0},{2,3},{3,2},{4,5},{5,4},{6,7},{7,6},{8,9},{9,8},{10,11... | collective-permute-start | bytes 1572872 | tf_op jit(solution)/shard_map/ppermute | solution.py:159
  98.5 2.1 %collective-permute-done.6 = bf16[8,256,128]{2,1,0:T(8,128)(2,1)S(1)} collective-permute-done((bf16[8,256,128]{2,1,0:T(8,128)(2,1)S(1)}, bf16[8,256,128]{2,1,0:T(8,128)(2,1)S(1)}, u32[]{:S(2)}, u32[]{:S(2)}) %collective-permute-start.6) | collective-permute-done | bytes 524320 | tf_op jit(solution)/shard_map/ppermute | solution.py:160
  101.6 6.8 %all-to-all-start.1 = ((bf16[8,256,128]{2,1,0:T(8,128)(2,1)}), bf16[8,256,128]{2,1,0:T(8,128)(2,1)S(1)}, u32[]{:S(2)}, u32[]{:S(2)}) async-start(bf16[8,256,128]{2,1,0:T(8,128)(2,1)} %add_convert_fusion.2), calls=%async_computation.1 | async-start | bytes 1048576 | tf_op jit(solution)/shard_map/all_to_all | solution.py:162
  108.6 2.5 %collective-permute-start.13 = (bf16[8,256,128]{2,1,0:T(8,128)(2,1)S(1)}, bf16[8,256,128]{2,1,0:T(8,128)(2,1)S(1)}, u32[]{:S(2)}, u32[]{:S(2)}) collective-permute-start(bf16[8,256,128]{2,1,0:T(8,128)(2,1)S(1)} %add_convert_fusion.1), channel_id=1, source_target_pairs={{0,16},{16,0},{1,17},{17,1},{2,18},{18,2},{3,19},{19,3},{4,20},{20... | collective-permute-start | bytes 1572872 | tf_op jit(solution)/shard_map/ppermute | solution.py:160
  111.1 12.3 %collective-permute-done.13 = bf16[8,256,128]{2,1,0:T(8,128)(2,1)S(1)} collective-permute-done((bf16[8,256,128]{2,1,0:T(8,128)(2,1)S(1)}, bf16[8,256,128]{2,1,0:T(8,128)(2,1)S(1)}, u32[]{:S(2)}, u32[]{:S(2)}) %collective-permute-start.13) | collective-permute-done | bytes 524320 | tf_op jit(solution)/shard_map/ppermute | solution.py:160
  124.4 1.0 all-to-all-done.1
  125.4 5.9 %all-to-all-start.3 = ((bf16[8,256,128]{2,1,0:T(8,128)(2,1)}), bf16[8,256,128]{2,1,0:T(8,128)(2,1)S(1)}, u32[]{:S(2)}, u32[]{:S(2)}) async-start(bf16[8,256,128]{2,1,0:T(8,128)(2,1)} %add_convert_fusion), calls=%async_computation.3 | async-start | bytes 1048576 | tf_op jit(solution)/shard_map/all_to_all | solution.py:162
  132.0 14.9 %all-to-all-done.3 = bf16[8,256,128]{2,1,0:T(8,128)(2,1)S(1)} async-done(((bf16[8,256,128]{2,1,0:T(8,128)(2,1)}), bf16[8,256,128]{2,1,0:T(8,128)(2,1)S(1)}, u32[]{:S(2)}, u32[]{:S(2)}) %all-to-all-start.3) | async-done | bytes 524320 | tf_op jit(solution)/shard_map/all_to_all | solution.py:162
  (40 shorter events, 5.7 us)
Async XLA Ops:
  0.6 47.7 %copy-start.8 = (s32[6144]{0:T(1024)S(1)}, s32[6144]{0:T(1024)}, u32[]{:S(2)}) copy-start(s32[6144]{0:T(1024)} %param.11) | copy-start | bytes 73732
  0.6 52.9 %copy-start = (bf16[4096,3,128]{2,0,1:T(8,128)(2,1)S(1)}, bf16[4096,3,128]{2,0,1:T(8,128)(2,1)}, u32[]{:S(2)}) copy-start(bf16[4096,3,128]{2,0,1:T(8,128)(2,1)} %param.8) | copy-start | bytes 9437188
  27.9 39.5 %copy-start.7 = (f32[128,128]{1,0:T(8,128)S(1)}, f32[128,128]{1,0:T(8,128)}, u32[]{:S(2)}) copy-start(f32[128,128]{1,0:T(8,128)} %taps.3) | copy-start | bytes 196612
  27.9 20.6 %all-to-all-start.2 = ((bf16[8,256,128]{2,1,0:T(8,128)(2,1)}), bf16[8,256,128]{2,1,0:T(8,128)(2,1)}, u32[]{:S(2)}, u32[]{:S(2)}) async-start(bf16[8,256,128]{2,1,0:T(8,128)(2,1)} %broadcast_in_dim.10), calls=%async_computation.2 | async-start | bytes 1048576 | tf_op jit(solution)/shard_map/all_to_all | solution.py:148
  32.2 14.2 %collective-permute-start.1 = (bf16[8,256,128]{2,1,0:T(8,128)(2,1)}, bf16[8,256,128]{2,1,0:T(8,128)(2,1)}, u32[]{:S(2)}, u32[]{:S(2)}) collective-permute-start(bf16[8,256,128]{2,1,0:T(8,128)(2,1)} %all_to_all.20.t0), channel_id=1, source_target_pairs={{0,16},{16,0},{1,17},{17,1},{2,18},{18,2},{3,19},{19,3},{4,20},{20... | collective-permute-start | bytes 1572872 | tf_op jit(solution)/shard_map/ppermute | solution.py:152
  35.6 17.9 %collective-permute-start = (bf16[8,256,128]{2,1,0:T(8,128)(2,1)}, bf16[8,256,128]{2,1,0:T(8,128)(2,1)}, u32[]{:S(2)}, u32[]{:S(2)}) collective-permute-start(bf16[8,256,128]{2,1,0:T(8,128)(2,1)} %all_to_all.20.t0), channel_id=1, source_target_pairs={{0,1},{1,0},{2,3},{3,2},{4,5},{5,4},{6,7},{7,6},{8,9},{9,8},{10,11... | collective-permute-start | bytes 1572872 | tf_op jit(solution)/shard_map/ppermute | solution.py:153
  46.4 7.1 %collective-permute-start.2 = (bf16[8,256,128]{2,1,0:T(8,128)(2,1)}, bf16[8,256,128]{2,1,0:T(8,128)(2,1)}, u32[]{:S(2)}, u32[]{:S(2)}) collective-permute-start(bf16[8,256,128]{2,1,0:T(8,128)(2,1)} %collective-permute-done.1.t2), channel_id=1, source_target_pairs={{0,1},{1,0},{2,3},{3,2},{4,5},{5,4},{6,7},{7,6},{8,9},{9,8},{10,11... | collective-permute-start | bytes 1572872 | tf_op jit(solution)/shard_map/ppermute | solution.py:153
  48.5 18.9 %copy-start.1 = (bf16[128,4096]{1,0:T(8,128)(2,1)S(1)}, bf16[128,4096]{1,0:T(8,128)(2,1)}, u32[]{:S(2)}) copy-start(bf16[128,4096]{1,0:T(8,128)(2,1)} %w.3) | copy-start | bytes 3145732
  48.5 16.9 %collective-permute-start.8 = (bf16[8,256,128]{2,1,0:T(8,128)(2,1)}, bf16[8,256,128]{2,1,0:T(8,128)(2,1)S(1)}, u32[]{:S(2)}, u32[]{:S(2)}) collective-permute-start(bf16[8,256,128]{2,1,0:T(8,128)(2,1)} %all-to-all-done.2.c0), channel_id=1, source_target_pairs={{0,16},{16,0},{1,17},{17,1},{2,18},{18,2},{3,19},{19,3},{4,20},{20... | collective-permute-start | bytes 1572872 | tf_op jit(solution)/shard_map/ppermute | solution.py:152
  53.6 1.0 copy-start.2
  57.8 9.5 %collective-permute-start.3 = (bf16[128,128]{1,0:T(8,128)(2,1)S(1)}, bf16[128,128]{1,0:T(8,128)(2,1)S(1)}, u32[]{:S(2)}, u32[]{:S(2)}) collective-permute-start(bf16[128,128]{1,0:T(8,128)(2,1)S(1)} %get-tuple-element.19), channel_id=1, source_target_pairs={{0,32},{32,64},{64,96},{96,128},{128,160},{160,192},{192,224},{224... | collective-permute-start | bytes 98312 | tf_op jit(solution)/shard_map/ppermute | solution.py:143
  62.5 13.1 %collective-permute-start.7 = (bf16[8,256,128]{2,1,0:T(8,128)(2,1)}, bf16[8,256,128]{2,1,0:T(8,128)(2,1)S(1)}, u32[]{:S(2)}, u32[]{:S(2)}) collective-permute-start(bf16[8,256,128]{2,1,0:T(8,128)(2,1)} %all-to-all-done.2.c0), channel_id=1, source_target_pairs={{0,1},{1,0},{2,3},{3,2},{4,5},{5,4},{6,7},{7,6},{8,9},{9,8},{10,11... | collective-permute-start | bytes 1572872 | tf_op jit(solution)/shard_map/ppermute | solution.py:153
  65.4 10.2 %collective-permute-start.9 = (bf16[8,256,128]{2,1,0:T(8,128)(2,1)S(1)}, bf16[8,256,128]{2,1,0:T(8,128)(2,1)S(1)}, u32[]{:S(2)}, u32[]{:S(2)}) collective-permute-start(bf16[8,256,128]{2,1,0:T(8,128)(2,1)S(1)} %collective-permute-done.8.c2), channel_id=1, source_target_pairs={{0,1},{1,0},{2,3},{3,2},{4,5},{5,4},{6,7},{7,6},{8,9},{9,8},{10,11... | collective-permute-start | bytes 1572872 | tf_op jit(solution)/shard_map/ppermute | solution.py:153
  71.3 13.2 %collective-permute-start.5 = (bf16[8,256,128]{2,1,0:T(8,128)(2,1)S(1)}, bf16[8,256,128]{2,1,0:T(8,128)(2,1)S(1)}, u32[]{:S(2)}, u32[]{:S(2)}) collective-permute-start(bf16[8,256,128]{2,1,0:T(8,128)(2,1)S(1)} %get-tuple-element.25), channel_id=1, source_target_pairs={{0,1},{1,0},{2,3},{3,2},{4,5},{5,4},{6,7},{7,6},{8,9},{9,8},{10,11... | collective-permute-start | bytes 1572872 | tf_op jit(solution)/shard_map/ppermute | solution.py:157
  73.7 24.8 %collective-permute-start.4 = (bf16[8,256,128]{2,1,0:T(8,128)(2,1)S(1)}, bf16[8,256,128]{2,1,0:T(8,128)(2,1)S(1)}, u32[]{:S(2)}, u32[]{:S(2)}) collective-permute-start(bf16[8,256,128]{2,1,0:T(8,128)(2,1)S(1)} %get-tuple-element.23), channel_id=1, source_target_pairs={{0,1},{1,0},{2,3},{3,2},{4,5},{5,4},{6,7},{7,6},{8,9},{9,8},{10,11... | collective-permute-start | bytes 1572872 | tf_op jit(solution)/shard_map/ppermute | solution.py:159
  78.0 9.2 %collective-permute-start.10 = (bf16[128,128]{1,0:T(8,128)(2,1)S(1)}, bf16[128,128]{1,0:T(8,128)(2,1)S(1)}, u32[]{:S(2)}, u32[]{:S(2)}) collective-permute-start(bf16[128,128]{1,0:T(8,128)(2,1)S(1)} %get-tuple-element.28), channel_id=1, source_target_pairs={{32,0},{64,32},{96,64},{128,96},{160,128},{192,160},{224,192},{256... | collective-permute-start | bytes 98312 | tf_op jit(solution)/shard_map/ppermute | solution.py:143
  84.6 15.9 %collective-permute-start.6 = (bf16[8,256,128]{2,1,0:T(8,128)(2,1)S(1)}, bf16[8,256,128]{2,1,0:T(8,128)(2,1)S(1)}, u32[]{:S(2)}, u32[]{:S(2)}) collective-permute-start(bf16[8,256,128]{2,1,0:T(8,128)(2,1)S(1)} %add_convert_fusion.3), channel_id=1, source_target_pairs={{0,16},{16,0},{1,17},{17,1},{2,18},{18,2},{3,19},{19,3},{4,20},{20... | collective-permute-start | bytes 1572872 | tf_op jit(solution)/shard_map/ppermute | solution.py:160
  92.4 0.8 copy-start.3
  93.2 0.8 copy-start.5
  94.0 14.4 %copy-start.4 = (bf16[8,256,128]{2,1,0:T(8,128)(2,1)S(1)}, bf16[8,256,128]{2,1,0:T(8,128)(2,1)}, u32[]{:S(2)}) copy-start(bf16[8,256,128]{2,1,0:T(8,128)(2,1)} %copy-done.3) | copy-start | bytes 1572868
  94.0 29.4 %copy-start.6 = (bf16[8,256,128]{2,1,0:T(8,128)(2,1)S(1)}, bf16[8,256,128]{2,1,0:T(8,128)(2,1)}, u32[]{:S(2)}) copy-start(bf16[8,256,128]{2,1,0:T(8,128)(2,1)} %copy-done.5) | copy-start | bytes 1572868
  94.0 14.4 %collective-permute-start.12 = (bf16[8,256,128]{2,1,0:T(8,128)(2,1)}, bf16[8,256,128]{2,1,0:T(8,128)(2,1)S(1)}, u32[]{:S(2)}, u32[]{:S(2)}) collective-permute-start(bf16[8,256,128]{2,1,0:T(8,128)(2,1)} %get-tuple-element.35), channel_id=1, source_target_pairs={{0,1},{1,0},{2,3},{3,2},{4,5},{5,4},{6,7},{7,6},{8,9},{9,8},{10,11... | collective-permute-start | bytes 1572872 | tf_op jit(solution)/shard_map/ppermute | solution.py:157
  96.0 15.0 %collective-permute-start.11 = (bf16[8,256,128]{2,1,0:T(8,128)(2,1)}, bf16[8,256,128]{2,1,0:T(8,128)(2,1)S(1)}, u32[]{:S(2)}, u32[]{:S(2)}) collective-permute-start(bf16[8,256,128]{2,1,0:T(8,128)(2,1)} %get-tuple-element.33), channel_id=1, source_target_pairs={{0,1},{1,0},{2,3},{3,2},{4,5},{5,4},{6,7},{7,6},{8,9},{9,8},{10,11... | collective-permute-start | bytes 1572872 | tf_op jit(solution)/shard_map/ppermute | solution.py:159
  101.6 23.8 %all-to-all-start.1 = ((bf16[8,256,128]{2,1,0:T(8,128)(2,1)}), bf16[8,256,128]{2,1,0:T(8,128)(2,1)S(1)}, u32[]{:S(2)}, u32[]{:S(2)}) async-start(bf16[8,256,128]{2,1,0:T(8,128)(2,1)} %add_convert_fusion.2), calls=%async_computation.1 | async-start | bytes 1048576 | tf_op jit(solution)/shard_map/all_to_all | solution.py:162
  108.6 14.8 %collective-permute-start.13 = (bf16[8,256,128]{2,1,0:T(8,128)(2,1)S(1)}, bf16[8,256,128]{2,1,0:T(8,128)(2,1)S(1)}, u32[]{:S(2)}, u32[]{:S(2)}) collective-permute-start(bf16[8,256,128]{2,1,0:T(8,128)(2,1)S(1)} %add_convert_fusion.1), channel_id=1, source_target_pairs={{0,16},{16,0},{1,17},{17,1},{2,18},{18,2},{3,19},{19,3},{4,20},{20... | collective-permute-start | bytes 1572872 | tf_op jit(solution)/shard_map/ppermute | solution.py:160
  125.4 21.5 %all-to-all-start.3 = ((bf16[8,256,128]{2,1,0:T(8,128)(2,1)}), bf16[8,256,128]{2,1,0:T(8,128)(2,1)S(1)}, u32[]{:S(2)}, u32[]{:S(2)}) async-start(bf16[8,256,128]{2,1,0:T(8,128)(2,1)} %add_convert_fusion), calls=%async_computation.3 | async-start | bytes 1048576 | tf_op jit(solution)/shard_map/all_to_all | solution.py:162

commit v2 on v1

v2 whole, which is shorter than its diff:
```python
import jax
import jax.numpy as jnp
from jax import lax
from jax.experimental import pallas as pl
from jax.experimental.pallas import tpu as pltpu
from jax.sharding import Mesh
from jax.sharding import PartitionSpec as P

X, Y, CORE = 2, 8, 2
SWAP = [(0, 1), (1, 0)]
LANES = 128
STRIP = 64
INTERPRET = False
BF, F32 = jnp.bfloat16, jnp.float32


def f32(a):
    return a.astype(F32)


def call(kernel, outs, scratch, flops, nbytes, *args):
    return pl.pallas_call(
        kernel,
        out_shape=[jax.ShapeDtypeStruct(s, d) for s, d in outs],
        in_specs=[pl.BlockSpec(memory_space=pltpu.SMEM)]
        + [pl.BlockSpec(memory_space=pltpu.VMEM)] * (len(args) - 1),
        out_specs=[pl.BlockSpec(memory_space=pltpu.VMEM)] * len(outs),
        scratch_shapes=scratch,
        cost_estimate=pl.CostEstimate(flops=flops, bytes_accessed=nbytes, transcendentals=0),
        compiler_params=pltpu.CompilerParams(vmem_limit_bytes=48 << 20),
        interpret=INTERPRET,
    )(*args)


def offset(pos, far, other, j):
    x = 1 - pos[0] if far else pos[0]
    core = 1 - pos[1] if other else pos[1]
    return pl.multiple_of(((x * Y + j) * CORE + core) * LANES, LANES)


def lay_out(pos, parts, whole):
    for at, part in enumerate(parts):
        for j in range(Y):
            whole[:, pl.ds(offset(pos, at // 2, at % 2, j), LANES)] = part[j]


def project(pos, t0, t1, t2, t3, w, q, k, v, mix, tail, whole):
    lay_out(pos, (t0, t1, t2, t3), whole)
    rhs = jnp.concatenate([w[0], w[1], w[2]], axis=1)
    proj = jnp.dot(whole[...], rhs, preferred_element_type=F32).astype(BF)
    q[...] = proj[:, :LANES]
    k[...] = proj[:, LANES : 2 * LANES]
    v[...] = proj[:, 2 * LANES :]
    product = (f32(proj[:, LANES : 2 * LANES]) * f32(proj[:, 2 * LANES :])).astype(BF)
    mix[...] = product
    tail[...] = product[-tail.shape[0] :]


def convolve(ext, limit, taps, shifted, back, result):
    total = ext.shape[0]
    for b in range(8):
        by = (total - b) % total if back else b
        shifted[b] = pltpu.roll(ext, by, 0) if by else ext
    n_taps = taps.shape[0]

    def strip(i, carry):
        at = pl.multiple_of(i * STRIP, STRIP)
        lim = limit[pl.ds(at, STRIP), :]

        def eight(a, acc):
            if back:
                start = pl.multiple_of(at + 8 * a, 8)
            else:
                start = pl.multiple_of(at + n_taps - 8 * a, 8)
            for b in range(8):
                s = 8 * a + b
                piece = shifted[b, pl.ds(start, STRIP), :]
                acc = acc + jnp.where(lim >= s, piece, 0.0) * taps[pl.ds(s, 1), :]
            return acc

        acc = lax.fori_loop(0, n_taps // 8, eight, jnp.zeros((STRIP, LANES), F32))
        result[pl.ds(at, STRIP), :] = acc
        return carry

    lax.fori_loop(0, limit.shape[0] // STRIP, strip, 0)


def pack(pos, w, ow, sent):
    for far in range(2):
        for j in range(Y):
            off = offset(pos, far, 1, j)
            at = far * Y + j
            for b in range(3):
                sent[b, at] = w[b, pl.ds(off, LANES), :]
            sent[3, at] = ow[:, pl.ds(off, LANES)]


def filtered(pos, prior, mix, q, reach, taps, conv, gated, shifted):
    ext = jnp.concatenate([f32(prior[...]), f32(mix[...])], axis=0)
    convolve(ext, reach, taps, shifted, False, conv)
    gated[...] = (f32(q[...]) * conv[...]).astype(BF)


def slot(pos, far, j):
    return (1 - pos[0] if far else pos[0]) * Y + j


def out_terms(pos, mine, theirs, w, given, terms):
    both = jnp.concatenate([mine[...], theirs[...]], axis=1)
    for far in range(2):
        for j in range(0, Y, 2):
            rhs = jnp.concatenate(
                [
                    jnp.concatenate(
                        [w[:, pl.ds(offset(pos, far, 0, i), LANES)], given[3, far * Y + i]], axis=0
                    )
                    for i in (j, j + 1)
                ],
                axis=1,
            )
            term = jnp.dot(both, rhs, preferred_element_type=F32).astype(BF)
            terms[slot(pos, far, j)] = term[:, :LANES]
            terms[slot(pos, far, j + 1)] = term[:, LANES:]


def back_gate(pos, c0, c1, w, q, conv, dq, dconv, head, whole):
    rows = whole.shape[0]
    for other, part in enumerate((c0, c1)):
        for far in range(2):
            for j in range(Y):
                off = offset(pos, far, other, j)
                whole[:, pl.ds(off, LANES)] = part[j, far * rows : (far + 1) * rows]
    dgated = lax.dot_general(
        whole[...], w[...], (((1,), (1,)), ((), ())), preferred_element_type=F32
    )
    dq[...] = (dgated * conv[...]).astype(BF)
    d = (dgated * f32(q[...])).astype(BF)
    dconv[...] = d
    head[...] = d[: head.shape[0]]


def back_filtered(pos, dconv, after, k, v, dq, rem, taps, dproj, shifted, dmix):
    ext = jnp.concatenate([f32(dconv[...]), f32(after[...])], axis=0)
    convolve(ext, rem, taps, shifted, True, dmix)
    dproj[:, :LANES] = dq[...]
    dproj[:, LANES : 2 * LANES] = (dmix[...] * f32(v[...])).astype(BF)
    dproj[:, 2 * LANES :] = (dmix[...] * f32(k[...])).astype(BF)


def grad_terms(pos, mine, theirs, w, given, terms):
    both = jnp.concatenate([mine[...], theirs[...]], axis=1)
    for far in range(2):
        for j in range(0, Y, 2):
            rhs = jnp.concatenate(
                [
                    jnp.concatenate(
                        [w[b, pl.ds(offset(pos, far, 0, i), LANES), :] for b in range(3)]
                        + [given[b, far * Y + i] for b in range(3)],
                        axis=1,
                    )
                    for i in (j, j + 1)
                ],
                axis=0,
            )
            term = lax.dot_general(
                both, rhs, (((1,), (1,)), ((), ())), preferred_element_type=F32
            ).astype(BF)
            terms[slot(pos, far, j)] = term[:, :LANES]
            terms[slot(pos, far, j + 1)] = term[:, LANES:]


def passed_along(block, distance):
    devices = range(lax.axis_size("ctx"))
    route = [(i - distance, i) for i in devices if i - distance in devices]
    return lax.ppermute(block, "ctx", route)


def spread_y(block):
    copies = jnp.broadcast_to(block[None], (Y,) + block.shape)
    return lax.all_to_all(copies, "y", split_axis=0, concat_axis=0, tiled=True)


def swapped(block, axis):
    return lax.ppermute(block, axis, SWAP)


def summed(terms):
    arrived = lax.all_to_all(terms, ("x", "y"), split_axis=0, concat_axis=0, tiled=True)
    return f32(arrived).sum(axis=0).astype(BF)


def block_step(tokens, cotangent, in_weight, filter_taps, out_weight, segment_ids):
    width, _, chans = in_weight.shape
    rows = tokens.shape[0]
    taps = filter_taps.shape[0]
    n_chips = X * Y
    block, edge = (rows, chans), (taps, chans)
    whole = [pltpu.VMEM((rows, width), BF)]
    shifted = [pltpu.VMEM((8, rows + taps, chans), F32)]
    macs = rows * width * chans
    small = rows * width * 2

    w3 = in_weight.transpose(1, 0, 2)
    pos = jnp.stack([lax.axis_index("x"), lax.axis_index("core")]).astype(jnp.int32)
    far_cot = swapped(cotangent, "x")
    t0 = spread_y(tokens)
    (sent,) = call(pack, [((4, n_chips, LANES, chans), BF)], [], 0, 4 * small, pos, w3, out_weight)
    given = swapped(sent, "core")
    base = lax.axis_index("ctx") * rows
    positions = base + jnp.arange(rows, dtype=jnp.int32)
    seg_here = lax.dynamic_slice_in_dim(segment_ids, base, rows)
    first = jnp.sum((segment_ids[None, :] < seg_here[:, None]).astype(jnp.int32), axis=1)
    end = jnp.sum((segment_ids[None, :] <= seg_here[:, None]).astype(jnp.int32), axis=1)
    reach = jnp.broadcast_to((positions - first)[:, None], block)
    rem = jnp.broadcast_to((end - 1 - positions)[:, None], block)

    t2 = swapped(t0, "x")
    t1 = swapped(t0, "core")
    t3 = swapped(t2, "core")
    c0 = spread_y(jnp.concatenate([cotangent, far_cot], axis=0))
    c1 = swapped(c0, "core")

    q, k, v, mix, tail = call(
        project, [(block, BF)] * 4 + [(edge, BF)], whole,
        6 * macs, small + width * chans * 6, pos, t0, t1, t2, t3, w3,
    )
    prior = passed_along(tail, 1)
    conv, gated = call(
        filtered, [(block, F32), (block, BF)], shifted,
        macs, small, pos, prior, mix, q, reach, filter_taps,
    )
    theirs = swapped(gated, "core")
    (terms,) = call(
        out_terms, [((n_chips, rows, LANES), BF)], [],
        2 * macs, 2 * small, pos, gated, theirs, out_weight, given,
    )
    block_out = summed(terms)
    dq, dconv, head = call(
        back_gate, [(block, BF)] * 2 + [(edge, BF)], whole,
        2 * macs, small + width * chans * 2, pos, c0, c1, out_weight, q, conv,
    )
    after = passed_along(head, -1)
    (dproj,) = call(
        back_filtered, [((rows, 3 * chans), BF)], shifted + [pltpu.VMEM(block, F32)],
        macs, small, pos, dconv, after, k, v, dq, rem, filter_taps,
    )
    theirs = swapped(dproj, "core")
    (terms,) = call(
        grad_terms, [((n_chips, rows, LANES), BF)], [],
        6 * macs, 4 * small, pos, dproj, theirs, w3, given,
    )
    return block_out, summed(terms)


def solution(mesh):
    fine = Mesh(
        mesh.devices.reshape(mesh.shape["ctx"], X, Y, CORE), ("ctx", "x", "y", "core")
    )
    tp = ("x", "y", "core")
    placed = (P("ctx", tp), P("ctx", tp), P(None, None, tp), P(None, tp), P(tp, None), P())
    return jax.shard_map(
        block_step,
        mesh=fine,
        in_specs=placed,
        out_specs=(P("ctx", tp), P("ctx", tp)),
        check_vma=False,
    )
```

time: 149 us -> 150 us (level)
  blocking collectives: 24.5 us -> 0 us
  waiting for transfers between devices: 40.2 us -> 59.2 us
  Pallas kernels: 14.5 us -> 23.2 us
    all_to_all x1 -> x0, blocking collectives: 24.5 us -> none  [spread_y(): return lax.all_to_all(copies, 'y', split_axis=0, concat_axis=0, tiled=True)]
    all_to_all x2, waiting for transfers between devices: 15.9 us -> 25.6 us  [summed(): lax.all_to_all(terms, ('x', 'y'), split_axis=0, concat_axis=0, tiled=True)]
    ppermute x2, waiting for transfers between devices: 0.01 us -> 9.62 us  [passed_along(): return lax.ppermute(block, 'ctx', route)]
    ppermute x12 -> x8, starting transfers between devices: 28.3 us -> 18.8 us  [swapped(): return lax.ppermute(block, axis, SWAP)]
    pallas_call x4 -> x7, Pallas kernels: 14.5 us -> 23.2 us  [call(): pl.pallas_call(kernel, out_shape=[jax.ShapeDtypeStruct(s, d) for s, d in...]
    all_to_all x1 -> x2, starting transfers between devices: 4.28 us -> 11.3 us  [spread_y(): return lax.all_to_all(copies, 'y', split_axis=0, concat_axis=0, tiled=True)]
    all_to_all x2, starting transfers between devices: 12.7 us -> 18 us  [summed(): lax.all_to_all(terms, ('x', 'y'), split_axis=0, concat_axis=0, tiled=True)]
    ppermute x12 -> x8, waiting for transfers between devices: 24.3 us -> 19.8 us  [swapped(): return lax.ppermute(block, axis, SWAP)]
  transfers between devices with their start and end apart: 17 -> 14, of which waited for: 6 -> 11; matrix products, arithmetic and copies ran while one was open for 3% -> 3% of each run, Pallas kernels for 10% -> 16%
where the time goes in v2:
time: 150 us; the launch traced here: 149 us
  waiting for transfers between devices  59.2 us (39%)
  starting transfers between devices  56.8 us (38%)
  Pallas kernels  23.2 us (15%)
  other arithmetic  4.39 us (3%)
  local copies, waits for them, and re-layouts  4.36 us (3%)
    all_to_all x2, waiting for transfers between devices, summed(): lax.all_to_all(terms, ('x', 'y'), split_axis=0, concat_axis=0, tiled=True)  25.6 us
    pallas_call x7, Pallas kernels, call(): pl.pallas_call(kernel, out_shape=[jax.ShapeDtypeStruct(s, d) for s, d in...  23.2 us
    ppermute x8, waiting for transfers between devices, swapped(): return lax.ppermute(block, axis, SWAP)  19.8 us
    ppermute x8, starting transfers between devices, swapped(): return lax.ppermute(block, axis, SWAP)  18.8 us
    all_to_all x2, starting transfers between devices, summed(): lax.all_to_all(terms, ('x', 'y'), split_axis=0, concat_axis=0, tiled=True)  18 us
    all_to_all x2, starting transfers between devices, spread_y(): return lax.all_to_all(copies, 'y', split_axis=0, concat_axis=0, tiled=True)  11.3 us
    ppermute x2, waiting for transfers between devices, passed_along(): return lax.ppermute(block, 'ctx', route)  9.62 us
    ppermute x2, starting transfers between devices, passed_along(): return lax.ppermute(block, 'ctx', route)  8.65 us
  transfers between devices with their start and end apart: 14, of which 11 were waited for; matrix products, arithmetic and copies ran while one was open for 3% of the time, Pallas kernels for 16%

profile of v2, /device:TPU:512, one launch (start us, length us, event | category | flops | bytes accessed | tf_op | source)
XLA Modules:
  0.0 148.8 jit_solution(2713726582136968439)
XLA Ops:
  0.6 1.7 %broadcast_in_dim.8 = bf16[8,256,128]{2,1,0:T(8,128)(2,1)} broadcast(bf16[256,128]{1,0:T(8,128)(2,1)} %param.6), dimensions={1,2} | broadcast | bytes 589824 | tf_op jit(solution)/shard_map/broadcast_in_dim | solution.py:179
  2.3 7.1 %all-to-all-start = ((bf16[8,256,128]{2,1,0:T(8,128)(2,1)}), bf16[8,256,128]{2,1,0:T(8,128)(2,1)}, u32[]{:S(2)}, u32[]{:S(2)}) async-start(bf16[8,256,128]{2,1,0:T(8,128)(2,1)} %broadcast_in_dim.8), calls=%async_computation | async-start | bytes 1048576 | tf_op jit(solution)/shard_map/all_to_all | solution.py:180
  10.7 3.5 %shard_map.79 = bf16[4,16,128,128]{3,2,1,0:T(8,128)(2,1)} custom-call(s32[2]{0:T(128)S(1)} %pad_add_fusion.pos, bf16[3,4096,128]{2,1,0:T(8,128)(2,1)} %bitcast.3, bf16[128,4096]{1,0:T(8,128)(2,1)S(1)} %copy-done.1), custom_call_target="tpu_custom_call" | custom-call | bytes 8388608 | tf_op jit(solution)/shard_map/pallas_call | solution.py:22
  14.2 2.2 %collective-permute-start.5 = (bf16[4,16,128,128]{3,2,1,0:T(8,128)(2,1)}, bf16[4,16,128,128]{3,2,1,0:T(8,128)(2,1)}, u32[]{:S(2)}, u32[]{:S(2)}) collective-permute-start(bf16[4,16,128,128]{3,2,1,0:T(8,128)(2,1)} %shard_map.79), channel_id=1, source_target_pairs={{0,1},{1,0},{2,3},{3,2},{4,5},{5,4},{6,7},{7,6},{8,9},{9,8},{10,11... | collective-permute-start | bytes 6291464 | tf_op jit(solution)/shard_map/ppermute | solution.py:184
  16.4 3.4 %collective-permute-start.6 = (bf16[256,128]{1,0:T(8,128)(2,1)S(1)}, bf16[256,128]{1,0:T(8,128)(2,1)S(1)}, u32[]{:S(2)}, u32[]{:S(2)}) collective-permute-start(bf16[256,128]{1,0:T(8,128)(2,1)S(1)} %copy-done.5), channel_id=1, source_target_pairs={{0,16},{16,0},{1,17},{17,1},{2,18},{18,2},{3,19},{19,3},{4,20},{20... | collective-permute-start | bytes 196616 | tf_op jit(solution)/shard_map/ppermute | solution.py:184
  19.8 3.0 %collective-permute-done.6 = bf16[256,128]{1,0:T(8,128)(2,1)S(1)} collective-permute-done((bf16[256,128]{1,0:T(8,128)(2,1)S(1)}, bf16[256,128]{1,0:T(8,128)(2,1)S(1)}, u32[]{:S(2)}, u32[]{:S(2)}) %collective-permute-start.6) | collective-permute-done | bytes 65568 | tf_op jit(solution)/shard_map/ppermute | solution.py:184
  22.8 4.2 %all-to-all-done.t0 = bf16[8,256,128]{2,1,0:T(8,128)(2,1)} async-done(((bf16[8,256,128]{2,1,0:T(8,128)(2,1)}), bf16[8,256,128]{2,1,0:T(8,128)(2,1)}, u32[]{:S(2)}, u32[]{:S(2)}) %all-to-all-start) | async-done | bytes 524320 | tf_op jit(solution)/shard_map/all_to_all | solution.py:180
  28.2 4.2 %all-to-all-start.2 = ((bf16[8,512,128]{2,1,0:T(8,128)(2,1)}), bf16[8,512,128]{2,1,0:T(8,128)(2,1)}, u32[]{:S(2)}, u32[]{:S(2)}) async-start(bf16[8,512,128]{2,1,0:T(8,128)(2,1)} %broadcast_in_dim.10), calls=%async_computation.2 | async-start | bytes 2097152 | tf_op jit(solution)/shard_map/all_to_all | solution.py:180
  32.4 3.5 %collective-permute-start.1 = (bf16[8,256,128]{2,1,0:T(8,128)(2,1)}, bf16[8,256,128]{2,1,0:T(8,128)(2,1)}, u32[]{:S(2)}, u32[]{:S(2)}) collective-permute-start(bf16[8,256,128]{2,1,0:T(8,128)(2,1)} %all-to-all-done.t0), channel_id=1, source_target_pairs={{0,16},{16,0},{1,17},{17,1},{2,18},{18,2},{3,19},{19,3},{4,20},{20... | collective-permute-start | bytes 1572872 | tf_op jit(solution)/shard_map/ppermute | solution.py:184
  36.0 1.9 %collective-permute-start = (bf16[8,256,128]{2,1,0:T(8,128)(2,1)}, bf16[8,256,128]{2,1,0:T(8,128)(2,1)}, u32[]{:S(2)}, u32[]{:S(2)}) collective-permute-start(bf16[8,256,128]{2,1,0:T(8,128)(2,1)} %all-to-all-done.t0), channel_id=1, source_target_pairs={{0,1},{1,0},{2,3},{3,2},{4,5},{5,4},{6,7},{7,6},{8,9},{9,8},{10,11... | collective-permute-start | bytes 1572872 | tf_op jit(solution)/shard_map/ppermute | solution.py:184
  37.9 10.7 %collective-permute-done.1.t2 = bf16[8,256,128]{2,1,0:T(8,128)(2,1)} collective-permute-done((bf16[8,256,128]{2,1,0:T(8,128)(2,1)}, bf16[8,256,128]{2,1,0:T(8,128)(2,1)}, u32[]{:S(2)}, u32[]{:S(2)}) %collective-permute-start.1) | collective-permute-done | bytes 524320 | tf_op jit(solution)/shard_map/ppermute | solution.py:184
  48.6 1.9 %collective-permute-start.2 = (bf16[8,256,128]{2,1,0:T(8,128)(2,1)}, bf16[8,256,128]{2,1,0:T(8,128)(2,1)}, u32[]{:S(2)}, u32[]{:S(2)}) collective-permute-start(bf16[8,256,128]{2,1,0:T(8,128)(2,1)} %collective-permute-done.1.t2), channel_id=1, source_target_pairs={{0,1},{1,0},{2,3},{3,2},{4,5},{5,4},{6,7},{7,6},{8,9},{9,8},{10,11... | collective-permute-start | bytes 1572872 | tf_op jit(solution)/shard_map/ppermute | solution.py:184
  50.7 1.5 %convert_reduce_fusion = (s32[256]{0:T(256)S(1)}, s32[256]{0:T(256)S(1)}) fusion(s32[6144]{0:T(1024)S(1)} %copy-done.6, s32[256]{0:T(256)S(1)} %dynamic_slice.3), kind=kLoop, calls=%fused_computation | loop fusion | flops 9436672 | bytes 27648 | tf_op jit(solution)/shard_map/reduce_sum | solution.py:213
  52.8 3.4 %shard_map.77 = (bf16[256,128]{1,0:T(8,128)(2,1)S(1)}, bf16[256,128]{1,0:T(8,128)(2,1)S(1)}, bf16[256,128]{1,0:T(8,128)(2,1)S(1)}, bf16[256,128]{1,0:T(8,128)(2,1)S(1)}, bf16[128,128]{1,0:T(8,128)(2,1)S(1)}) custom-call(s32[2]{0:T(128)S(1)} %pad_add_fusion.pos, bf16[8,256,128]{2,1,0:T(8,128)(2,1)} %all-to-all-done.t0, ...), custom_call_target="tpu_custom_call" | custom-call | flops 805306368 | bytes 5242880 | tf_op jit(solution)/shard_map/pallas_call | solution.py:22
  56.1 4.9 %collective-permute-start.3 = (bf16[128,128]{1,0:T(8,128)(2,1)S(1)}, bf16[128,128]{1,0:T(8,128)(2,1)S(1)}, u32[]{:S(2)}, u32[]{:S(2)}) collective-permute-start(bf16[128,128]{1,0:T(8,128)(2,1)S(1)} %get-tuple-element.12), channel_id=1, source_target_pairs={{0,32},{32,64},{64,96},{96,128},{128,160},{160,192},{192,224},{224... | collective-permute-start | bytes 98312 | tf_op jit(solution)/shard_map/ppermute | solution.py:175
  61.1 4.5 %collective-permute-done.3.prior = bf16[128,128]{1,0:T(8,128)(2,1)S(1)} collective-permute-done((bf16[128,128]{1,0:T(8,128)(2,1)S(1)}, bf16[128,128]{1,0:T(8,128)(2,1)S(1)}, u32[]{:S(2)}, u32[]{:S(2)}) %collective-permute-start.3) | collective-permute-done | bytes 32800 | tf_op jit(solution)/shard_map/ppermute | solution.py:175
  65.7 3.1 %shard_map.78 = (f32[256,128]{1,0:T(8,128)S(1)}, bf16[256,128]{1,0:T(8,128)(2,1)S(1)}) custom-call(s32[2]{0:T(128)S(1)} %pad_add_fusion.pos, bf16[128,128]{1,0:T(8,128)(2,1)S(1)} %collective-permute-done.3.prior, bf16[256,128]{1,0:T(8,128)(2,1)S(1)} %get-tuple-element.13.mix, bf16[256,128]{1,0:T(8,128)(2,1)S(1)} %get-tuple-element.14.q, ...), custom_call_target="tpu_custom_call" | custom-call | flops 134217728 | bytes 2097152 | tf_op jit(solution)/shard_map/pallas_call | solution.py:22
  68.8 2.1 %collective-permute-start.4 = (bf16[256,128]{1,0:T(8,128)(2,1)S(1)}, bf16[256,128]{1,0:T(8,128)(2,1)S(1)}, u32[]{:S(2)}, u32[]{:S(2)}) collective-permute-start(bf16[256,128]{1,0:T(8,128)(2,1)S(1)} %get-tuple-element.15.mine), channel_id=1, source_target_pairs={{0,1},{1,0},{2,3},{3,2},{4,5},{5,4},{6,7},{7,6},{8,9},{9,8},{10,11... | collective-permute-start | bytes 196616 | tf_op jit(solution)/shard_map/ppermute | solution.py:184
  72.0 3.1 %shard_map.80 = bf16[16,256,128]{2,1,0:T(8,128)(2,1)} custom-call(s32[2]{0:T(128)S(1)} %pad_add_fusion.pos, bf16[256,128]{1,0:T(8,128)(2,1)S(1)} %get-tuple-element.15.mine, bf16[256,128]{1,0:T(8,128)(2,1)S(1)} %collective-permute-done.4.theirs, bf16[128,4096]{1,0:T(8,128)(2,1)S(1)} %copy-done.2, bf16[4,16,128,128]{3,2,1,0:T(8,128)(2,1)} %collective-permute-done.5.given), custom_call_target="tpu_custom_call" | custom-call | flops 268435456 | bytes 4194304 | tf_op jit(solution)/shard_map/pallas_call | solution.py:22
  75.1 7.9 %all-to-all-start.1 = ((bf16[16,256,128]{2,1,0:T(8,128)(2,1)}), bf16[16,256,128]{2,1,0:T(8,128)(2,1)}, u32[]{:S(2)}, u32[]{:S(2)}) async-start(bf16[16,256,128]{2,1,0:T(8,128)(2,1)} %shard_map.80), calls=%async_computation.1 | async-start | bytes 2097152 | tf_op jit(solution)/shard_map/all_to_all | solution.py:188
  83.0 1.9 %collective-permute-start.7 = (bf16[8,512,128]{2,1,0:T(8,128)(2,1)}, bf16[8,512,128]{2,1,0:T(8,128)(2,1)S(1)}, u32[]{:S(2)}, u32[]{:S(2)}) collective-permute-start(bf16[8,512,128]{2,1,0:T(8,128)(2,1)} %all-to-all-done.2.c0), channel_id=1, source_target_pairs={{0,1},{1,0},{2,3},{3,2},{4,5},{5,4},{6,7},{7,6},{8,9},{9,8},{10,11... | collective-permute-start | bytes 3145736 | tf_op jit(solution)/shard_map/ppermute | solution.py:184
  84.9 2.8 %collective-permute-done.7.c1 = bf16[8,512,128]{2,1,0:T(8,128)(2,1)S(1)} collective-permute-done((bf16[8,512,128]{2,1,0:T(8,128)(2,1)}, bf16[8,512,128]{2,1,0:T(8,128)(2,1)S(1)}, u32[]{:S(2)}, u32[]{:S(2)}) %collective-permute-start.7) | collective-permute-done | bytes 1048608 | tf_op jit(solution)/shard_map/ppermute | solution.py:184
  87.8 2.5 %shard_map.81 = (bf16[256,128]{1,0:T(8,128)(2,1)S(1)}, bf16[256,128]{1,0:T(8,128)(2,1)S(1)}, bf16[128,128]{1,0:T(8,128)(2,1)S(1)}) custom-call(s32[2]{0:T(128)S(1)} %pad_add_fusion.pos, bf16[8,512,128]{2,1,0:T(8,128)(2,1)} %all-to-all-done.2.c0, bf16[8,512,128]{2,1,0:T(8,128)(2,1)S(1)} %collective-permute-done.7.c1, bf16[128,4096]{1,0:T(8,128)(2,1)S(1)} %copy-done.3, ...), custom_call_target="tpu_custom_call" | custom-call | flops 268435456 | bytes 3145728 | tf_op jit(solution)/shard_map/pallas_call | solution.py:22
  90.3 3.7 %collective-permute-start.8 = (bf16[128,128]{1,0:T(8,128)(2,1)S(1)}, bf16[128,128]{1,0:T(8,128)(2,1)S(1)}, u32[]{:S(2)}, u32[]{:S(2)}) collective-permute-start(bf16[128,128]{1,0:T(8,128)(2,1)S(1)} %get-tuple-element.18), channel_id=1, source_target_pairs={{32,0},{64,32},{96,64},{128,96},{160,128},{192,160},{224,192},{256... | collective-permute-start | bytes 98312 | tf_op jit(solution)/shard_map/ppermute | solution.py:175
  94.0 5.1 %collective-permute-done.8.after = bf16[128,128]{1,0:T(8,128)(2,1)S(1)} collective-permute-done((bf16[128,128]{1,0:T(8,128)(2,1)S(1)}, bf16[128,128]{1,0:T(8,128)(2,1)S(1)}, u32[]{:S(2)}, u32[]{:S(2)}) %collective-permute-start.8) | collective-permute-done | bytes 32800 | tf_op jit(solution)/shard_map/ppermute | solution.py:175
  99.3 3.1 %shard_map.82.mine = bf16[256,384]{1,0:T(8,128)(2,1)S(1)} custom-call(s32[2]{0:T(128)S(1)} %pad_add_fusion.pos, bf16[256,128]{1,0:T(8,128)(2,1)S(1)} %get-tuple-element.17.dconv, bf16[128,128]{1,0:T(8,128)(2,1)S(1)} %collective-permute-done.8.after, bf16[256,128]{1,0:T(8,128)(2,1)S(1)} %get-tuple-element.19.k, bf16[256,128]{1,0:T(8,128)(2,1)S(1)} %get-tuple-element.20.v, ...), custom_call_target="tpu_custom_call" | custom-call | flops 134217728 | bytes 2097152 | tf_op jit(solution)/shard_map/pallas_call | solution.py:22
  102.4 1.9 %collective-permute-start.9 = (bf16[256,384]{1,0:T(8,128)(2,1)S(1)}, bf16[256,384]{1,0:T(8,128)(2,1)S(1)}, u32[]{:S(2)}, u32[]{:S(2)}) collective-permute-start(bf16[256,384]{1,0:T(8,128)(2,1)S(1)} %shard_map.82.mine), channel_id=1, source_target_pairs={{0,1},{1,0},{2,3},{3,2},{4,5},{5,4},{6,7},{7,6},{8,9},{9,8},{10,11... | collective-permute-start | bytes 589832 | tf_op jit(solution)/shard_map/ppermute | solution.py:184
  104.3 1.4 collective-permute-done.9.theirs
  105.7 4.6 %shard_map.83 = bf16[16,256,128]{2,1,0:T(8,128)(2,1)} custom-call(s32[2]{0:T(128)S(1)} %pad_add_fusion.pos, bf16[256,384]{1,0:T(8,128)(2,1)S(1)} %shard_map.82.mine, bf16[256,384]{1,0:T(8,128)(2,1)S(1)} %collective-permute-done.9.theirs, bf16[3,4096,128]{2,1,0:T(8,128)(2,1)} %bitcast.4, bf16[4,16,128,128]{3,2,1,0:T(8,128)(2,1)} %collective-permute-done.5.given), custom_call_target="tpu_custom_call" | custom-call | flops 805306368 | bytes 8388608 | tf_op jit(solution)/shard_map/pallas_call | solution.py:22
  110.5 10.1 %all-to-all-start.3 = ((bf16[16,256,128]{2,1,0:T(8,128)(2,1)}), bf16[16,256,128]{2,1,0:T(8,128)(2,1)S(1)}, u32[]{:S(2)}, u32[]{:S(2)}) async-start(bf16[16,256,128]{2,1,0:T(8,128)(2,1)} %shard_map.83), calls=%async_computation.3 | async-start | bytes 2097152 | tf_op jit(solution)/shard_map/all_to_all | solution.py:188
  120.6 2.0 %reduce_sum.43 = bf16[256,128]{1,0:T(8,128)(2,1)} reduce(bf16[16,256,128]{2,1,0:T(8,128)(2,1)} %all-to-all-done.1, bf16[]{:T(256)} %constant.24.clone.1), dimensions={0}, to_apply=%region_1.0 | reduce | flops 491520 | bytes 1114114 | tf_op jit(solution)/shard_map/reduce_sum | solution.py:189
  122.7 25.4 %all-to-all-done.3 = bf16[16,256,128]{2,1,0:T(8,128)(2,1)S(1)} async-done(((bf16[16,256,128]{2,1,0:T(8,128)(2,1)}), bf16[16,256,128]{2,1,0:T(8,128)(2,1)S(1)}, u32[]{:S(2)}, u32[]{:S(2)}) %all-to-all-start.3) | async-done | bytes 1048608 | tf_op jit(solution)/shard_map/all_to_all | solution.py:188
  (29 shorter events, 5.5 us)
Async XLA Ops:
  2.3 24.7 %all-to-all-start = ((bf16[8,256,128]{2,1,0:T(8,128)(2,1)}), bf16[8,256,128]{2,1,0:T(8,128)(2,1)}, u32[]{:S(2)}, u32[]{:S(2)}) async-start(bf16[8,256,128]{2,1,0:T(8,128)(2,1)} %broadcast_in_dim.8), calls=%async_computation | async-start | bytes 1048576 | tf_op jit(solution)/shard_map/all_to_all | solution.py:180
  9.5 1.2 copy-start.1
  10.7 5.7 %copy-start.5 = (bf16[256,128]{1,0:T(8,128)(2,1)S(1)}, bf16[256,128]{1,0:T(8,128)(2,1)}, u32[]{:S(2)}) copy-start(bf16[256,128]{1,0:T(8,128)(2,1)} %param.7) | copy-start | bytes 196612
  14.2 36.4 %copy-start.6 = (s32[6144]{0:T(1024)S(1)}, s32[6144]{0:T(1024)}, u32[]{:S(2)}) copy-start(s32[6144]{0:T(1024)} %param.11) | copy-start | bytes 73732
  14.2 38.6 %copy-start = (bf16[4096,3,128]{2,0,1:T(8,128)(2,1)S(1)}, bf16[4096,3,128]{2,0,1:T(8,128)(2,1)}, u32[]{:S(2)}) copy-start(bf16[4096,3,128]{2,0,1:T(8,128)(2,1)} %param.8) | copy-start | bytes 9437188
  14.2 57.8 %collective-permute-start.5 = (bf16[4,16,128,128]{3,2,1,0:T(8,128)(2,1)}, bf16[4,16,128,128]{3,2,1,0:T(8,128)(2,1)}, u32[]{:S(2)}, u32[]{:S(2)}) collective-permute-start(bf16[4,16,128,128]{3,2,1,0:T(8,128)(2,1)} %shard_map.79), channel_id=1, source_target_pairs={{0,1},{1,0},{2,3},{3,2},{4,5},{5,4},{6,7},{7,6},{8,9},{9,8},{10,11... | collective-permute-start | bytes 6291464 | tf_op jit(solution)/shard_map/ppermute | solution.py:184
  16.4 6.4 %collective-permute-start.6 = (bf16[256,128]{1,0:T(8,128)(2,1)S(1)}, bf16[256,128]{1,0:T(8,128)(2,1)S(1)}, u32[]{:S(2)}, u32[]{:S(2)}) collective-permute-start(bf16[256,128]{1,0:T(8,128)(2,1)S(1)} %copy-done.5), channel_id=1, source_target_pairs={{0,16},{16,0},{1,17},{17,1},{2,18},{18,2},{3,19},{19,3},{4,20},{20... | collective-permute-start | bytes 196616 | tf_op jit(solution)/shard_map/ppermute | solution.py:184
  28.2 46.9 %all-to-all-start.2 = ((bf16[8,512,128]{2,1,0:T(8,128)(2,1)}), bf16[8,512,128]{2,1,0:T(8,128)(2,1)}, u32[]{:S(2)}, u32[]{:S(2)}) async-start(bf16[8,512,128]{2,1,0:T(8,128)(2,1)} %broadcast_in_dim.10), calls=%async_computation.2 | async-start | bytes 2097152 | tf_op jit(solution)/shard_map/all_to_all | solution.py:180
  32.4 33.2 %copy-start.4 = (f32[128,128]{1,0:T(8,128)S(1)}, f32[128,128]{1,0:T(8,128)}, u32[]{:S(2)}) copy-start(f32[128,128]{1,0:T(8,128)} %taps.3) | copy-start | bytes 196612
  32.4 16.2 %collective-permute-start.1 = (bf16[8,256,128]{2,1,0:T(8,128)(2,1)}, bf16[8,256,128]{2,1,0:T(8,128)(2,1)}, u32[]{:S(2)}, u32[]{:S(2)}) collective-permute-start(bf16[8,256,128]{2,1,0:T(8,128)(2,1)} %all-to-all-done.t0), channel_id=1, source_target_pairs={{0,16},{16,0},{1,17},{17,1},{2,18},{18,2},{3,19},{19,3},{4,20},{20... | collective-permute-start | bytes 1572872 | tf_op jit(solution)/shard_map/ppermute | solution.py:184
  36.0 16.2 %collective-permute-start = (bf16[8,256,128]{2,1,0:T(8,128)(2,1)}, bf16[8,256,128]{2,1,0:T(8,128)(2,1)}, u32[]{:S(2)}, u32[]{:S(2)}) collective-permute-start(bf16[8,256,128]{2,1,0:T(8,128)(2,1)} %all-to-all-done.t0), channel_id=1, source_target_pairs={{0,1},{1,0},{2,3},{3,2},{4,5},{5,4},{6,7},{7,6},{8,9},{9,8},{10,11... | collective-permute-start | bytes 1572872 | tf_op jit(solution)/shard_map/ppermute | solution.py:184
  48.6 4.1 %collective-permute-start.2 = (bf16[8,256,128]{2,1,0:T(8,128)(2,1)}, bf16[8,256,128]{2,1,0:T(8,128)(2,1)}, u32[]{:S(2)}, u32[]{:S(2)}) collective-permute-start(bf16[8,256,128]{2,1,0:T(8,128)(2,1)} %collective-permute-done.1.t2), channel_id=1, source_target_pairs={{0,1},{1,0},{2,3},{3,2},{4,5},{5,4},{6,7},{7,6},{8,9},{9,8},{10,11... | collective-permute-start | bytes 1572872 | tf_op jit(solution)/shard_map/ppermute | solution.py:184
  50.6 21.5 %copy-start.2 = (bf16[128,4096]{1,0:T(8,128)(2,1)S(1)}, bf16[128,4096]{1,0:T(8,128)(2,1)}, u32[]{:S(2)}) copy-start(bf16[128,4096]{1,0:T(8,128)(2,1)} %w.3) | copy-start | bytes 3145732
  56.1 9.4 %collective-permute-start.3 = (bf16[128,128]{1,0:T(8,128)(2,1)S(1)}, bf16[128,128]{1,0:T(8,128)(2,1)S(1)}, u32[]{:S(2)}, u32[]{:S(2)}) collective-permute-start(bf16[128,128]{1,0:T(8,128)(2,1)S(1)} %get-tuple-element.12), channel_id=1, source_target_pairs={{0,32},{32,64},{64,96},{96,128},{128,160},{160,192},{192,224},{224... | collective-permute-start | bytes 98312 | tf_op jit(solution)/shard_map/ppermute | solution.py:175
  68.7 19.0 %copy-start.3 = (bf16[128,4096]{1,0:T(8,128)(2,1)S(1)}, bf16[128,4096]{1,0:T(8,128)(2,1)}, u32[]{:S(2)}) copy-start(bf16[128,4096]{1,0:T(8,128)(2,1)} %w.3) | copy-start | bytes 3145732
  68.8 3.3 %collective-permute-start.4 = (bf16[256,128]{1,0:T(8,128)(2,1)S(1)}, bf16[256,128]{1,0:T(8,128)(2,1)S(1)}, u32[]{:S(2)}, u32[]{:S(2)}) collective-permute-start(bf16[256,128]{1,0:T(8,128)(2,1)S(1)} %get-tuple-element.15.mine), channel_id=1, source_target_pairs={{0,1},{1,0},{2,3},{3,2},{4,5},{5,4},{6,7},{7,6},{8,9},{9,8},{10,11... | collective-permute-start | bytes 196616 | tf_op jit(solution)/shard_map/ppermute | solution.py:184
  75.1 35.4 %all-to-all-start.1 = ((bf16[16,256,128]{2,1,0:T(8,128)(2,1)}), bf16[16,256,128]{2,1,0:T(8,128)(2,1)}, u32[]{:S(2)}, u32[]{:S(2)}) async-start(bf16[16,256,128]{2,1,0:T(8,128)(2,1)} %shard_map.80), calls=%async_computation.1 | async-start | bytes 2097152 | tf_op jit(solution)/shard_map/all_to_all | solution.py:188
  83.0 4.8 %collective-permute-start.7 = (bf16[8,512,128]{2,1,0:T(8,128)(2,1)}, bf16[8,512,128]{2,1,0:T(8,128)(2,1)S(1)}, u32[]{:S(2)}, u32[]{:S(2)}) collective-permute-start(bf16[8,512,128]{2,1,0:T(8,128)(2,1)} %all-to-all-done.2.c0), channel_id=1, source_target_pairs={{0,1},{1,0},{2,3},{3,2},{4,5},{5,4},{6,7},{7,6},{8,9},{9,8},{10,11... | collective-permute-start | bytes 3145736 | tf_op jit(solution)/shard_map/ppermute | solution.py:184
  90.3 8.9 %collective-permute-start.8 = (bf16[128,128]{1,0:T(8,128)(2,1)S(1)}, bf16[128,128]{1,0:T(8,128)(2,1)S(1)}, u32[]{:S(2)}, u32[]{:S(2)}) collective-permute-start(bf16[128,128]{1,0:T(8,128)(2,1)S(1)} %get-tuple-element.18), channel_id=1, source_target_pairs={{32,0},{64,32},{96,64},{128,96},{160,128},{192,160},{224,192},{256... | collective-permute-start | bytes 98312 | tf_op jit(solution)/shard_map/ppermute | solution.py:175
  102.4 3.3 %collective-permute-start.9 = (bf16[256,384]{1,0:T(8,128)(2,1)S(1)}, bf16[256,384]{1,0:T(8,128)(2,1)S(1)}, u32[]{:S(2)}, u32[]{:S(2)}) collective-permute-start(bf16[256,384]{1,0:T(8,128)(2,1)S(1)} %shard_map.82.mine), channel_id=1, source_target_pairs={{0,1},{1,0},{2,3},{3,2},{4,5},{5,4},{6,7},{7,6},{8,9},{9,8},{10,11... | collective-permute-start | bytes 589832 | tf_op jit(solution)/shard_map/ppermute | solution.py:184
  110.5 37.6 %all-to-all-start.3 = ((bf16[16,256,128]{2,1,0:T(8,128)(2,1)}), bf16[16,256,128]{2,1,0:T(8,128)(2,1)S(1)}, u32[]{:S(2)}, u32[]{:S(2)}) async-start(bf16[16,256,128]{2,1,0:T(8,128)(2,1)} %shard_map.83), calls=%async_computation.3 | async-start | bytes 2097152 | tf_op jit(solution)/shard_map/all_to_all | solution.py:188

commit v3 on v2

v3 whole, which is shorter than its diff:
```python
import jax
import jax.numpy as jnp
from jax import lax
from jax.experimental import pallas as pl
from jax.experimental.pallas import tpu as pltpu
from jax.sharding import Mesh
from jax.sharding import PartitionSpec as P

X, Y, CORE = 2, 8, 2
SWAP = [(0, 1), (1, 0)]
LANES = 128
STRIP = 64
INTERPRET = False
BF, F32 = jnp.bfloat16, jnp.float32


def f32(a):
    return a.astype(F32)


def call(kernel, outs, scratch, flops, nbytes, *args):
    return pl.pallas_call(
        kernel,
        out_shape=[jax.ShapeDtypeStruct(s, d) for s, d in outs],
        in_specs=[pl.BlockSpec(memory_space=pltpu.SMEM)]
        + [pl.BlockSpec(memory_space=pltpu.VMEM)] * (len(args) - 1),
        out_specs=[pl.BlockSpec(memory_space=pltpu.VMEM)] * len(outs),
        scratch_shapes=scratch,
        cost_estimate=pl.CostEstimate(flops=flops, bytes_accessed=nbytes, transcendentals=0),
        compiler_params=pltpu.CompilerParams(vmem_limit_bytes=48 << 20),
        interpret=INTERPRET,
    )(*args)


def offset(pos, far, other, j):
    x = 1 - pos[0] if far else pos[0]
    core = 1 - pos[1] if other else pos[1]
    return pl.multiple_of(((x * Y + j) * CORE + core) * LANES, LANES)


def lay_out(pos, parts, whole):
    for j in range(Y):
        for other, part in enumerate(parts):
            at = pl.multiple_of((j * CORE + (1 - pos[1] if other else pos[1])) * LANES, LANES)
            whole[:, pl.ds(at, LANES)] = part[j]


def side(pos, far):
    x = 1 - pos[0] if far else pos[0]
    return pl.multiple_of(x * (Y * CORE * LANES), LANES)


def pack(pos, w, ow, sent_w, sent_ow):
    for far in range(2):
        for j in range(Y):
            off = offset(pos, far, 1, j)
            for b in range(3):
                sent_w[b, far * Y + j] = w[b, pl.ds(off, LANES), :].T
            sent_ow[far * Y + j] = ow[:, pl.ds(off, LANES)]


def turn(pos, w, own):
    for far in range(2):
        for j in range(Y):
            off = offset(pos, far, 0, j)
            for b in range(3):
                own[b, far * Y + j] = w[b, pl.ds(off, LANES), :].T


def project_side(pos, far, t0, t1, w, whole):
    lay_out(pos, (t0, t1), whole)
    rows = pl.ds(side(pos, far), whole.shape[1])
    rhs = jnp.concatenate([w[b, rows, :] for b in range(3)], axis=1)
    return jnp.dot(whole[...], rhs, preferred_element_type=F32)


def project_near(pos, t0, t1, w, near, whole):
    near[...] = project_side(pos, 0, t0, t1, w, whole)


def project(pos, t2, t3, near, w, q, k, v, mix, tail, whole):
    proj = (near[...] + project_side(pos, 1, t2, t3, w, whole)).astype(BF)
    q[...] = proj[:, :LANES]
    k[...] = proj[:, LANES : 2 * LANES]
    v[...] = proj[:, 2 * LANES :]
    product = (f32(proj[:, LANES : 2 * LANES]) * f32(proj[:, 2 * LANES :])).astype(BF)
    mix[...] = product
    tail[...] = product[-tail.shape[0] :]


def shift_all(ext, shifted, back):
    total = ext.shape[0]
    for b in range(8):
        by = (total - b) % total if back else b
        shifted[b] = pltpu.roll(ext, by, 0) if by else ext


def strip_sum(at, zero, first, last, limit, taps, shifted, back):
    lim = limit[at : at + STRIP, :]

    def eight(a, acc):
        start = pl.multiple_of(zero + 8 * a if back else zero - 8 * a, 8)
        for b in range(8):
            s = 8 * a + b
            piece = shifted[b, pl.ds(start, STRIP), :]
            acc = acc + jnp.where(lim >= s, piece, 0.0) * taps[pl.ds(s, 1), :]
        return acc

    return lax.fori_loop(first, last, eight, jnp.zeros((STRIP, LANES), F32))


def filtered_near(pos, mix, reach, taps, near, shifted):
    n_taps = taps.shape[0]
    shift_all(jnp.concatenate([jnp.zeros((n_taps, LANES), F32), f32(mix[...])], axis=0), shifted, False)
    for at in range(0, mix.shape[0], STRIP):
        last = min(n_taps, at + STRIP) // 8
        near[at : at + STRIP] = strip_sum(at, n_taps + at, 0, last, reach, taps, shifted, False)


def filtered(pos, prior, near, q, reach, taps, conv, gated, shifted):
    n_taps = taps.shape[0]
    shift_all(jnp.concatenate([f32(prior[...]), jnp.zeros((n_taps, LANES), F32)], axis=0), shifted, False)
    for at in range(0, conv.shape[0], STRIP):
        total = near[at : at + STRIP]
        if at < n_taps:
            total += strip_sum(at, n_taps + at, at // 8, n_taps // 8, reach, taps, shifted, False)
        conv[at : at + STRIP] = total
        gated[at : at + STRIP] = (f32(q[at : at + STRIP]) * total).astype(BF)


def slot(pos, far, j):
    return (1 - pos[0] if far else pos[0]) * Y + j


def out_terms(pos, mine, theirs, w, given, terms):
    both = jnp.concatenate([mine[...], theirs[...]], axis=1)
    for far in range(2):
        for j in range(0, Y, 2):
            rhs = jnp.concatenate(
                [
                    jnp.concatenate(
                        [w[:, pl.ds(offset(pos, far, 0, i), LANES)], given[far * Y + i]], axis=0
                    )
                    for i in (j, j + 1)
                ],
                axis=1,
            )
            term = jnp.dot(both, rhs, preferred_element_type=F32).astype(BF)
            terms[slot(pos, far, j)] = term[:, :LANES]
            terms[slot(pos, far, j + 1)] = term[:, LANES:]


def gate_side(pos, other, part, w, whole, weights):
    rows = whole.shape[0]
    for far in range(2):
        for j in range(Y):
            at = (far * Y + j) * LANES
            whole[:, at : at + LANES] = part[j, far * rows : (far + 1) * rows]
            weights[:, at : at + LANES] = w[:, pl.ds(offset(pos, far, other, j), LANES)]
    return lax.dot_general(
        whole[...], weights[...], (((1,), (1,)), ((), ())), preferred_element_type=F32
    )


def gate_near(pos, c0, w, near, whole, weights):
    near[...] = gate_side(pos, 0, c0, w, whole, weights)


def back_gate(pos, c1, near, w, q, dgated, dconv, head, whole, weights):
    total = near[...] + gate_side(pos, 1, c1, w, whole, weights)
    dgated[...] = total
    d = (total * f32(q[...])).astype(BF)
    dconv[...] = d
    head[...] = d[: head.shape[0]]


def back_near(pos, dconv, rem, taps, near, shifted):
    n_taps, rows = taps.shape[0], dconv.shape[0]
    shift_all(jnp.concatenate([f32(dconv[...]), jnp.zeros((n_taps, LANES), F32)], axis=0), shifted, True)
    for at in range(0, rows, STRIP):
        last = min(n_taps, rows - at) // 8
        near[at : at + STRIP] = strip_sum(at, at, 0, last, rem, taps, shifted, True)


def back_filtered(pos, after, near, k, v, dgated, conv, rem, taps, dproj, shifted):
    n_taps, rows = taps.shape[0], near.shape[0]
    shift_all(jnp.concatenate([jnp.zeros((n_taps, LANES), F32), f32(after[...])], axis=0), shifted, True)
    for at in range(0, rows, STRIP):
        here = slice(at, at + STRIP)
        dmix = near[here]
        left = rows - at - STRIP
        if left < n_taps:
            first = left // 8
            dmix += strip_sum(
                at, at - (rows - n_taps), first, n_taps // 8, rem, taps, shifted, True
            )
        dproj[here, :LANES] = (dgated[here] * conv[here]).astype(BF)
        dproj[here, LANES : 2 * LANES] = (dmix * f32(v[here])).astype(BF)
        dproj[here, 2 * LANES :] = (dmix * f32(k[here])).astype(BF)


def grad_terms(pos, mine, theirs, own, given, near, far_terms):
    both = jnp.concatenate([mine[...], theirs[...]], axis=1)
    for far, terms in ((1, far_terms), (0, near)):
        for j in range(0, Y, 2):
            rhs = jnp.concatenate(
                [
                    jnp.concatenate(
                        [own[b, far * Y + i] for b in range(3)]
                        + [given[b, far * Y + i] for b in range(3)],
                        axis=0,
                    )
                    for i in (j, j + 1)
                ],
                axis=1,
            )
            term = jnp.dot(both, rhs, preferred_element_type=F32).astype(BF)
            terms[j] = term[:, :LANES]
            terms[j + 1] = term[:, LANES:]


def passed_along(block, distance):
    devices = range(lax.axis_size("ctx"))
    route = [(i - distance, i) for i in devices if i - distance in devices]
    return lax.ppermute(block, "ctx", route)


def spread_y(block):
    copies = jnp.broadcast_to(block[None], (Y,) + block.shape)
    return lax.all_to_all(copies, "y", split_axis=0, concat_axis=0, tiled=True)


def swapped(block, axis):
    return lax.ppermute(block, axis, SWAP)


def summed(terms, axes):
    arrived = lax.all_to_all(terms, axes, split_axis=0, concat_axis=0, tiled=True)
    return f32(arrived).sum(axis=0).astype(BF)


def block_step(tokens, cotangent, in_weight, filter_taps, out_weight, segment_ids):
    width, _, chans = in_weight.shape
    rows = tokens.shape[0]
    taps = filter_taps.shape[0]
    n_chips = X * Y
    block, edge, triple = (rows, chans), (taps, chans), (rows, 3 * chans)
    weights = [pltpu.VMEM((chans, width // 2), BF)]
    half = [pltpu.VMEM((rows, width // 2), BF)]
    long = [pltpu.VMEM((8, rows + taps, chans), F32)]
    short = [pltpu.VMEM((8, 2 * taps, chans), F32)]
    macs = rows * width * chans
    small = rows * width * 2

    w3 = in_weight.transpose(1, 0, 2)
    pos = jnp.stack([lax.axis_index("x"), lax.axis_index("core")]).astype(jnp.int32)
    t0 = spread_y(tokens)
    far_cot = swapped(cotangent, "x")
    sent_w, sent_ow = call(
        pack,
        [((3, n_chips, chans, LANES), BF), ((n_chips, chans, LANES), BF)], [],
        macs, 4 * small, pos, w3, out_weight,
    )
    given_w = swapped(sent_w, "core")
    given_ow = swapped(sent_ow, "core")
    (own_w,) = call(turn, [((3, n_chips, chans, LANES), BF)], [], macs, 4 * small, pos, w3)
    base = lax.axis_index("ctx") * rows
    positions = base + jnp.arange(rows, dtype=jnp.int32)
    seg_here = lax.dynamic_slice_in_dim(segment_ids, base, rows)
    first = jnp.sum((segment_ids[None, :] < seg_here[:, None]).astype(jnp.int32), axis=1)
    end = jnp.sum((segment_ids[None, :] <= seg_here[:, None]).astype(jnp.int32), axis=1)
    reach = jnp.broadcast_to((positions - first)[:, None], block)
    rem = jnp.broadcast_to((end - 1 - positions)[:, None], block)

    c0 = spread_y(jnp.concatenate([cotangent, far_cot], axis=0))
    t2 = swapped(t0, "x")
    t1 = swapped(t0, "core")
    t3 = swapped(t2, "core")
    c1 = swapped(c0, "core")

    (near,) = call(project_near, [(triple, F32)], half, 3 * macs, 2 * small, pos, t0, t1, w3)
    q, k, v, mix, tail = call(
        project, [(block, BF)] * 4 + [(edge, BF)], half,
        3 * macs, 2 * small, pos, t2, t3, near, w3,
    )
    prior = passed_along(tail, 1)
    (near,) = call(
        filtered_near, [(block, F32)], long,
        macs, small, pos, mix, reach, filter_taps,
    )
    conv, gated = call(
        filtered, [(block, F32), (block, BF)], short,
        macs // 2, small // 2, pos, prior, near, q, reach, filter_taps,
    )
    theirs = swapped(gated, "core")
    (terms,) = call(
        out_terms, [((n_chips, rows, LANES), BF)], [],
        2 * macs, 2 * small, pos, gated, theirs, out_weight, given_ow,
    )
    block_out = summed(terms, ("x", "y"))
    (near,) = call(gate_near, [(block, F32)], half + weights, macs, small, pos, c0, out_weight)
    dgated, dconv, head = call(
        back_gate, [(block, F32), (block, BF), (edge, BF)], half + weights,
        macs, small, pos, c1, near, out_weight, q,
    )
    after = passed_along(head, -1)
    (near,) = call(back_near, [(block, F32)], long, macs, small, pos, dconv, rem, filter_taps)
    (dproj,) = call(
        back_filtered, [(triple, BF)], short,
        macs // 2, small // 2, pos, after, near, k, v, dgated, conv, rem, filter_taps,
    )
    theirs = swapped(dproj, "core")
    near, far = call(
        grad_terms, [((Y, rows, LANES), BF)] * 2, [],
        6 * macs, 4 * small, pos, dproj, theirs, own_w, given_w,
    )
    got = swapped(far, "x")
    return block_out, summed((f32(near) + f32(got)).astype(BF), "y")


def solution(mesh):
    fine = Mesh(
        mesh.devices.reshape(mesh.shape["ctx"], X, Y, CORE), ("ctx", "x", "y", "core")
    )
    tp = ("x", "y", "core")
    placed = (P("ctx", tp), P("ctx", tp), P(None, None, tp), P(None, tp), P(tp, None), P())
    return jax.shard_map(
        block_step,
        mesh=fine,
        in_specs=placed,
        out_specs=(P("ctx", tp), P("ctx", tp)),
        check_vma=False,
    )
```

time: 150 us -> 161 us (1.073)
  the two profiles are of different devices: /device:TPU:512 before, /device:TPU:196 now
where the time goes in v3:
time: 161 us; the launch traced here: 160 us
  starting transfers between devices  59.2 us (37%)
  waiting for transfers between devices  58.7 us (36%)
  Pallas kernels  25 us (16%)
  local copies, waits for them, and re-layouts  9.6 us (6%)
  other arithmetic  6.1 us (4%)
    ppermute x10, waiting for transfers between devices, swapped(): return lax.ppermute(block, axis, SWAP)  28 us
    pallas_call x12, Pallas kernels, call(): pl.pallas_call(kernel, out_shape=[jax.ShapeDtypeStruct(s, d) for s, d in...  25 us
    ppermute x10, starting transfers between devices, swapped(): return lax.ppermute(block, axis, SWAP)  24 us
    all_to_all x2, starting transfers between devices, summed(): lax.all_to_all(terms, axes, split_axis=0, concat_axis=0, tiled=True)  16.2 us
    all_to_all x2, waiting for transfers between devices, summed(): lax.all_to_all(terms, axes, split_axis=0, concat_axis=0, tiled=True)  14.9 us
    all_to_all x2, starting transfers between devices, spread_y(): return lax.all_to_all(copies, 'y', split_axis=0, concat_axis=0, tiled=True)  11.6 us
    all_to_all x2, waiting for transfers between devices, spread_y(): return lax.all_to_all(copies, 'y', split_axis=0, concat_axis=0, tiled=True)  10.7 us
    ppermute x2, starting transfers between devices, passed_along(): return lax.ppermute(block, 'ctx', route)  7.35 us
  transfers between devices with their start and end apart: 16, of which 9 were waited for; matrix products, arithmetic and copies ran while one was open for 4% of the time, Pallas kernels for 16%

profile of v3, /device:TPU:196, one launch (start us, length us, event | category | flops | bytes accessed | tf_op | source)
XLA Modules:
  0.0 159.6 jit_solution(15712282381147882652)
XLA Ops:
  0.6 1.7 %broadcast_in_dim.8 = bf16[8,256,128]{2,1,0:T(8,128)(2,1)} broadcast(bf16[256,128]{1,0:T(8,128)(2,1)} %param.6), dimensions={1,2} | broadcast | bytes 589824 | tf_op jit(solution)/shard_map/broadcast_in_dim | solution.py:229
  2.3 7.1 %all-to-all-start = ((bf16[8,256,128]{2,1,0:T(8,128)(2,1)}), bf16[8,256,128]{2,1,0:T(8,128)(2,1)S(1)}, u32[]{:S(2)}, u32[]{:S(2)}) async-start(bf16[8,256,128]{2,1,0:T(8,128)(2,1)} %broadcast_in_dim.8), calls=%async_computation | async-start | bytes 1048576 | tf_op jit(solution)/shard_map/all_to_all | solution.py:230
  9.4 3.1 %collective-permute-start.6 = (bf16[256,128]{1,0:T(8,128)(2,1)}, bf16[256,128]{1,0:T(8,128)(2,1)S(1)}, u32[]{:S(2)}, u32[]{:S(2)}) collective-permute-start(bf16[256,128]{1,0:T(8,128)(2,1)} %param.7), channel_id=1, source_target_pairs={{0,16},{16,0},{1,17},{17,1},{2,18},{18,2},{3,19},{19,3},{4,20},{20... | collective-permute-start | bytes 196616 | tf_op jit(solution)/shard_map/ppermute | solution.py:234
  12.6 3.3 %collective-permute-done.6 = bf16[256,128]{1,0:T(8,128)(2,1)S(1)} collective-permute-done((bf16[256,128]{1,0:T(8,128)(2,1)}, bf16[256,128]{1,0:T(8,128)(2,1)S(1)}, u32[]{:S(2)}, u32[]{:S(2)}) %collective-permute-start.6) | collective-permute-done | bytes 65568 | tf_op jit(solution)/shard_map/ppermute | solution.py:234
  16.7 10.3 %all-to-all-done.t0 = bf16[8,256,128]{2,1,0:T(8,128)(2,1)S(1)} async-done(((bf16[8,256,128]{2,1,0:T(8,128)(2,1)}), bf16[8,256,128]{2,1,0:T(8,128)(2,1)S(1)}, u32[]{:S(2)}, u32[]{:S(2)}) %all-to-all-start) | async-done | bytes 524320 | tf_op jit(solution)/shard_map/all_to_all | solution.py:230
  28.9 4.5 %all-to-all-start.2 = ((bf16[8,512,128]{2,1,0:T(8,128)(2,1)}), bf16[8,512,128]{2,1,0:T(8,128)(2,1)}, u32[]{:S(2)}, u32[]{:S(2)}) async-start(bf16[8,512,128]{2,1,0:T(8,128)(2,1)} %broadcast_in_dim.10), calls=%async_computation.2 | async-start | bytes 2097152 | tf_op jit(solution)/shard_map/all_to_all | solution.py:230
  33.4 3.1 %collective-permute-start = (bf16[8,256,128]{2,1,0:T(8,128)(2,1)}, bf16[8,256,128]{2,1,0:T(8,128)(2,1)}, u32[]{:S(2)}, u32[]{:S(2)}) collective-permute-start(bf16[8,256,128]{2,1,0:T(8,128)(2,1)} %copy-done.6), channel_id=1, source_target_pairs={{0,16},{16,0},{1,17},{17,1},{2,18},{18,2},{3,19},{19,3},{4,20},{20... | collective-permute-start | bytes 1572872 | tf_op jit(solution)/shard_map/ppermute | solution.py:234
  36.5 1.9 %collective-permute-start.2 = (bf16[8,256,128]{2,1,0:T(8,128)(2,1)}, bf16[8,256,128]{2,1,0:T(8,128)(2,1)}, u32[]{:S(2)}, u32[]{:S(2)}) collective-permute-start(bf16[8,256,128]{2,1,0:T(8,128)(2,1)} %copy-done.6), channel_id=1, source_target_pairs={{0,1},{1,0},{2,3},{3,2},{4,5},{5,4},{6,7},{7,6},{8,9},{9,8},{10,11... | collective-permute-start | bytes 1572872 | tf_op jit(solution)/shard_map/ppermute | solution.py:234
  38.5 11.0 %collective-permute-done.t2 = bf16[8,256,128]{2,1,0:T(8,128)(2,1)} collective-permute-done((bf16[8,256,128]{2,1,0:T(8,128)(2,1)}, bf16[8,256,128]{2,1,0:T(8,128)(2,1)}, u32[]{:S(2)}, u32[]{:S(2)}) %collective-permute-start) | collective-permute-done | bytes 524320 | tf_op jit(solution)/shard_map/ppermute | solution.py:234
  49.5 1.9 %collective-permute-start.1 = (bf16[8,256,128]{2,1,0:T(8,128)(2,1)}, bf16[8,256,128]{2,1,0:T(8,128)(2,1)}, u32[]{:S(2)}, u32[]{:S(2)}) collective-permute-start(bf16[8,256,128]{2,1,0:T(8,128)(2,1)} %collective-permute-done.t2), channel_id=1, source_target_pairs={{0,1},{1,0},{2,3},{3,2},{4,5},{5,4},{6,7},{7,6},{8,9},{9,8},{10,11... | collective-permute-start | bytes 1572872 | tf_op jit(solution)/shard_map/ppermute | solution.py:234
  52.7 3.6 %shard_map.81 = (bf16[3,16,128,128]{3,2,1,0:T(8,128)(2,1)}, bf16[16,128,128]{2,1,0:T(8,128)(2,1)}) custom-call(s32[2]{0:T(128)S(1)} %pad_add_fusion.pos, bf16[3,4096,128]{2,1,0:T(8,128)(2,1)} %bitcast.3, bf16[128,4096]{1,0:T(8,128)(2,1)S(1)} %copy-done.1), custom_call_target="tpu_custom_call" | custom-call | flops 134217728 | bytes 8388608 | tf_op jit(solution)/shard_map/pallas_call | solution.py:22
  56.3 2.4 %collective-permute-start.10 = (bf16[3,16,128,128]{3,2,1,0:T(8,128)(2,1)}, bf16[3,16,128,128]{3,2,1,0:T(8,128)(2,1)}, u32[]{:S(2)}, u32[]{:S(2)}) collective-permute-start(bf16[3,16,128,128]{3,2,1,0:T(8,128)(2,1)} %get-tuple-element.27), channel_id=1, source_target_pairs={{0,1},{1,0},{2,3},{3,2},{4,5},{5,4},{6,7},{7,6},{8,9},{9,8},{10,11... | collective-permute-start | bytes 4718600 | tf_op jit(solution)/shard_map/ppermute | solution.py:234
  58.7 1.9 %collective-permute-start.5 = (bf16[16,128,128]{2,1,0:T(8,128)(2,1)}, bf16[16,128,128]{2,1,0:T(8,128)(2,1)}, u32[]{:S(2)}, u32[]{:S(2)}) collective-permute-start(bf16[16,128,128]{2,1,0:T(8,128)(2,1)} %get-tuple-element.20), channel_id=1, source_target_pairs={{0,1},{1,0},{2,3},{3,2},{4,5},{5,4},{6,7},{7,6},{8,9},{9,8},{10,11... | collective-permute-start | bytes 1572872 | tf_op jit(solution)/shard_map/ppermute | solution.py:234
  62.6 2.0 %collective-permute-start.7 = (bf16[8,512,128]{2,1,0:T(8,128)(2,1)}, bf16[8,512,128]{2,1,0:T(8,128)(2,1)}, u32[]{:S(2)}, u32[]{:S(2)}) collective-permute-start(bf16[8,512,128]{2,1,0:T(8,128)(2,1)} %all-to-all-done.2.c0), channel_id=1, source_target_pairs={{0,1},{1,0},{2,3},{3,2},{4,5},{5,4},{6,7},{7,6},{8,9},{9,8},{10,11... | collective-permute-start | bytes 3145736 | tf_op jit(solution)/shard_map/ppermute | solution.py:234
  65.7 2.0 %shard_map.77.near = f32[256,384]{1,0:T(8,128)S(1)} custom-call(s32[2]{0:T(128)S(1)} %pad_add_fusion.pos, bf16[8,256,128]{2,1,0:T(8,128)(2,1)S(1)} %copy-done.7, bf16[8,256,128]{2,1,0:T(8,128)(2,1)} %collective-permute-done.2.t1, bf16[3,4096,128]{2,1,0:T(8,128)(2,1)S(1)} %bitcast.4), custom_call_target="tpu_custom_call" | custom-call | flops 402653184 | bytes 4194304 | tf_op jit(solution)/shard_map/pallas_call | solution.py:22
  67.8 2.3 %shard_map.78 = (bf16[256,128]{1,0:T(8,128)(2,1)S(1)}, bf16[256,128]{1,0:T(8,128)(2,1)S(1)}, bf16[256,128]{1,0:T(8,128)(2,1)S(1)}, bf16[256,128]{1,0:T(8,128)(2,1)S(1)}, bf16[128,128]{1,0:T(8,128)(2,1)S(1)}) custom-call(s32[2]{0:T(128)S(1)} %pad_add_fusion.pos, bf16[8,256,128]{2,1,0:T(8,128)(2,1)} %collective-permute-done.t2, ...), custom_call_target="tpu_custom_call" | custom-call | flops 402653184 | bytes 4194304 | tf_op jit(solution)/shard_map/pallas_call | solution.py:22
  70.1 5.4 %collective-permute-start.3 = (bf16[128,128]{1,0:T(8,128)(2,1)S(1)}, bf16[128,128]{1,0:T(8,128)(2,1)S(1)}, u32[]{:S(2)}, u32[]{:S(2)}) collective-permute-start(bf16[128,128]{1,0:T(8,128)(2,1)S(1)} %get-tuple-element.16), channel_id=1, source_target_pairs={{0,32},{32,64},{64,96},{96,128},{128,160},{160,192},{192,224},{224... | collective-permute-start | bytes 98312 | tf_op jit(solution)/shard_map/ppermute | solution.py:225
  75.7 2.7 %shard_map.79.near = f32[256,128]{1,0:T(8,128)S(1)} custom-call(s32[2]{0:T(128)S(1)} %pad_add_fusion.pos, bf16[256,128]{1,0:T(8,128)(2,1)S(1)} %get-tuple-element.17.mix, s32[256,128]{1,0:T(8,128)S(1)} %broadcast_in_dim.9.reach, f32[128,128]{1,0:T(8,128)S(1)} %copy-done.8), custom_call_target="tpu_custom_call" | custom-call | flops 134217728 | bytes 2097152 | tf_op jit(solution)/shard_map/pallas_call | solution.py:22
  79.9 2.0 %collective-permute-start.4 = (bf16[256,128]{1,0:T(8,128)(2,1)S(1)}, bf16[256,128]{1,0:T(8,128)(2,1)S(1)}, u32[]{:S(2)}, u32[]{:S(2)}) collective-permute-start(bf16[256,128]{1,0:T(8,128)(2,1)S(1)} %get-tuple-element.19.mine), channel_id=1, source_target_pairs={{0,1},{1,0},{2,3},{3,2},{4,5},{5,4},{6,7},{7,6},{8,9},{9,8},{10,11... | collective-permute-start | bytes 196616 | tf_op jit(solution)/shard_map/ppermute | solution.py:234
  85.6 8.5 %all-to-all-start.1 = ((bf16[16,256,128]{2,1,0:T(8,128)(2,1)}), bf16[16,256,128]{2,1,0:T(8,128)(2,1)}, u32[]{:S(2)}, u32[]{:S(2)}) async-start(bf16[16,256,128]{2,1,0:T(8,128)(2,1)} %copy-done.5), calls=%async_computation.1 | async-start | bytes 2097152 | tf_op jit(solution)/shard_map/all_to_all | solution.py:238
  95.3 1.8 %shard_map.83.near = f32[256,128]{1,0:T(8,128)S(1)} custom-call(s32[2]{0:T(128)S(1)} %pad_add_fusion.pos, bf16[8,512,128]{2,1,0:T(8,128)(2,1)} %all-to-all-done.2.c0, bf16[128,4096]{1,0:T(8,128)(2,1)S(1)} %copy-done.3), custom_call_target="tpu_custom_call" | custom-call | flops 134217728 | bytes 2097152 | tf_op jit(solution)/shard_map/pallas_call | solution.py:22
  98.3 1.8 %shard_map.84 = (f32[256,128]{1,0:T(8,128)S(1)}, bf16[256,128]{1,0:T(8,128)(2,1)S(1)}, bf16[128,128]{1,0:T(8,128)(2,1)S(1)}) custom-call(s32[2]{0:T(128)S(1)} %pad_add_fusion.pos, bf16[8,512,128]{2,1,0:T(8,128)(2,1)} %collective-permute-done.7.c1, f32[256,128]{1,0:T(8,128)S(1)} %shard_map.83.near, bf16[128,4096]{1,0:T(8,128)(2,1)S(1)} %copy-done.4, ...), custom_call_target="tpu_custom_call" | custom-call | flops 134217728 | bytes 2097152 | tf_op jit(solution)/shard_map/pallas_call | solution.py:22
  100.1 1.9 %collective-permute-start.8 = (bf16[128,128]{1,0:T(8,128)(2,1)S(1)}, bf16[128,128]{1,0:T(8,128)(2,1)S(1)}, u32[]{:S(2)}, u32[]{:S(2)}) collective-permute-start(bf16[128,128]{1,0:T(8,128)(2,1)S(1)} %get-tuple-element.21), channel_id=1, source_target_pairs={{32,0},{64,32},{96,64},{128,96},{160,128},{192,160},{224,192},{256... | collective-permute-start | bytes 98312 | tf_op jit(solution)/shard_map/ppermute | solution.py:225
  102.2 2.8 %shard_map.85.near = f32[256,128]{1,0:T(8,128)S(1)} custom-call(s32[2]{0:T(128)S(1)} %pad_add_fusion.pos, bf16[256,128]{1,0:T(8,128)(2,1)S(1)} %get-tuple-element.22.dconv, s32[256,128]{1,0:T(8,128)S(1)} %broadcast_in_dim.11.rem, f32[128,128]{1,0:T(8,128)S(1)} %copy-done.8), custom_call_target="tpu_custom_call" | custom-call | flops 134217728 | bytes 2097152 | tf_op jit(solution)/shard_map/pallas_call | solution.py:22
  104.9 5.1 %collective-permute-done.8.after = bf16[128,128]{1,0:T(8,128)(2,1)S(1)} collective-permute-done((bf16[128,128]{1,0:T(8,128)(2,1)S(1)}, bf16[128,128]{1,0:T(8,128)(2,1)S(1)}, u32[]{:S(2)}, u32[]{:S(2)}) %collective-permute-start.8) | collective-permute-done | bytes 32800 | tf_op jit(solution)/shard_map/ppermute | solution.py:225
  111.6 1.9 %collective-permute-start.9 = (bf16[256,384]{1,0:T(8,128)(2,1)S(1)}, bf16[256,384]{1,0:T(8,128)(2,1)S(1)}, u32[]{:S(2)}, u32[]{:S(2)}) collective-permute-start(bf16[256,384]{1,0:T(8,128)(2,1)S(1)} %shard_map.86.mine), channel_id=1, source_target_pairs={{0,1},{1,0},{2,3},{3,2},{4,5},{5,4},{6,7},{7,6},{8,9},{9,8},{10,11... | collective-permute-start | bytes 589832 | tf_op jit(solution)/shard_map/ppermute | solution.py:234
  114.9 2.4 %shard_map.88 = (bf16[8,256,128]{2,1,0:T(8,128)(2,1)S(1)}, bf16[8,256,128]{2,1,0:T(8,128)(2,1)S(1)}) custom-call(s32[2]{0:T(128)S(1)} %pad_add_fusion.pos, bf16[256,384]{1,0:T(8,128)(2,1)S(1)} %shard_map.86.mine, bf16[256,384]{1,0:T(8,128)(2,1)S(1)} %collective-permute-done.9.theirs, bf16[3,16,128,128]{3,2,1,0:T(8,128)(2,1)S(1)} %shard_map.87.own, ...), custom_call_target="tpu_custom_call" | custom-call | flops 805306368 | bytes 8388608 | tf_op jit(solution)/shard_map/pallas_call | solution.py:22
  117.3 3.7 %collective-permute-start.11 = (bf16[8,256,128]{2,1,0:T(8,128)(2,1)S(1)}, bf16[8,256,128]{2,1,0:T(8,128)(2,1)S(1)}, u32[]{:S(2)}, u32[]{:S(2)}) collective-permute-start(bf16[8,256,128]{2,1,0:T(8,128)(2,1)S(1)} %get-tuple-element.29), channel_id=1, source_target_pairs={{0,16},{16,0},{1,17},{17,1},{2,18},{18,2},{3,19},{19,3},{4,20},{20... | collective-permute-start | bytes 1572872 | tf_op jit(solution)/shard_map/ppermute | solution.py:234
  121.1 12.2 %collective-permute-done.11 = bf16[8,256,128]{2,1,0:T(8,128)(2,1)S(1)} collective-permute-done((bf16[8,256,128]{2,1,0:T(8,128)(2,1)S(1)}, bf16[8,256,128]{2,1,0:T(8,128)(2,1)S(1)}, u32[]{:S(2)}, u32[]{:S(2)}) %collective-permute-start.11) | collective-permute-done | bytes 524320 | tf_op jit(solution)/shard_map/ppermute | solution.py:234
  134.2 7.7 %all-to-all-start.3 = ((bf16[8,256,128]{2,1,0:T(8,128)(2,1)}), bf16[8,256,128]{2,1,0:T(8,128)(2,1)S(1)}, u32[]{:S(2)}, u32[]{:S(2)}) async-start(bf16[8,256,128]{2,1,0:T(8,128)(2,1)} %add_convert_fusion), calls=%async_computation.3 | async-start | bytes 1048576 | tf_op jit(solution)/shard_map/all_to_all | solution.py:238
  141.9 2.0 %reduce_sum.43 = bf16[256,128]{1,0:T(8,128)(2,1)} reduce(bf16[16,256,128]{2,1,0:T(8,128)(2,1)} %all-to-all-done.1, bf16[]{:T(256)} %constant.24.clone.1), dimensions={0}, to_apply=%region_1.0 | reduce | flops 491520 | bytes 1114114 | tf_op jit(solution)/shard_map/reduce_sum | solution.py:239
  143.9 14.9 %all-to-all-done.3 = bf16[8,256,128]{2,1,0:T(8,128)(2,1)S(1)} async-done(((bf16[8,256,128]{2,1,0:T(8,128)(2,1)}), bf16[8,256,128]{2,1,0:T(8,128)(2,1)S(1)}, u32[]{:S(2)}, u32[]{:S(2)}) %all-to-all-start.3) | async-done | bytes 524320 | tf_op jit(solution)/shard_map/all_to_all | solution.py:238
  (45 shorter events, 19.5 us)
Async XLA Ops:
  2.3 24.6 %all-to-all-start = ((bf16[8,256,128]{2,1,0:T(8,128)(2,1)}), bf16[8,256,128]{2,1,0:T(8,128)(2,1)S(1)}, u32[]{:S(2)}, u32[]{:S(2)}) async-start(bf16[8,256,128]{2,1,0:T(8,128)(2,1)} %broadcast_in_dim.8), calls=%async_computation | async-start | bytes 1048576 | tf_op jit(solution)/shard_map/all_to_all | solution.py:230
  9.4 6.4 %collective-permute-start.6 = (bf16[256,128]{1,0:T(8,128)(2,1)}, bf16[256,128]{1,0:T(8,128)(2,1)S(1)}, u32[]{:S(2)}, u32[]{:S(2)}) collective-permute-start(bf16[256,128]{1,0:T(8,128)(2,1)} %param.7), channel_id=1, source_target_pairs={{0,16},{16,0},{1,17},{17,1},{2,18},{18,2},{3,19},{19,3},{4,20},{20... | collective-permute-start | bytes 196616 | tf_op jit(solution)/shard_map/ppermute | solution.py:234
  26.9 0.8 copy-start.6
  27.7 32.9 %copy-start.9 = (s32[6144]{0:T(1024)S(1)}, s32[6144]{0:T(1024)}, u32[]{:S(2)}) copy-start(s32[6144]{0:T(1024)} %param.11) | copy-start | bytes 73732
  28.9 35.8 %copy-start = (bf16[4096,3,128]{2,0,1:T(8,128)(2,1)S(1)}, bf16[4096,3,128]{2,0,1:T(8,128)(2,1)}, u32[]{:S(2)}) copy-start(bf16[4096,3,128]{2,0,1:T(8,128)(2,1)} %param.8) | copy-start | bytes 9437188
  28.9 33.7 %all-to-all-start.2 = ((bf16[8,512,128]{2,1,0:T(8,128)(2,1)}), bf16[8,512,128]{2,1,0:T(8,128)(2,1)}, u32[]{:S(2)}, u32[]{:S(2)}) async-start(bf16[8,512,128]{2,1,0:T(8,128)(2,1)} %broadcast_in_dim.10), calls=%async_computation.2 | async-start | bytes 2097152 | tf_op jit(solution)/shard_map/all_to_all | solution.py:230
  33.4 16.1 %collective-permute-start = (bf16[8,256,128]{2,1,0:T(8,128)(2,1)}, bf16[8,256,128]{2,1,0:T(8,128)(2,1)}, u32[]{:S(2)}, u32[]{:S(2)}) collective-permute-start(bf16[8,256,128]{2,1,0:T(8,128)(2,1)} %copy-done.6), channel_id=1, source_target_pairs={{0,16},{16,0},{1,17},{17,1},{2,18},{18,2},{3,19},{19,3},{4,20},{20... | collective-permute-start | bytes 1572872 | tf_op jit(solution)/shard_map/ppermute | solution.py:234
  36.5 28.1 %collective-permute-start.2 = (bf16[8,256,128]{2,1,0:T(8,128)(2,1)}, bf16[8,256,128]{2,1,0:T(8,128)(2,1)}, u32[]{:S(2)}, u32[]{:S(2)}) collective-permute-start(bf16[8,256,128]{2,1,0:T(8,128)(2,1)} %copy-done.6), channel_id=1, source_target_pairs={{0,1},{1,0},{2,3},{3,2},{4,5},{5,4},{6,7},{7,6},{8,9},{9,8},{10,11... | collective-permute-start | bytes 1572872 | tf_op jit(solution)/shard_map/ppermute | solution.py:234
  49.5 18.3 %collective-permute-start.1 = (bf16[8,256,128]{2,1,0:T(8,128)(2,1)}, bf16[8,256,128]{2,1,0:T(8,128)(2,1)}, u32[]{:S(2)}, u32[]{:S(2)}) collective-permute-start(bf16[8,256,128]{2,1,0:T(8,128)(2,1)} %collective-permute-done.t2), channel_id=1, source_target_pairs={{0,1},{1,0},{2,3},{3,2},{4,5},{5,4},{6,7},{7,6},{8,9},{9,8},{10,11... | collective-permute-start | bytes 1572872 | tf_op jit(solution)/shard_map/ppermute | solution.py:234
  51.5 1.2 copy-start.1
  56.3 58.2 %collective-permute-start.10 = (bf16[3,16,128,128]{3,2,1,0:T(8,128)(2,1)}, bf16[3,16,128,128]{3,2,1,0:T(8,128)(2,1)}, u32[]{:S(2)}, u32[]{:S(2)}) collective-permute-start(bf16[3,16,128,128]{3,2,1,0:T(8,128)(2,1)} %get-tuple-element.27), channel_id=1, source_target_pairs={{0,1},{1,0},{2,3},{3,2},{4,5},{5,4},{6,7},{7,6},{8,9},{9,8},{10,11... | collective-permute-start | bytes 4718600 | tf_op jit(solution)/shard_map/ppermute | solution.py:234
  58.7 23.3 %collective-permute-start.5 = (bf16[16,128,128]{2,1,0:T(8,128)(2,1)}, bf16[16,128,128]{2,1,0:T(8,128)(2,1)}, u32[]{:S(2)}, u32[]{:S(2)}) collective-permute-start(bf16[16,128,128]{2,1,0:T(8,128)(2,1)} %get-tuple-element.20), channel_id=1, source_target_pairs={{0,1},{1,0},{2,3},{3,2},{4,5},{5,4},{6,7},{7,6},{8,9},{9,8},{10,11... | collective-permute-start | bytes 1572872 | tf_op jit(solution)/shard_map/ppermute | solution.py:234
  62.6 34.5 %collective-permute-start.7 = (bf16[8,512,128]{2,1,0:T(8,128)(2,1)}, bf16[8,512,128]{2,1,0:T(8,128)(2,1)}, u32[]{:S(2)}, u32[]{:S(2)}) collective-permute-start(bf16[8,512,128]{2,1,0:T(8,128)(2,1)} %all-to-all-done.2.c0), channel_id=1, source_target_pairs={{0,1},{1,0},{2,3},{3,2},{4,5},{5,4},{6,7},{7,6},{8,9},{9,8},{10,11... | collective-permute-start | bytes 3145736 | tf_op jit(solution)/shard_map/ppermute | solution.py:234
  64.7 1.0 copy-start.7
  67.8 7.9 %copy-start.8 = (f32[128,128]{1,0:T(8,128)S(1)}, f32[128,128]{1,0:T(8,128)}, u32[]{:S(2)}) copy-start(f32[128,128]{1,0:T(8,128)} %taps.7) | copy-start | bytes 196612
  67.8 15.3 %copy-start.2 = (bf16[128,4096]{1,0:T(8,128)(2,1)S(1)}, bf16[128,4096]{1,0:T(8,128)(2,1)}, u32[]{:S(2)}) copy-start(bf16[128,4096]{1,0:T(8,128)(2,1)} %w.5) | copy-start | bytes 3145732
  70.1 8.3 %collective-permute-start.3 = (bf16[128,128]{1,0:T(8,128)(2,1)S(1)}, bf16[128,128]{1,0:T(8,128)(2,1)S(1)}, u32[]{:S(2)}, u32[]{:S(2)}) collective-permute-start(bf16[128,128]{1,0:T(8,128)(2,1)S(1)} %get-tuple-element.16), channel_id=1, source_target_pairs={{0,32},{32,64},{64,96},{96,128},{128,160},{160,192},{192,224},{224... | collective-permute-start | bytes 98312 | tf_op jit(solution)/shard_map/ppermute | solution.py:225
  79.9 3.1 %collective-permute-start.4 = (bf16[256,128]{1,0:T(8,128)(2,1)S(1)}, bf16[256,128]{1,0:T(8,128)(2,1)S(1)}, u32[]{:S(2)}, u32[]{:S(2)}) collective-permute-start(bf16[256,128]{1,0:T(8,128)(2,1)S(1)} %get-tuple-element.19.mine), channel_id=1, source_target_pairs={{0,1},{1,0},{2,3},{3,2},{4,5},{5,4},{6,7},{7,6},{8,9},{9,8},{10,11... | collective-permute-start | bytes 196616 | tf_op jit(solution)/shard_map/ppermute | solution.py:234
  84.6 1.0 copy-start.5
  85.6 48.6 %all-to-all-start.1 = ((bf16[16,256,128]{2,1,0:T(8,128)(2,1)}), bf16[16,256,128]{2,1,0:T(8,128)(2,1)}, u32[]{:S(2)}, u32[]{:S(2)}) async-start(bf16[16,256,128]{2,1,0:T(8,128)(2,1)} %copy-done.5), calls=%async_computation.1 | async-start | bytes 2097152 | tf_op jit(solution)/shard_map/all_to_all | solution.py:238
  94.1 1.2 copy-start.3
  97.1 1.2 copy-start.4
  100.1 9.9 %collective-permute-start.8 = (bf16[128,128]{1,0:T(8,128)(2,1)S(1)}, bf16[128,128]{1,0:T(8,128)(2,1)S(1)}, u32[]{:S(2)}, u32[]{:S(2)}) collective-permute-start(bf16[128,128]{1,0:T(8,128)(2,1)S(1)} %get-tuple-element.21), channel_id=1, source_target_pairs={{32,0},{64,32},{96,64},{128,96},{160,128},{192,160},{224,192},{256... | collective-permute-start | bytes 98312 | tf_op jit(solution)/shard_map/ppermute | solution.py:225
  111.6 3.3 %collective-permute-start.9 = (bf16[256,384]{1,0:T(8,128)(2,1)S(1)}, bf16[256,384]{1,0:T(8,128)(2,1)S(1)}, u32[]{:S(2)}, u32[]{:S(2)}) collective-permute-start(bf16[256,384]{1,0:T(8,128)(2,1)S(1)} %shard_map.86.mine), channel_id=1, source_target_pairs={{0,1},{1,0},{2,3},{3,2},{4,5},{5,4},{6,7},{7,6},{8,9},{9,8},{10,11... | collective-permute-start | bytes 589832 | tf_op jit(solution)/shard_map/ppermute | solution.py:234
  117.3 15.9 %collective-permute-start.11 = (bf16[8,256,128]{2,1,0:T(8,128)(2,1)S(1)}, bf16[8,256,128]{2,1,0:T(8,128)(2,1)S(1)}, u32[]{:S(2)}, u32[]{:S(2)}) collective-permute-start(bf16[8,256,128]{2,1,0:T(8,128)(2,1)S(1)} %get-tuple-element.29), channel_id=1, source_target_pairs={{0,16},{16,0},{1,17},{17,1},{2,18},{18,2},{3,19},{19,3},{4,20},{20... | collective-permute-start | bytes 1572872 | tf_op jit(solution)/shard_map/ppermute | solution.py:234
  134.2 24.7 %all-to-all-start.3 = ((bf16[8,256,128]{2,1,0:T(8,128)(2,1)}), bf16[8,256,128]{2,1,0:T(8,128)(2,1)S(1)}, u32[]{:S(2)}, u32[]{:S(2)}) async-start(bf16[8,256,128]{2,1,0:T(8,128)(2,1)} %add_convert_fusion), calls=%async_computation.3 | async-start | bytes 1048576 | tf_op jit(solution)/shard_map/all_to_all | solution.py:238

commit v4 on v3

--- a/solution.py
+++ b/solution.py
@@ -128,13 +128,9 @@
         gated[at : at + STRIP] = (f32(q[at : at + STRIP]) * total).astype(BF)
 
 
-def slot(pos, far, j):
-    return (1 - pos[0] if far else pos[0]) * Y + j
-
-
-def out_terms(pos, mine, theirs, w, given, terms):
+def out_terms(pos, mine, theirs, w, given, near, far_terms):
     both = jnp.concatenate([mine[...], theirs[...]], axis=1)
-    for far in range(2):
+    for far, terms in ((1, far_terms), (0, near)):
         for j in range(0, Y, 2):
             rhs = jnp.concatenate(
                 [
@@ -146,8 +142,14 @@
                 axis=1,
             )
             term = jnp.dot(both, rhs, preferred_element_type=F32).astype(BF)
-            terms[slot(pos, far, j)] = term[:, :LANES]
-            terms[slot(pos, far, j + 1)] = term[:, LANES:]
+            terms[j] = term[:, :LANES]
+            terms[j + 1] = term[:, LANES:]
+
+
+def fold(pos, near, got, *by_distance):
+    for d, out in enumerate(by_distance):
+        at = lax.rem(pos[2] + d, Y)
+        out[...] = (f32(near[at]) + f32(got[at])).astype(BF)
 
 
 def gate_side(pos, other, part, w, whole, weights):
@@ -199,24 +201,31 @@
         dproj[here, 2 * LANES :] = (dmix * f32(k[here])).astype(BF)
 
 
-def grad_terms(pos, mine, theirs, own, given, near, far_terms):
+def grad_terms(pos, mine, theirs, own, given, terms, far):
     both = jnp.concatenate([mine[...], theirs[...]], axis=1)
-    for far, terms in ((1, far_terms), (0, near)):
-        for j in range(0, Y, 2):
-            rhs = jnp.concatenate(
-                [
-                    jnp.concatenate(
-                        [own[b, far * Y + i] for b in range(3)]
-                        + [given[b, far * Y + i] for b in range(3)],
-                        axis=0,
-                    )
-                    for i in (j, j + 1)
-                ],
-                axis=1,
-            )
-            term = jnp.dot(both, rhs, preferred_element_type=F32).astype(BF)
-            terms[j] = term[:, :LANES]
-            terms[j + 1] = term[:, LANES:]
+    for j in range(0, Y, 2):
+        rhs = jnp.concatenate(
+            [
+                jnp.concatenate(
+                    [own[b, far * Y + i] for b in range(3)]
+                    + [given[b, far * Y + i] for b in range(3)],
+                    axis=0,
+                )
+                for i in (j, j + 1)
+            ],
+            axis=1,
+        )
+        term = jnp.dot(both, rhs, preferred_element_type=F32).astype(BF)
+        terms[j] = term[:, :LANES]
+        terms[j + 1] = term[:, LANES:]
+
+
+def grad_far(*refs):
+    grad_terms(*refs, 1)
+
+
+def grad_near(*refs):
+    grad_terms(*refs, 0)
 
 
 def passed_along(block, distance):
@@ -234,9 +243,17 @@
     return lax.ppermute(block, axis, SWAP)
 
 
-def summed(terms, axes):
-    arrived = lax.all_to_all(terms, axes, split_axis=0, concat_axis=0, tiled=True)
+def summed(terms):
+    arrived = lax.all_to_all(terms, "y", split_axis=0, concat_axis=0, tiled=True)
     return f32(arrived).sum(axis=0).astype(BF)
+
+
+def summed_by_steps(by_distance):
+    total = f32(by_distance[0])
+    for d in (4, 3, 5, 2, 6, 1, 7):
+        got = lax.ppermute(by_distance[d], "y", [(i, (i + d) % Y) for i in range(Y)])
+        total += f32(got)
+    return total.astype(BF)
 
 
 def block_step(tokens, cotangent, in_weight, filter_taps, out_weight, segment_ids):
@@ -253,7 +270,7 @@
     small = rows * width * 2
 
     w3 = in_weight.transpose(1, 0, 2)
-    pos = jnp.stack([lax.axis_index("x"), lax.axis_index("core")]).astype(jnp.int32)
+    pos = jnp.stack([lax.axis_index(n) for n in ("x", "core", "y")]).astype(jnp.int32)
     t0 = spread_y(tokens)
     far_cot = swapped(cotangent, "x")
     sent_w, sent_ow = call(
@@ -293,11 +310,13 @@
         macs // 2, small // 2, pos, prior, near, q, reach, filter_taps,
     )
     theirs = swapped(gated, "core")
-    (terms,) = call(
-        out_terms, [((n_chips, rows, LANES), BF)], [],
+    near, far = call(
+        out_terms, [((Y, rows, LANES), BF)] * 2, [],
         2 * macs, 2 * small, pos, gated, theirs, out_weight, given_ow,
     )
-    block_out = summed(terms, ("x", "y"))
+    got = swapped(far, "x")
+    parts = call(fold, [(block, BF)] * Y, [], small, 2 * small, pos, near, got)
+    block_out = summed_by_steps(parts)
     (near,) = call(gate_near, [(block, F32)], half + weights, macs, small, pos, c0, out_weight)
     dgated, dconv, head = call(
         back_gate, [(block, F32), (block, BF), (edge, BF)], half + weights,
@@ -310,12 +329,11 @@
         macs // 2, small // 2, pos, after, near, k, v, dgated, conv, rem, filter_taps,
     )
     theirs = swapped(dproj, "core")
-    near, far = call(
-        grad_terms, [((Y, rows, LANES), BF)] * 2, [],
-        6 * macs, 4 * small, pos, dproj, theirs, own_w, given_w,
-    )
+    weights = (dproj, theirs, own_w, given_w)
+    (far,) = call(grad_far, [((Y, rows, LANES), BF)], [], 3 * macs, 2 * small, pos, *weights)
     got = swapped(far, "x")
-    return block_out, summed((f32(near) + f32(got)).astype(BF), "y")
+    (near,) = call(grad_near, [((Y, rows, LANES), BF)], [], 3 * macs, 2 * small, pos, *weights)
+    return block_out, summed((f32(near) + f32(got)).astype(BF))
 
 
 def solution(mesh):

time: 161 us -> 176 us (1.093)
  the two profiles are of different devices: /device:TPU:196 before, /device:TPU:520 now
where the time goes in v4:
time: 176 us; the launch traced here: 175 us
  starting transfers between devices  85 us (48%)
  waiting for transfers between devices  51.7 us (29%)
  Pallas kernels  26.7 us (15%)
  local copies, waits for them, and re-layouts  5.17 us (3%)
  other arithmetic  4.79 us (3%)
    ppermute x7, starting transfers between devices, summed_by_steps(): lax.ppermute(by_distance[d], 'y', [(i, (i + d) % Y) for i in range(Y)])  29 us
    ppermute x11, starting transfers between devices, swapped(): return lax.ppermute(block, axis, SWAP)  28.2 us
    pallas_call x14, Pallas kernels, call(): pl.pallas_call(kernel, out_shape=[jax.ShapeDtypeStruct(s, d) for s, d in...  26.7 us
    all_to_all x2, waiting for transfers between devices, spread_y(): return lax.all_to_all(copies, 'y', split_axis=0, concat_axis=0, tiled=True)  25.8 us
    ppermute x11, waiting for transfers between devices, swapped(): return lax.ppermute(block, axis, SWAP)  20.7 us
    all_to_all x2, starting transfers between devices, spread_y(): return lax.all_to_all(copies, 'y', split_axis=0, concat_axis=0, tiled=True)  13.4 us
    ppermute x2, starting transfers between devices, passed_along(): return lax.ppermute(block, 'ctx', route)  9.46 us
    ppermute x7, waiting for transfers between devices, summed_by_steps(): lax.ppermute(by_distance[d], 'y', [(i, (i + d) % Y) for i in range(Y)])  5.19 us
  transfers between devices with their start and end apart: 23, of which 8 were waited for; matrix products, arithmetic and copies ran while one was open for 2% of the time, Pallas kernels for 14%

profile of v4, /device:TPU:520, one launch (start us, length us, event | category | flops | bytes accessed | tf_op | source)
XLA Modules:
  0.0 174.5 jit_solution(6355457922892910090)
XLA Ops:
  2.3 7.5 %all-to-all-start = ((bf16[8,256,128]{2,1,0:T(8,128)(2,1)}), bf16[8,256,128]{2,1,0:T(8,128)(2,1)}, u32[]{:S(2)}, u32[]{:S(2)}) async-start(bf16[8,256,128]{2,1,0:T(8,128)(2,1)} %broadcast_in_dim.8), calls=%async_computation | async-start | bytes 1048576 | tf_op jit(solution)/shard_map/all_to_all | solution.py:239
  9.9 3.4 %collective-permute-start.14 = (bf16[256,128]{1,0:T(8,128)(2,1)}, bf16[256,128]{1,0:T(8,128)(2,1)S(1)}, u32[]{:S(2)}, u32[]{:S(2)}) collective-permute-start(bf16[256,128]{1,0:T(8,128)(2,1)} %param.7), channel_id=1, source_target_pairs={{0,16},{16,0},{1,17},{17,1},{2,18},{18,2},{3,19},{19,3},{4,20},{20... | collective-permute-start | bytes 196616 | tf_op jit(solution)/shard_map/ppermute | solution.py:243
  13.3 3.0 %collective-permute-done.14 = bf16[256,128]{1,0:T(8,128)(2,1)S(1)} collective-permute-done((bf16[256,128]{1,0:T(8,128)(2,1)}, bf16[256,128]{1,0:T(8,128)(2,1)S(1)}, u32[]{:S(2)}, u32[]{:S(2)}) %collective-permute-start.14) | collective-permute-done | bytes 65568 | tf_op jit(solution)/shard_map/ppermute | solution.py:243
  17.1 8.9 %all-to-all-done.t0 = bf16[8,256,128]{2,1,0:T(8,128)(2,1)} async-done(((bf16[8,256,128]{2,1,0:T(8,128)(2,1)}), bf16[8,256,128]{2,1,0:T(8,128)(2,1)}, u32[]{:S(2)}, u32[]{:S(2)}) %all-to-all-start) | async-done | bytes 524320 | tf_op jit(solution)/shard_map/all_to_all | solution.py:239
  27.2 5.8 %all-to-all-start.1 = ((bf16[8,512,128]{2,1,0:T(8,128)(2,1)}), bf16[8,512,128]{2,1,0:T(8,128)(2,1)}, u32[]{:S(2)}, u32[]{:S(2)}) async-start(bf16[8,512,128]{2,1,0:T(8,128)(2,1)} %broadcast_in_dim.10), calls=%async_computation.1 | async-start | bytes 2097152 | tf_op jit(solution)/shard_map/all_to_all | solution.py:239
  34.3 3.6 %shard_map.81 = (bf16[3,16,128,128]{3,2,1,0:T(8,128)(2,1)}, bf16[16,128,128]{2,1,0:T(8,128)(2,1)S(1)}) custom-call(s32[3]{0:T(128)S(1)} %pad_add_fusion.pos.refs_0_, bf16[3,4096,128]{2,1,0:T(8,128)(2,1)} %bitcast.4, bf16[128,4096]{1,0:T(8,128)(2,1)S(1)} %copy-done.1), custom_call_target="tpu_custom_call" | custom-call | flops 134217728 | bytes 8388608 | tf_op jit(solution)/shard_map/pallas_call | solution.py:22
  40.6 3.4 %collective-permute-start = (bf16[8,256,128]{2,1,0:T(8,128)(2,1)}, bf16[8,256,128]{2,1,0:T(8,128)(2,1)}, u32[]{:S(2)}, u32[]{:S(2)}) collective-permute-start(bf16[8,256,128]{2,1,0:T(8,128)(2,1)} %all-to-all-done.t0), channel_id=1, source_target_pairs={{0,16},{16,0},{1,17},{17,1},{2,18},{18,2},{3,19},{19,3},{4,20},{20... | collective-permute-start | bytes 1572872 | tf_op jit(solution)/shard_map/ppermute | solution.py:243
  44.0 16.9 %all-to-all-done.1.c0 = bf16[8,512,128]{2,1,0:T(8,128)(2,1)} async-done(((bf16[8,512,128]{2,1,0:T(8,128)(2,1)}), bf16[8,512,128]{2,1,0:T(8,128)(2,1)}, u32[]{:S(2)}, u32[]{:S(2)}) %all-to-all-start.1) | async-done | bytes 1048608 | tf_op jit(solution)/shard_map/all_to_all | solution.py:239
  62.8 2.4 %collective-permute-start.2 = (bf16[8,256,128]{2,1,0:T(8,128)(2,1)}, bf16[8,256,128]{2,1,0:T(8,128)(2,1)}, u32[]{:S(2)}, u32[]{:S(2)}) collective-permute-start(bf16[8,256,128]{2,1,0:T(8,128)(2,1)} %all-to-all-done.t0), channel_id=1, source_target_pairs={{0,1},{1,0},{2,3},{3,2},{4,5},{5,4},{6,7},{7,6},{8,9},{9,8},{10,11... | collective-permute-start | bytes 1572872 | tf_op jit(solution)/shard_map/ppermute | solution.py:243
  65.4 2.0 %collective-permute-start.1 = (bf16[8,256,128]{2,1,0:T(8,128)(2,1)}, bf16[8,256,128]{2,1,0:T(8,128)(2,1)S(1)}, u32[]{:S(2)}, u32[]{:S(2)}) collective-permute-start(bf16[8,256,128]{2,1,0:T(8,128)(2,1)} %collective-permute-done.t2), channel_id=1, source_target_pairs={{0,1},{1,0},{2,3},{3,2},{4,5},{5,4},{6,7},{7,6},{8,9},{9,8},{10,11... | collective-permute-start | bytes 1572872 | tf_op jit(solution)/shard_map/ppermute | solution.py:243
  68.9 2.2 %shard_map.77.near = f32[256,384]{1,0:T(8,128)S(1)} custom-call(s32[3]{0:T(128)S(1)} %pad_add_fusion.pos.refs_0_, bf16[8,256,128]{2,1,0:T(8,128)(2,1)} %all-to-all-done.t0, bf16[8,256,128]{2,1,0:T(8,128)(2,1)} %collective-permute-done.2.t1, bf16[3,4096,128]{2,1,0:T(8,128)(2,1)S(1)} %bitcast.5), custom_call_target="tpu_custom_call" | custom-call | flops 402653184 | bytes 4194304 | tf_op jit(solution)/shard_map/pallas_call | solution.py:22
  73.0 2.1 %shard_map.78 = (bf16[256,128]{1,0:T(8,128)(2,1)S(1)}, bf16[256,128]{1,0:T(8,128)(2,1)S(1)}, bf16[256,128]{1,0:T(8,128)(2,1)S(1)}, bf16[256,128]{1,0:T(8,128)(2,1)S(1)}, bf16[128,128]{1,0:T(8,128)(2,1)S(1)}) custom-call(s32[3]{0:T(128)S(1)} %pad_add_fusion.pos.refs_0_, bf16[8,256,128]{2,1,0:T(8,128)(2,1)} %collective-permute-done.t2, ...), custom_call_target="tpu_custom_call" | custom-call | flops 402653184 | bytes 4194304 | tf_op jit(solution)/shard_map/pallas_call | solution.py:22
  75.1 4.9 %collective-permute-start.3 = (bf16[128,128]{1,0:T(8,128)(2,1)S(1)}, bf16[128,128]{1,0:T(8,128)(2,1)S(1)}, u32[]{:S(2)}, u32[]{:S(2)}) collective-permute-start(bf16[128,128]{1,0:T(8,128)(2,1)S(1)} %get-tuple-element.24), channel_id=1, source_target_pairs={{0,32},{32,64},{64,96},{96,128},{128,160},{160,192},{192,224},{224... | collective-permute-start | bytes 98312 | tf_op jit(solution)/shard_map/ppermute | solution.py:234
  81.8 4.5 %collective-permute-start.16 = (bf16[128,128]{1,0:T(8,128)(2,1)S(1)}, bf16[128,128]{1,0:T(8,128)(2,1)S(1)}, u32[]{:S(2)}, u32[]{:S(2)}) collective-permute-start(bf16[128,128]{1,0:T(8,128)(2,1)S(1)} %get-tuple-element.39), channel_id=1, source_target_pairs={{32,0},{64,32},{96,64},{128,96},{160,128},{192,160},{224,192},{256... | collective-permute-start | bytes 98312 | tf_op jit(solution)/shard_map/ppermute | solution.py:234
  86.5 2.7 %shard_map.79.near = f32[256,128]{1,0:T(8,128)S(1)} custom-call(s32[3]{0:T(128)S(1)} %pad_add_fusion.pos.refs_0_, bf16[256,128]{1,0:T(8,128)(2,1)S(1)} %get-tuple-element.25.mix, s32[256,128]{1,0:T(8,128)S(1)} %broadcast_in_dim.9.reach, f32[128,128]{1,0:T(8,128)S(1)} %copy-done.4), custom_call_target="tpu_custom_call" | custom-call | flops 134217728 | bytes 2097152 | tf_op jit(solution)/shard_map/pallas_call | solution.py:22
  90.8 2.8 %shard_map.86.near = f32[256,128]{1,0:T(8,128)S(1)} custom-call(s32[3]{0:T(128)S(1)} %pad_add_fusion.pos.refs_0_, bf16[256,128]{1,0:T(8,128)(2,1)S(1)} %get-tuple-element.40.dconv, s32[256,128]{1,0:T(8,128)S(1)} %broadcast_in_dim.11.rem, f32[128,128]{1,0:T(8,128)S(1)} %copy-done.4), custom_call_target="tpu_custom_call" | custom-call | flops 134217728 | bytes 2097152 | tf_op jit(solution)/shard_map/pallas_call | solution.py:22
  98.5 2.0 %shard_map.90 = bf16[8,256,128]{2,1,0:T(8,128)(2,1)S(1)} custom-call(s32[3]{0:T(128)S(1)} %pad_add_fusion.pos.refs_0_, bf16[256,384]{1,0:T(8,128)(2,1)S(1)} %shard_map.87.refs_1_, bf16[256,384]{1,0:T(8,128)(2,1)S(1)} %collective-permute-done.17.refs_2_, bf16[3,16,128,128]{3,2,1,0:T(8,128)(2,1)S(1)} %shard_map.88.refs_3_, ...), custom_call_target="tpu_custom_call" | custom-call | flops 402653184 | bytes 4194304 | tf_op jit(solution)/shard_map/pallas_call | solution.py:22
  100.5 3.4 %collective-permute-start.19 = (bf16[8,256,128]{2,1,0:T(8,128)(2,1)S(1)}, bf16[8,256,128]{2,1,0:T(8,128)(2,1)S(1)}, u32[]{:S(2)}, u32[]{:S(2)}) collective-permute-start(bf16[8,256,128]{2,1,0:T(8,128)(2,1)S(1)} %shard_map.90), channel_id=1, source_target_pairs={{0,16},{16,0},{1,17},{17,1},{2,18},{18,2},{3,19},{19,3},{4,20},{20... | collective-permute-start | bytes 1572872 | tf_op jit(solution)/shard_map/ppermute | solution.py:243
  105.9 2.5 %collective-permute-start.4 = (bf16[256,128]{1,0:T(8,128)(2,1)S(1)}, bf16[256,128]{1,0:T(8,128)(2,1)S(1)}, u32[]{:S(2)}, u32[]{:S(2)}) collective-permute-start(bf16[256,128]{1,0:T(8,128)(2,1)S(1)} %get-tuple-element.27.mine), channel_id=1, source_target_pairs={{0,1},{1,0},{2,3},{3,2},{4,5},{5,4},{6,7},{7,6},{8,9},{9,8},{10,11... | collective-permute-start | bytes 196616 | tf_op jit(solution)/shard_map/ppermute | solution.py:243
  108.4 2.0 %shard_map.89 = bf16[8,256,128]{2,1,0:T(8,128)(2,1)S(1)} custom-call(s32[3]{0:T(128)S(1)} %pad_add_fusion.pos.refs_0_, bf16[256,384]{1,0:T(8,128)(2,1)S(1)} %shard_map.87.refs_1_, bf16[256,384]{1,0:T(8,128)(2,1)S(1)} %collective-permute-done.17.refs_2_, bf16[3,16,128,128]{3,2,1,0:T(8,128)(2,1)S(1)} %shard_map.88.refs_3_, ...), custom_call_target="tpu_custom_call" | custom-call | flops 402653184 | bytes 4194304 | tf_op jit(solution)/shard_map/pallas_call | solution.py:22
  110.4 6.0 %collective-permute-done.19 = bf16[8,256,128]{2,1,0:T(8,128)(2,1)S(1)} collective-permute-done((bf16[8,256,128]{2,1,0:T(8,128)(2,1)S(1)}, bf16[8,256,128]{2,1,0:T(8,128)(2,1)S(1)}, u32[]{:S(2)}, u32[]{:S(2)}) %collective-permute-start.19) | collective-permute-done | bytes 524320 | tf_op jit(solution)/shard_map/ppermute | solution.py:243
  117.4 4.9 %all-to-all-start.2 = ((bf16[8,256,128]{2,1,0:T(8,128)(2,1)}), bf16[8,256,128]{2,1,0:T(8,128)(2,1)S(1)}, u32[]{:S(2)}, u32[]{:S(2)}) async-start(bf16[8,256,128]{2,1,0:T(8,128)(2,1)} %add_convert_fusion), calls=%async_computation.2 | async-start | bytes 1048576 | tf_op jit(solution)/shard_map/all_to_all | solution.py:247
  123.3 3.4 %collective-permute-start.6 = (bf16[8,256,128]{2,1,0:T(8,128)(2,1)S(1)}, bf16[8,256,128]{2,1,0:T(8,128)(2,1)S(1)}, u32[]{:S(2)}, u32[]{:S(2)}) collective-permute-start(bf16[8,256,128]{2,1,0:T(8,128)(2,1)S(1)} %get-tuple-element.30), channel_id=1, source_target_pairs={{0,16},{16,0},{1,17},{17,1},{2,18},{18,2},{3,19},{19,3},{4,20},{20... | collective-permute-start | bytes 1572872 | tf_op jit(solution)/shard_map/ppermute | solution.py:243
  126.7 11.4 %collective-permute-done.6.got = bf16[8,256,128]{2,1,0:T(8,128)(2,1)S(1)} collective-permute-done((bf16[8,256,128]{2,1,0:T(8,128)(2,1)S(1)}, bf16[8,256,128]{2,1,0:T(8,128)(2,1)S(1)}, u32[]{:S(2)}, u32[]{:S(2)}) %collective-permute-start.6) | collective-permute-done | bytes 524320 | tf_op jit(solution)/shard_map/ppermute | solution.py:243
  138.8 4.3 %collective-permute-start.10 = (bf16[256,128]{1,0:T(8,128)(2,1)S(1)}, bf16[256,128]{1,0:T(8,128)(2,1)S(1)}, u32[]{:S(2)}, u32[]{:S(2)}) collective-permute-start(bf16[256,128]{1,0:T(8,128)(2,1)S(1)} %get-tuple-element.35), channel_id=1, source_target_pairs={{0,4},{2,6},{4,8},{6,10},{8,12},{10,14},{12,0},{14,2},{1,5},{3,7},... | collective-permute-start | bytes 196616 | tf_op jit(solution)/shard_map/ppermute | solution.py:254
  143.1 3.7 %collective-permute-start.11 = (bf16[256,128]{1,0:T(8,128)(2,1)S(1)}, bf16[256,128]{1,0:T(8,128)(2,1)S(1)}, u32[]{:S(2)}, u32[]{:S(2)}) collective-permute-start(bf16[256,128]{1,0:T(8,128)(2,1)S(1)} %get-tuple-element.36), channel_id=1, source_target_pairs={{0,12},{2,14},{4,0},{6,2},{8,4},{10,6},{12,8},{14,10},{1,13},{3,15... | collective-permute-start | bytes 196616 | tf_op jit(solution)/shard_map/ppermute | solution.py:254
  146.7 2.8 %collective-permute-start.12 = (bf16[256,128]{1,0:T(8,128)(2,1)S(1)}, bf16[256,128]{1,0:T(8,128)(2,1)S(1)}, u32[]{:S(2)}, u32[]{:S(2)}) collective-permute-start(bf16[256,128]{1,0:T(8,128)(2,1)S(1)} %get-tuple-element.37), channel_id=1, source_target_pairs={{0,2},{2,4},{4,6},{6,8},{8,10},{10,12},{12,14},{14,0},{1,3},{3,5},... | collective-permute-start | bytes 196616 | tf_op jit(solution)/shard_map/ppermute | solution.py:254
  149.6 3.0 %collective-permute-start.13 = (bf16[256,128]{1,0:T(8,128)(2,1)S(1)}, bf16[256,128]{1,0:T(8,128)(2,1)S(1)}, u32[]{:S(2)}, u32[]{:S(2)}) collective-permute-start(bf16[256,128]{1,0:T(8,128)(2,1)S(1)} %get-tuple-element.38), channel_id=1, source_target_pairs={{0,14},{2,0},{4,2},{6,4},{8,6},{10,8},{12,10},{14,12},{1,15},{3,1}... | collective-permute-start | bytes 196616 | tf_op jit(solution)/shard_map/ppermute | solution.py:254
  152.6 6.4 %collective-permute-start.7 = (bf16[256,128]{1,0:T(8,128)(2,1)S(1)}, bf16[256,128]{1,0:T(8,128)(2,1)S(1)}, u32[]{:S(2)}, u32[]{:S(2)}) collective-permute-start(bf16[256,128]{1,0:T(8,128)(2,1)S(1)} %get-tuple-element.32), channel_id=1, source_target_pairs={{0,8},{2,10},{4,12},{6,14},{8,0},{10,2},{12,4},{14,6},{1,9},{3,11}... | collective-permute-start | bytes 196616 | tf_op jit(solution)/shard_map/ppermute | solution.py:254
  159.0 3.5 %collective-permute-start.8 = (bf16[256,128]{1,0:T(8,128)(2,1)S(1)}, bf16[256,128]{1,0:T(8,128)(2,1)S(1)}, u32[]{:S(2)}, u32[]{:S(2)}) collective-permute-start(bf16[256,128]{1,0:T(8,128)(2,1)S(1)} %get-tuple-element.33), channel_id=1, source_target_pairs={{0,6},{2,8},{4,10},{6,12},{8,14},{10,0},{12,2},{14,4},{1,7},{3,9},... | collective-permute-start | bytes 196616 | tf_op jit(solution)/shard_map/ppermute | solution.py:254
  162.5 5.4 %collective-permute-start.9 = (bf16[256,128]{1,0:T(8,128)(2,1)S(1)}, bf16[256,128]{1,0:T(8,128)(2,1)S(1)}, u32[]{:S(2)}, u32[]{:S(2)}) collective-permute-start(bf16[256,128]{1,0:T(8,128)(2,1)S(1)} %get-tuple-element.34), channel_id=1, source_target_pairs={{0,10},{2,12},{4,14},{6,0},{8,2},{10,4},{12,6},{14,8},{1,11},{3,13... | collective-permute-start | bytes 196616 | tf_op jit(solution)/shard_map/ppermute | solution.py:254
  168.3 4.8 %collective-permute-done.9 = bf16[256,128]{1,0:T(8,128)(2,1)S(1)} collective-permute-done((bf16[256,128]{1,0:T(8,128)(2,1)S(1)}, bf16[256,128]{1,0:T(8,128)(2,1)S(1)}, u32[]{:S(2)}, u32[]{:S(2)}) %collective-permute-start.9) | collective-permute-done | bytes 65568 | tf_op jit(solution)/shard_map/ppermute | solution.py:254
  (57 shorter events, 27.8 us)
Async XLA Ops:
  2.3 23.7 %all-to-all-start = ((bf16[8,256,128]{2,1,0:T(8,128)(2,1)}), bf16[8,256,128]{2,1,0:T(8,128)(2,1)}, u32[]{:S(2)}, u32[]{:S(2)}) async-start(bf16[8,256,128]{2,1,0:T(8,128)(2,1)} %broadcast_in_dim.8), calls=%async_computation | async-start | bytes 1048576 | tf_op jit(solution)/shard_map/all_to_all | solution.py:239
  9.9 6.4 %collective-permute-start.14 = (bf16[256,128]{1,0:T(8,128)(2,1)}, bf16[256,128]{1,0:T(8,128)(2,1)S(1)}, u32[]{:S(2)}, u32[]{:S(2)}) collective-permute-start(bf16[256,128]{1,0:T(8,128)(2,1)} %param.7), channel_id=1, source_target_pairs={{0,16},{16,0},{1,17},{17,1},{2,18},{18,2},{3,19},{19,3},{4,20},{20... | collective-permute-start | bytes 196616 | tf_op jit(solution)/shard_map/ppermute | solution.py:243
  26.0 39.2 %copy-start.7 = (s32[6144]{0:T(1024)S(1)}, s32[6144]{0:T(1024)}, u32[]{:S(2)}) copy-start(s32[6144]{0:T(1024)} %param.11) | copy-start | bytes 73732
  27.2 41.7 %copy-start = (bf16[4096,3,128]{2,0,1:T(8,128)(2,1)S(1)}, bf16[4096,3,128]{2,0,1:T(8,128)(2,1)}, u32[]{:S(2)}) copy-start(bf16[4096,3,128]{2,0,1:T(8,128)(2,1)} %param.8) | copy-start | bytes 9437188
  27.2 33.7 %all-to-all-start.1 = ((bf16[8,512,128]{2,1,0:T(8,128)(2,1)}), bf16[8,512,128]{2,1,0:T(8,128)(2,1)}, u32[]{:S(2)}, u32[]{:S(2)}) async-start(bf16[8,512,128]{2,1,0:T(8,128)(2,1)} %broadcast_in_dim.10), calls=%async_computation.1 | async-start | bytes 2097152 | tf_op jit(solution)/shard_map/all_to_all | solution.py:239
  33.1 1.2 copy-start.1
  37.9 0.8 copy-start.5
  38.7 59.4 %collective-permute-start.18 = (bf16[3,16,128,128]{3,2,1,0:T(8,128)(2,1)}, bf16[3,16,128,128]{3,2,1,0:T(8,128)(2,1)}, u32[]{:S(2)}, u32[]{:S(2)}) collective-permute-start(bf16[3,16,128,128]{3,2,1,0:T(8,128)(2,1)} %get-tuple-element.45), channel_id=1, source_target_pairs={{0,1},{1,0},{2,3},{3,2},{4,5},{5,4},{6,7},{7,6},{8,9},{9,8},{10,11... | collective-permute-start | bytes 4718600 | tf_op jit(solution)/shard_map/ppermute | solution.py:243
  40.6 24.7 %collective-permute-start = (bf16[8,256,128]{2,1,0:T(8,128)(2,1)}, bf16[8,256,128]{2,1,0:T(8,128)(2,1)}, u32[]{:S(2)}, u32[]{:S(2)}) collective-permute-start(bf16[8,256,128]{2,1,0:T(8,128)(2,1)} %all-to-all-done.t0), channel_id=1, source_target_pairs={{0,16},{16,0},{1,17},{17,1},{2,18},{18,2},{3,19},{19,3},{4,20},{20... | collective-permute-start | bytes 1572872 | tf_op jit(solution)/shard_map/ppermute | solution.py:243
  60.9 19.1 %collective-permute-start.15 = (bf16[8,512,128]{2,1,0:T(8,128)(2,1)}, bf16[8,512,128]{2,1,0:T(8,128)(2,1)}, u32[]{:S(2)}, u32[]{:S(2)}) collective-permute-start(bf16[8,512,128]{2,1,0:T(8,128)(2,1)} %all-to-all-done.1.c0), channel_id=1, source_target_pairs={{0,1},{1,0},{2,3},{3,2},{4,5},{5,4},{6,7},{7,6},{8,9},{9,8},{10,11... | collective-permute-start | bytes 3145736 | tf_op jit(solution)/shard_map/ppermute | solution.py:243
  62.8 6.1 %collective-permute-start.2 = (bf16[8,256,128]{2,1,0:T(8,128)(2,1)}, bf16[8,256,128]{2,1,0:T(8,128)(2,1)}, u32[]{:S(2)}, u32[]{:S(2)}) collective-permute-start(bf16[8,256,128]{2,1,0:T(8,128)(2,1)} %all-to-all-done.t0), channel_id=1, source_target_pairs={{0,1},{1,0},{2,3},{3,2},{4,5},{5,4},{6,7},{7,6},{8,9},{9,8},{10,11... | collective-permute-start | bytes 1572872 | tf_op jit(solution)/shard_map/ppermute | solution.py:243
  65.3 5.9 %copy-start.2 = (bf16[128,4096]{1,0:T(8,128)(2,1)S(1)}, bf16[128,4096]{1,0:T(8,128)(2,1)}, u32[]{:S(2)}) copy-start(bf16[128,4096]{1,0:T(8,128)(2,1)} %w.5) | copy-start | bytes 3145732
  65.4 7.6 %collective-permute-start.1 = (bf16[8,256,128]{2,1,0:T(8,128)(2,1)}, bf16[8,256,128]{2,1,0:T(8,128)(2,1)S(1)}, u32[]{:S(2)}, u32[]{:S(2)}) collective-permute-start(bf16[8,256,128]{2,1,0:T(8,128)(2,1)} %collective-permute-done.t2), channel_id=1, source_target_pairs={{0,1},{1,0},{2,3},{3,2},{4,5},{5,4},{6,7},{7,6},{8,9},{9,8},{10,11... | collective-permute-start | bytes 1572872 | tf_op jit(solution)/shard_map/ppermute | solution.py:243
  72.9 13.5 %copy-start.4 = (f32[128,128]{1,0:T(8,128)S(1)}, f32[128,128]{1,0:T(8,128)}, u32[]{:S(2)}) copy-start(f32[128,128]{1,0:T(8,128)} %taps.7) | copy-start | bytes 196612
  75.1 14.1 %collective-permute-start.3 = (bf16[128,128]{1,0:T(8,128)(2,1)S(1)}, bf16[128,128]{1,0:T(8,128)(2,1)S(1)}, u32[]{:S(2)}, u32[]{:S(2)}) collective-permute-start(bf16[128,128]{1,0:T(8,128)(2,1)S(1)} %get-tuple-element.24), channel_id=1, source_target_pairs={{0,32},{32,64},{64,96},{96,128},{128,160},{160,192},{192,224},{224... | collective-permute-start | bytes 98312 | tf_op jit(solution)/shard_map/ppermute | solution.py:234
  81.8 11.8 %collective-permute-start.16 = (bf16[128,128]{1,0:T(8,128)(2,1)S(1)}, bf16[128,128]{1,0:T(8,128)(2,1)S(1)}, u32[]{:S(2)}, u32[]{:S(2)}) collective-permute-start(bf16[128,128]{1,0:T(8,128)(2,1)S(1)} %get-tuple-element.39), channel_id=1, source_target_pairs={{32,0},{64,32},{96,64},{128,96},{160,128},{192,160},{224,192},{256... | collective-permute-start | bytes 98312 | tf_op jit(solution)/shard_map/ppermute | solution.py:234
  95.2 3.3 %collective-permute-start.17 = (bf16[256,384]{1,0:T(8,128)(2,1)S(1)}, bf16[256,384]{1,0:T(8,128)(2,1)S(1)}, u32[]{:S(2)}, u32[]{:S(2)}) collective-permute-start(bf16[256,384]{1,0:T(8,128)(2,1)S(1)} %shard_map.87.refs_1_), channel_id=1, source_target_pairs={{0,1},{1,0},{2,3},{3,2},{4,5},{5,4},{6,7},{7,6},{8,9},{9,8},{10,11... | collective-permute-start | bytes 589832 | tf_op jit(solution)/shard_map/ppermute | solution.py:243
  98.1 5.8 %copy-start.6 = (bf16[16,128,128]{2,1,0:T(8,128)(2,1)S(1)}, bf16[16,128,128]{2,1,0:T(8,128)(2,1)}, u32[]{:S(2)}) copy-start(bf16[16,128,128]{2,1,0:T(8,128)(2,1)} %copy-done.5) | copy-start | bytes 1572868
  100.5 15.9 %collective-permute-start.19 = (bf16[8,256,128]{2,1,0:T(8,128)(2,1)S(1)}, bf16[8,256,128]{2,1,0:T(8,128)(2,1)S(1)}, u32[]{:S(2)}, u32[]{:S(2)}) collective-permute-start(bf16[8,256,128]{2,1,0:T(8,128)(2,1)S(1)} %shard_map.90), channel_id=1, source_target_pairs={{0,16},{16,0},{1,17},{17,1},{2,18},{18,2},{3,19},{19,3},{4,20},{20... | collective-permute-start | bytes 1572872 | tf_op jit(solution)/shard_map/ppermute | solution.py:243
  103.9 18.3 %collective-permute-start.5 = (bf16[16,128,128]{2,1,0:T(8,128)(2,1)S(1)}, bf16[16,128,128]{2,1,0:T(8,128)(2,1)S(1)}, u32[]{:S(2)}, u32[]{:S(2)}) collective-permute-start(bf16[16,128,128]{2,1,0:T(8,128)(2,1)S(1)} %copy-done.6), channel_id=1, source_target_pairs={{0,1},{1,0},{2,3},{3,2},{4,5},{5,4},{6,7},{7,6},{8,9},{9,8},{10,11... | collective-permute-start | bytes 1572872 | tf_op jit(solution)/shard_map/ppermute | solution.py:243
  105.9 16.4 %copy-start.3 = (bf16[128,4096]{1,0:T(8,128)(2,1)S(1)}, bf16[128,4096]{1,0:T(8,128)(2,1)}, u32[]{:S(2)}) copy-start(bf16[128,4096]{1,0:T(8,128)(2,1)} %w.5) | copy-start | bytes 3145732
  105.9 16.4 %collective-permute-start.4 = (bf16[256,128]{1,0:T(8,128)(2,1)S(1)}, bf16[256,128]{1,0:T(8,128)(2,1)S(1)}, u32[]{:S(2)}, u32[]{:S(2)}) collective-permute-start(bf16[256,128]{1,0:T(8,128)(2,1)S(1)} %get-tuple-element.27.mine), channel_id=1, source_target_pairs={{0,1},{1,0},{2,3},{3,2},{4,5},{5,4},{6,7},{7,6},{8,9},{9,8},{10,11... | collective-permute-start | bytes 196616 | tf_op jit(solution)/shard_map/ppermute | solution.py:243
  117.4 56.4 %all-to-all-start.2 = ((bf16[8,256,128]{2,1,0:T(8,128)(2,1)}), bf16[8,256,128]{2,1,0:T(8,128)(2,1)S(1)}, u32[]{:S(2)}, u32[]{:S(2)}) async-start(bf16[8,256,128]{2,1,0:T(8,128)(2,1)} %add_convert_fusion), calls=%async_computation.2 | async-start | bytes 1048576 | tf_op jit(solution)/shard_map/all_to_all | solution.py:247
  123.3 14.8 %collective-permute-start.6 = (bf16[8,256,128]{2,1,0:T(8,128)(2,1)S(1)}, bf16[8,256,128]{2,1,0:T(8,128)(2,1)S(1)}, u32[]{:S(2)}, u32[]{:S(2)}) collective-permute-start(bf16[8,256,128]{2,1,0:T(8,128)(2,1)S(1)} %get-tuple-element.30), channel_id=1, source_target_pairs={{0,16},{16,0},{1,17},{17,1},{2,18},{18,2},{3,19},{19,3},{4,20},{20... | collective-permute-start | bytes 1572872 | tf_op jit(solution)/shard_map/ppermute | solution.py:243
  138.8 20.2 %collective-permute-start.10 = (bf16[256,128]{1,0:T(8,128)(2,1)S(1)}, bf16[256,128]{1,0:T(8,128)(2,1)S(1)}, u32[]{:S(2)}, u32[]{:S(2)}) collective-permute-start(bf16[256,128]{1,0:T(8,128)(2,1)S(1)} %get-tuple-element.35), channel_id=1, source_target_pairs={{0,4},{2,6},{4,8},{6,10},{8,12},{10,14},{12,0},{14,2},{1,5},{3,7},... | collective-permute-start | bytes 196616 | tf_op jit(solution)/shard_map/ppermute | solution.py:254
  143.1 19.5 %collective-permute-start.11 = (bf16[256,128]{1,0:T(8,128)(2,1)S(1)}, bf16[256,128]{1,0:T(8,128)(2,1)S(1)}, u32[]{:S(2)}, u32[]{:S(2)}) collective-permute-start(bf16[256,128]{1,0:T(8,128)(2,1)S(1)} %get-tuple-element.36), channel_id=1, source_target_pairs={{0,12},{2,14},{4,0},{6,2},{8,4},{10,6},{12,8},{14,10},{1,13},{3,15... | collective-permute-start | bytes 196616 | tf_op jit(solution)/shard_map/ppermute | solution.py:254
  146.7 21.2 %collective-permute-start.12 = (bf16[256,128]{1,0:T(8,128)(2,1)S(1)}, bf16[256,128]{1,0:T(8,128)(2,1)S(1)}, u32[]{:S(2)}, u32[]{:S(2)}) collective-permute-start(bf16[256,128]{1,0:T(8,128)(2,1)S(1)} %get-tuple-element.37), channel_id=1, source_target_pairs={{0,2},{2,4},{4,6},{6,8},{8,10},{10,12},{12,14},{14,0},{1,3},{3,5},... | collective-permute-start | bytes 196616 | tf_op jit(solution)/shard_map/ppermute | solution.py:254
  149.6 18.3 %collective-permute-start.13 = (bf16[256,128]{1,0:T(8,128)(2,1)S(1)}, bf16[256,128]{1,0:T(8,128)(2,1)S(1)}, u32[]{:S(2)}, u32[]{:S(2)}) collective-permute-start(bf16[256,128]{1,0:T(8,128)(2,1)S(1)} %get-tuple-element.38), channel_id=1, source_target_pairs={{0,14},{2,0},{4,2},{6,4},{8,6},{10,8},{12,10},{14,12},{1,15},{3,1}... | collective-permute-start | bytes 196616 | tf_op jit(solution)/shard_map/ppermute | solution.py:254
  152.6 15.3 %collective-permute-start.7 = (bf16[256,128]{1,0:T(8,128)(2,1)S(1)}, bf16[256,128]{1,0:T(8,128)(2,1)S(1)}, u32[]{:S(2)}, u32[]{:S(2)}) collective-permute-start(bf16[256,128]{1,0:T(8,128)(2,1)S(1)} %get-tuple-element.32), channel_id=1, source_target_pairs={{0,8},{2,10},{4,12},{6,14},{8,0},{10,2},{12,4},{14,6},{1,9},{3,11}... | collective-permute-start | bytes 196616 | tf_op jit(solution)/shard_map/ppermute | solution.py:254
  159.0 9.3 %collective-permute-start.8 = (bf16[256,128]{1,0:T(8,128)(2,1)S(1)}, bf16[256,128]{1,0:T(8,128)(2,1)S(1)}, u32[]{:S(2)}, u32[]{:S(2)}) collective-permute-start(bf16[256,128]{1,0:T(8,128)(2,1)S(1)} %get-tuple-element.33), channel_id=1, source_target_pairs={{0,6},{2,8},{4,10},{6,12},{8,14},{10,0},{12,2},{14,4},{1,7},{3,9},... | collective-permute-start | bytes 196616 | tf_op jit(solution)/shard_map/ppermute | solution.py:254
  162.5 10.6 %collective-permute-start.9 = (bf16[256,128]{1,0:T(8,128)(2,1)S(1)}, bf16[256,128]{1,0:T(8,128)(2,1)S(1)}, u32[]{:S(2)}, u32[]{:S(2)}) collective-permute-start(bf16[256,128]{1,0:T(8,128)(2,1)S(1)} %get-tuple-element.34), channel_id=1, source_target_pairs={{0,10},{2,12},{4,14},{6,0},{8,2},{10,4},{12,6},{14,8},{1,11},{3,13... | collective-permute-start | bytes 196616 | tf_op jit(solution)/shard_map/ppermute | solution.py:254

commit v5 on v0

v5 whole, which is shorter than its diff:
```python
import jax
import jax.numpy as jnp
from jax import lax
from jax.experimental import pallas as pl
from jax.experimental.pallas import tpu as pltpu
from jax.sharding import Mesh
from jax.sharding import PartitionSpec as P

X, Y, CORE = 2, 8, 2
SWAP = [(0, 1), (1, 0)]
LANES = 128
STRIP = 64
INTERPRET = False
BF, F32 = jnp.bfloat16, jnp.float32


def f32(a):
    return a.astype(F32)


def call(kernel, outs, scratch, flops, nbytes, *args):
    return pl.pallas_call(
        kernel,
        out_shape=[jax.ShapeDtypeStruct(s, d) for s, d in outs],
        in_specs=[pl.BlockSpec(memory_space=pltpu.SMEM)]
        + [pl.BlockSpec(memory_space=pltpu.VMEM)] * (len(args) - 1),
        out_specs=[pl.BlockSpec(memory_space=pltpu.VMEM)] * len(outs),
        scratch_shapes=scratch,
        cost_estimate=pl.CostEstimate(flops=flops, bytes_accessed=nbytes, transcendentals=0),
        compiler_params=pltpu.CompilerParams(vmem_limit_bytes=48 << 20),
        interpret=INTERPRET,
    )(*args)


def x_side(pos, far):
    return 1 - pos[0] if far else pos[0]


def core_side(pos, other):
    return 1 - pos[1] if other else pos[1]


def lanes(at):
    return pl.ds(pl.multiple_of(at * LANES, LANES), LANES)


def lay_out(pos, part, first, whole, start):
    rows = whole.shape[0]
    for j in range(Y):
        for other in range(2):
            at = first + other * rows
            to = start + j * CORE + core_side(pos, other)
            whole[:, lanes(to)] = part[j, at : at + rows]


def turn(pos, own, other, turned):
    span = turned.shape[3]
    for b in range(3):
        for o, w in enumerate((own, other)):
            for n in range(turned.shape[1]):
                turned[2 * b + o, n] = w[b, n * span : (n + 1) * span, :].T


def project_side(pos, far, part, own, other, whole):
    lay_out(pos, part, 0, whole, 0)
    depth = whole.shape[1]
    rows = pl.ds(pl.multiple_of(x_side(pos, far) * depth, depth), depth)
    rhs = jnp.concatenate([w[b, rows, :] for b in range(3) for w in (own, other)], axis=1)
    return jnp.dot(whole[...], rhs, preferred_element_type=F32)


def project_near(pos, part, own, other, near, whole):
    near[...] = project_side(pos, 0, part, own, other, whole)


def put(pos, value, out):
    for o in range(2):
        out[:, lanes(core_side(pos, o))] = value[:, o * LANES : (o + 1) * LANES]


def project(pos, part, near, own, other, q, k, v, mix, tail, whole):
    proj = (near[...] + project_side(pos, 1, part, own, other, whole)).astype(BF)
    wide = q.shape[1]
    key, value = proj[:, wide : 2 * wide], proj[:, 2 * wide :]
    q[...] = proj[:, :wide]
    k[...] = key
    v[...] = value
    product = (f32(key) * f32(value)).astype(BF)
    mix[...] = product
    put(pos, product, tail)


def shift_all(ext, shifted, back):
    total = ext.shape[0]
    for b in range(8):
        by = (total - b) % total if back else b
        shifted[b] = pltpu.roll(ext, by, 0) if by else ext


def strip_sum(at, zero, first, last, limit, taps, shifted, back):
    lim = limit[at : at + STRIP, :]

    def eight(a, acc):
        start = pl.multiple_of(zero + 8 * a if back else zero - 8 * a, 8)
        for b in range(8):
            s = 8 * a + b
            piece = shifted[b, pl.ds(start, STRIP), :]
            acc = acc + jnp.where(lim >= s, piece, 0.0) * taps[pl.ds(s, 1), :]
        return acc

    return lax.fori_loop(first, last, eight, jnp.zeros((STRIP, LANES), F32))


def filtered_near(pos, mix, reach, taps, taps_other, near, shifted):
    n_taps = taps.shape[0]
    for o, t in enumerate((taps, taps_other)):
        cols = slice(o * LANES, (o + 1) * LANES)
        shift_all(
            jnp.concatenate([jnp.zeros((n_taps, LANES), F32), f32(mix[:, cols])], axis=0),
            shifted, False,
        )
        for at in range(0, mix.shape[0], STRIP):
            last = min(n_taps, at + STRIP) // 8
            near[at : at + STRIP, cols] = strip_sum(
                at, n_taps + at, 0, last, reach, t, shifted, False
            )


def filtered(pos, prior, near, q, reach, taps, taps_other, conv, gated, shifted):
    n_taps = taps.shape[0]
    for o, t in enumerate((taps, taps_other)):
        cols = slice(o * LANES, (o + 1) * LANES)
        shift_all(
            jnp.concatenate(
                [f32(prior[:, lanes(core_side(pos, o))]), jnp.zeros((n_taps, LANES), F32)], axis=0
            ),
            shifted, False,
        )
        for at in range(0, conv.shape[0], STRIP):
            here = slice(at, at + STRIP)
            total = near[here, cols]
            if at < n_taps:
                total += strip_sum(
                    at, n_taps + at, at // 8, n_taps // 8, reach, t, shifted, False
                )
            conv[here, cols] = total
            gated[here, cols] = (f32(q[here, cols]) * total).astype(BF)


def out_terms(pos, gated, own, other, terms):
    span = terms.shape[2]
    for n in range(terms.shape[0]):
        cols = slice(n * span, (n + 1) * span)
        rhs = jnp.concatenate([own[:, cols], other[:, cols]], axis=0)
        terms[n] = jnp.dot(gated[...], rhs, preferred_element_type=F32).astype(BF)


def back_gate(pos, part, own, other, q, dgated, dconv, head, whole):
    rows = whole.shape[0]
    for far in range(2):
        lay_out(pos, part, 2 * far * rows, whole, x_side(pos, far) * (Y * CORE))
    total = lax.dot_general(
        whole[...],
        jnp.concatenate([own[...], other[...]], axis=0),
        (((1,), (1,)), ((), ())),
        preferred_element_type=F32,
    )
    dgated[...] = total
    d = (total * f32(q[...])).astype(BF)
    dconv[...] = d
    put(pos, d, head)


def back_near(pos, dconv, rem, taps, taps_other, near, shifted):
    n_taps, rows = taps.shape[0], dconv.shape[0]
    for o, t in enumerate((taps, taps_other)):
        cols = slice(o * LANES, (o + 1) * LANES)
        shift_all(
            jnp.concatenate([f32(dconv[:, cols]), jnp.zeros((n_taps, LANES), F32)], axis=0),
            shifted, True,
        )
        for at in range(0, rows, STRIP):
            last = min(n_taps, rows - at) // 8
            near[at : at + STRIP, cols] = strip_sum(at, at, 0, last, rem, t, shifted, True)


def back_filtered(pos, after, near, k, v, dgated, conv, rem, taps, taps_other, dproj, shifted):
    n_taps, (rows, wide) = taps.shape[0], near.shape
    for o, t in enumerate((taps, taps_other)):
        cols = slice(o * LANES, (o + 1) * LANES)
        shift_all(
            jnp.concatenate(
                [jnp.zeros((rows, LANES), F32), f32(after[:, lanes(core_side(pos, o))])], axis=0
            ),
            shifted, True,
        )
        for at in range(0, rows, STRIP):
            here = slice(at, at + STRIP)
            dmix = near[here, cols]
            left = rows - at - STRIP
            if left < n_taps:
                dmix += strip_sum(at, at, left // 8, n_taps // 8, rem, t, shifted, True)
            for b, d in enumerate(
                (dgated[here, cols] * conv[here, cols], dmix * f32(v[here, cols]), dmix * f32(k[here, cols]))
            ):
                at_col = b * wide + o * LANES
                dproj[here, at_col : at_col + LANES] = d.astype(BF)


def grad_terms(pos, dproj, turned, terms, far):
    for j in range(Y):
        n = x_side(pos, far) * Y + j
        rhs = jnp.concatenate([turned[i, n] for i in range(6)], axis=0)
        terms[j] = jnp.dot(dproj[...], rhs, preferred_element_type=F32).astype(BF)


def grad_far(*refs):
    grad_terms(*refs, 1)


def grad_near(*refs):
    grad_terms(*refs, 0)


def add_up(pos, arrived, keep, give):
    total = f32(arrived[0])
    for n in range(1, arrived.shape[0]):
        total += f32(arrived[n])
    total = total.astype(BF)
    for core in range(2):
        part = total[:, core * LANES : (core + 1) * LANES]

        @pl.when(pos[1] == core)
        def _():
            keep[...] = part

        @pl.when(pos[1] != core)
        def _():
            give[...] = part


def join(pos, keep, got, out):
    rows = keep.shape[0]
    for other, part in enumerate((keep, got)):
        out[pl.ds(pl.multiple_of(core_side(pos, other) * rows, rows), rows), :] = part[...]


def passed_along(block, distance):
    devices = range(lax.axis_size("ctx") * CORE)
    route = [(i - distance, i) for i in devices if i - distance in devices]
    return lax.ppermute(block, ("ctx", "core"), route)


def spread_y(block):
    copies = jnp.broadcast_to(block[None], (Y,) + block.shape)
    return lax.all_to_all(copies, "y", split_axis=0, concat_axis=0, tiled=True)


def swapped(block, axis):
    return lax.ppermute(block, axis, SWAP)


def summed(terms, axes, pos, rows):
    arrived = lax.all_to_all(terms, axes, split_axis=0, concat_axis=0, tiled=True)
    size = terms.size
    keep, give = call(add_up, [((rows // CORE, LANES), BF)] * 2, [], size, 2 * size, pos, arrived)
    got = swapped(give, "core")
    (out,) = call(join, [((rows, LANES), BF)], [], 0, 4 * rows * LANES, pos, keep, got)
    return out


def block_step(tokens, cotangent, in_weight, filter_taps, out_weight, segment_ids):
    width, _, chans = in_weight.shape
    rows, taps = tokens.shape[0], filter_taps.shape[0]
    part, wide, n_chips = rows // CORE, CORE * chans, X * Y
    block, triple, narrow = (part, wide), (part, 3 * wide), (part, chans)
    whole = [pltpu.VMEM((part, width), BF)]
    half = [pltpu.VMEM((part, width // 2), BF)]
    shifted = [pltpu.VMEM((8, part + taps, LANES), F32)]
    macs = rows * width * chans
    small = rows * width * 2

    core = lax.axis_index("core")
    pos = jnp.stack([lax.axis_index("x"), core]).astype(jnp.int32)
    w3 = in_weight.transpose(1, 0, 2)

    def rows_of(a, which):
        return lax.dynamic_slice_in_dim(a, which * part, part, 0)

    sent = jnp.concatenate([rows_of(tokens, 1 - core), rows_of(cotangent, 1 - core)])
    got = swapped(sent, "core")
    tok = jnp.concatenate([rows_of(tokens, core), got[:part]])
    cot = jnp.concatenate([rows_of(cotangent, core), got[part:]])
    t0 = spread_y(tok)
    far_cot = swapped(cot, "x")
    w_other = swapped(w3, "core")
    ow_other = swapped(out_weight, "core")
    taps_other = swapped(filter_taps, "core")
    both_taps = (filter_taps, taps_other)
    base = lax.axis_index("ctx") * rows + core * part
    positions = base + jnp.arange(part, dtype=jnp.int32)
    seg_here = lax.dynamic_slice_in_dim(segment_ids, base, part)
    first = jnp.sum((segment_ids[None, :] < seg_here[:, None]).astype(jnp.int32), axis=1)
    end = jnp.sum((segment_ids[None, :] <= seg_here[:, None]).astype(jnp.int32), axis=1)
    reach = jnp.broadcast_to((positions - first)[:, None], narrow)
    rem = jnp.broadcast_to((end - 1 - positions)[:, None], narrow)
    t2 = swapped(t0, "x")
    c0 = spread_y(jnp.concatenate([cot, far_cot]))

    (turned,) = call(turn, [((6, n_chips, chans, wide), BF)], [], macs, 8 * small, pos, w3, w_other)
    (near,) = call(
        project_near, [(triple, F32)], half, 3 * macs, 2 * small,
        pos, t0, w3, w_other,
    )
    q, k, v, mix, tail = call(
        project, [(block, BF)] * 5, half, 3 * macs, 2 * small,
        pos, t2, near, w3, w_other,
    )
    prior = passed_along(tail, 1)
    (near,) = call(
        filtered_near, [(block, F32)], shifted, macs, small,
        pos, mix, reach, *both_taps,
    )
    conv, gated = call(
        filtered, [(block, F32), (block, BF)], shifted, macs, small // 2,
        pos, prior, near, q, reach, *both_taps,
    )
    (terms,) = call(
        out_terms, [((n_chips, part, wide), BF)], [], 2 * macs, 2 * small,
        pos, gated, out_weight, ow_other,
    )
    block_out = summed(terms, ("x", "y"), pos, rows)
    dgated, dconv, head = call(
        back_gate, [(block, F32), (block, BF), (block, BF)], whole, 2 * macs, small,
        pos, c0, out_weight, ow_other, q,
    )
    after = passed_along(head, -1)
    (near,) = call(back_near, [(block, F32)], shifted, macs, small, pos, dconv, rem, *both_taps)
    (dproj,) = call(
        back_filtered, [(triple, BF)], shifted, macs, small // 2,
        pos, after, near, k, v, dgated, conv, rem, *both_taps,
    )
    sides = [((Y, part, wide), BF)]
    (far,) = call(grad_far, sides, [], 3 * macs, 2 * small, pos, dproj, turned)
    got = swapped(far, "x")
    (near,) = call(grad_near, sides, [], 3 * macs, 2 * small, pos, dproj, turned)
    return block_out, summed((f32(near) + f32(got)).astype(BF), "y", pos, rows)


def solution(mesh):
    fine = Mesh(
        mesh.devices.reshape(mesh.shape["ctx"], X, Y, CORE), ("ctx", "x", "y", "core")
    )
    tp = ("x", "y", "core")
    placed = (P("ctx", tp), P("ctx", tp), P(None, None, tp), P(None, tp), P(tp, None), P())
    return jax.shard_map(
        block_step,
        mesh=fine,
        in_specs=placed,
        out_specs=(P("ctx", tp), P("ctx", tp)),
        check_vma=False,
    )
```

time: 253 us -> 180 us (0.71)
  the two profiles are of different devices: /device:TPU:12 before, /device:TPU:1 now
where the time goes in v5:
time: 180 us; the launch traced here: 179 us
  waiting for transfers between devices  80.1 us (44%)
  starting transfers between devices  52.3 us (29%)
  Pallas kernels  38.3 us (21%)
  local copies, waits for them, and re-layouts  4.9 us (3%)
  other arithmetic  1.81 us (1%)
    pallas_call x15, Pallas kernels, call(): pl.pallas_call(kernel, out_shape=[jax.ShapeDtypeStruct(s, d) for s, d in...  38.3 us
    all_to_all x2, waiting for transfers between devices, summed(): lax.all_to_all(terms, axes, split_axis=0, concat_axis=0, tiled=True)  37 us
    ppermute x9, starting transfers between devices, swapped(): return lax.ppermute(block, axis, SWAP)  31.8 us
    ppermute x9, waiting for transfers between devices, swapped(): return lax.ppermute(block, axis, SWAP)  26.2 us
    all_to_all x2, waiting for transfers between devices, spread_y(): return lax.all_to_all(copies, 'y', split_axis=0, concat_axis=0, tiled=True)  16.9 us
    all_to_all x2, starting transfers between devices, spread_y(): return lax.all_to_all(copies, 'y', split_axis=0, concat_axis=0, tiled=True)  8.41 us
    all_to_all x2, starting transfers between devices, summed(): lax.all_to_all(terms, axes, split_axis=0, concat_axis=0, tiled=True)  7.8 us
    ppermute x2, starting transfers between devices, passed_along(): return lax.ppermute(block, ('ctx', 'core'), route)  4.31 us
  transfers between devices with their start and end apart: 15, of which 8 were waited for; matrix products, arithmetic and copies ran while one was open for 2% of the time, Pallas kernels for 17%

profile of v5, /device:TPU:1, one launch (start us, length us, event | category | flops | bytes accessed | tf_op | source)
XLA Modules:
  0.0 178.5 jit_solution(6585388347944339103)
XLA Ops:
  0.7 12.6 %collective-permute-start.2 = (bf16[3,4096,128]{2,1,0:T(8,128)(2,1)}, bf16[3,4096,128]{2,1,0:T(8,128)(2,1)}, u32[]{:S(2)}, u32[]{:S(2)}) collective-permute-start(bf16[3,4096,128]{2,1,0:T(8,128)(2,1)} %bitcast.3), channel_id=1, source_target_pairs={{0,1},{1,0},{2,3},{3,2},{4,5},{5,4},{6,7},{7,6},{8,9},{9,8},{10,11... | collective-permute-start | bytes 9437192 | tf_op jit(solution)/shard_map/ppermute | solution.py:260
  14.2 1.9 %collective-permute-start = (bf16[256,128]{1,0:T(8,128)(2,1)S(1)}, bf16[256,128]{1,0:T(8,128)(2,1)S(1)}, u32[]{:S(2)}, u32[]{:S(2)}) collective-permute-start(bf16[256,128]{1,0:T(8,128)(2,1)S(1)} %pad_maximum_fusion.1), channel_id=1, source_target_pairs={{0,1},{1,0},{2,3},{3,2},{4,5},{5,4},{6,7},{7,6},{8,9},{9,8},{10,11... | collective-permute-start | bytes 196616 | tf_op jit(solution)/shard_map/ppermute | solution.py:260
  16.1 2.8 %collective-permute-done = bf16[256,128]{1,0:T(8,128)(2,1)S(1)} collective-permute-done((bf16[256,128]{1,0:T(8,128)(2,1)S(1)}, bf16[256,128]{1,0:T(8,128)(2,1)S(1)}, u32[]{:S(2)}, u32[]{:S(2)}) %collective-permute-start) | collective-permute-done | bytes 65568 | tf_op jit(solution)/shard_map/ppermute | solution.py:260
  19.8 4.2 %all-to-all-start = ((bf16[8,256,128]{2,1,0:T(8,128)(2,1)}), bf16[8,256,128]{2,1,0:T(8,128)(2,1)}, u32[]{:S(2)}, u32[]{:S(2)}) async-start(bf16[8,256,128]{2,1,0:T(8,128)(2,1)} %broadcast_in_dim.8), calls=%async_computation | async-start | bytes 1048576 | tf_op jit(solution)/shard_map/all_to_all | solution.py:256
  24.0 1.9 %collective-permute-start.7 = (bf16[256,128]{1,0:T(8,128)(2,1)S(1)}, bf16[256,128]{1,0:T(8,128)(2,1)S(1)}, u32[]{:S(2)}, u32[]{:S(2)}) collective-permute-start(bf16[256,128]{1,0:T(8,128)(2,1)S(1)} %pad_maximum_fusion.3), channel_id=1, source_target_pairs={{0,16},{16,0},{1,17},{17,1},{2,18},{18,2},{3,19},{19,3},{4,20},{20... | collective-permute-start | bytes 196616 | tf_op jit(solution)/shard_map/ppermute | solution.py:260
  25.9 3.5 %collective-permute-done.7 = bf16[256,128]{1,0:T(8,128)(2,1)S(1)} collective-permute-done((bf16[256,128]{1,0:T(8,128)(2,1)S(1)}, bf16[256,128]{1,0:T(8,128)(2,1)S(1)}, u32[]{:S(2)}, u32[]{:S(2)}) %collective-permute-start.7) | collective-permute-done | bytes 65568 | tf_op jit(solution)/shard_map/ppermute | solution.py:260
  29.4 12.5 %all-to-all-done.part = bf16[8,256,128]{2,1,0:T(8,128)(2,1)} async-done(((bf16[8,256,128]{2,1,0:T(8,128)(2,1)}), bf16[8,256,128]{2,1,0:T(8,128)(2,1)}, u32[]{:S(2)}, u32[]{:S(2)}) %all-to-all-start) | async-done | bytes 524320 | tf_op jit(solution)/shard_map/all_to_all | solution.py:256
  43.0 4.3 %all-to-all-start.2 = ((bf16[8,512,128]{2,1,0:T(8,128)(2,1)}), bf16[8,512,128]{2,1,0:T(8,128)(2,1)}, u32[]{:S(2)}, u32[]{:S(2)}) async-start(bf16[8,512,128]{2,1,0:T(8,128)(2,1)} %broadcast_in_dim.10), calls=%async_computation.2 | async-start | bytes 2097152 | tf_op jit(solution)/shard_map/all_to_all | solution.py:256
  47.3 2.4 %collective-permute-start.5 = (bf16[128,4096]{1,0:T(8,128)(2,1)}, bf16[128,4096]{1,0:T(8,128)(2,1)}, u32[]{:S(2)}, u32[]{:S(2)}) collective-permute-start(bf16[128,4096]{1,0:T(8,128)(2,1)} %own.3), channel_id=1, source_target_pairs={{0,1},{1,0},{2,3},{3,2},{4,5},{5,4},{6,7},{7,6},{8,9},{9,8},{10,11... | collective-permute-start | bytes 3145736 | tf_op jit(solution)/shard_map/ppermute | solution.py:260
  49.7 1.9 %collective-permute-start.4 = (f32[128,128]{1,0:T(8,128)S(1)}, f32[128,128]{1,0:T(8,128)S(1)}, u32[]{:S(2)}, u32[]{:S(2)}) collective-permute-start(f32[128,128]{1,0:T(8,128)S(1)} %copy-done.3), channel_id=1, source_target_pairs={{0,1},{1,0},{2,3},{3,2},{4,5},{5,4},{6,7},{7,6},{8,9},{9,8},{10,11... | collective-permute-start | bytes 196616 | tf_op jit(solution)/shard_map/ppermute | solution.py:260
  54.6 2.8 %shard_map.77.near = f32[128,768]{1,0:T(8,128)S(1)} custom-call(s32[2]{0:T(128)S(1)} %pad_add_fusion.pos.refs_0_, bf16[8,256,128]{2,1,0:T(8,128)(2,1)} %all-to-all-done.part, bf16[3,4096,128]{2,1,0:T(8,128)(2,1)S(1)} %bitcast.4, bf16[3,4096,128]{2,1,0:T(8,128)(2,1)} %collective-permute-done.2.other), custom_call_target="tpu_custom_call" | custom-call | flops 402653184 | bytes 4194304 | tf_op jit(solution)/shard_map/pallas_call | solution.py:22
  57.3 9.6 %collective-permute-done.1.part = bf16[8,256,128]{2,1,0:T(8,128)(2,1)S(1)} collective-permute-done((bf16[8,256,128]{2,1,0:T(8,128)(2,1)}, bf16[8,256,128]{2,1,0:T(8,128)(2,1)S(1)}, u32[]{:S(2)}, u32[]{:S(2)}) %collective-permute-start.1) | collective-permute-done | bytes 524320 | tf_op jit(solution)/shard_map/ppermute | solution.py:260
  67.0 2.6 %shard_map.78 = (bf16[128,256]{1,0:T(8,128)(2,1)S(1)}, bf16[128,256]{1,0:T(8,128)(2,1)S(1)}, bf16[128,256]{1,0:T(8,128)(2,1)S(1)}, bf16[128,256]{1,0:T(8,128)(2,1)S(1)}, bf16[128,256]{1,0:T(8,128)(2,1)S(1)}) custom-call(s32[2]{0:T(128)S(1)} %pad_add_fusion.pos.refs_0_, bf16[8,256,128]{2,1,0:T(8,128)(2,1)S(1)} %collective-permute-done.1.part, ...), custom_call_target="tpu_custom_call" | custom-call | flops 402653184 | bytes 4194304 | tf_op jit(solution)/shard_map/pallas_call | solution.py:22
  72.1 4.4 %all-to-all-done.2.part = bf16[8,512,128]{2,1,0:T(8,128)(2,1)} async-done(((bf16[8,512,128]{2,1,0:T(8,128)(2,1)}), bf16[8,512,128]{2,1,0:T(8,128)(2,1)}, u32[]{:S(2)}, u32[]{:S(2)}) %all-to-all-start.2) | async-done | bytes 1048608 | tf_op jit(solution)/shard_map/all_to_all | solution.py:256
  77.8 2.6 %shard_map.84 = (f32[128,256]{1,0:T(8,128)S(1)}, bf16[128,256]{1,0:T(8,128)(2,1)S(1)}, bf16[128,256]{1,0:T(8,128)(2,1)S(1)}) custom-call(s32[2]{0:T(128)S(1)} %pad_add_fusion.pos.refs_0_, bf16[8,512,128]{2,1,0:T(8,128)(2,1)} %all-to-all-done.2.part, bf16[128,4096]{1,0:T(8,128)(2,1)S(1)} %copy-done.1, bf16[128,4096]{1,0:T(8,128)(2,1)} %collective-permute-done.5.other, ...), custom_call_target="tpu_custom_call" | custom-call | flops 268435456 | bytes 2097152 | tf_op jit(solution)/shard_map/pallas_call | solution.py:22
  80.4 2.4 %collective-permute-start.8 = (bf16[128,256]{1,0:T(8,128)(2,1)S(1)}, bf16[128,256]{1,0:T(8,128)(2,1)S(1)}, u32[]{:S(2)}, u32[]{:S(2)}) collective-permute-start(bf16[128,256]{1,0:T(8,128)(2,1)S(1)} %get-tuple-element.22), channel_id=1, source_target_pairs={{1,0},{32,1},{33,32},{64,33},{65,64},{96,65},{97,96},{128,97},{129... | collective-permute-start | bytes 196616 | tf_op jit(solution)/shard_map/ppermute | solution.py:251
  82.8 6.2 %shard_map.87.refs_2_ = bf16[6,16,128,256]{3,2,1,0:T(8,128)(2,1)} custom-call(s32[2]{0:T(128)S(1)} %pad_add_fusion.pos.refs_0_, bf16[3,4096,128]{2,1,0:T(8,128)(2,1)S(1)} %bitcast.6, bf16[3,4096,128]{2,1,0:T(8,128)(2,1)} %collective-permute-done.2.other), custom_call_target="tpu_custom_call" | custom-call | flops 134217728 | bytes 16777216 | tf_op jit(solution)/shard_map/pallas_call | solution.py:22
  89.1 2.5 %shard_map.79.near = f32[128,256]{1,0:T(8,128)S(1)} custom-call(s32[2]{0:T(128)S(1)} %pad_add_fusion.pos.refs_0_, bf16[128,256]{1,0:T(8,128)(2,1)S(1)} %copy-done.5, s32[128,128]{1,0:T(8,128)S(1)} %broadcast_in_dim.9.reach, f32[128,128]{1,0:T(8,128)S(1)} %copy-done.3, f32[128,128]{1,0:T(8,128)S(1)} %collective-permute-done.4.taps_other), custom_call_target="tpu_custom_call" | custom-call | flops 134217728 | bytes 2097152 | tf_op jit(solution)/shard_map/pallas_call | solution.py:22
  91.7 2.5 %shard_map.85.near = f32[128,256]{1,0:T(8,128)S(1)} custom-call(s32[2]{0:T(128)S(1)} %pad_add_fusion.pos.refs_0_, bf16[128,256]{1,0:T(8,128)(2,1)S(1)} %get-tuple-element.23.dconv, s32[128,128]{1,0:T(8,128)S(1)} %broadcast_in_dim.11.rem, f32[128,128]{1,0:T(8,128)S(1)} %copy-done.3, f32[128,128]{1,0:T(8,128)S(1)} %collective-permute-done.4.taps_other), custom_call_target="tpu_custom_call" | custom-call | flops 134217728 | bytes 2097152 | tf_op jit(solution)/shard_map/pallas_call | solution.py:22
  94.2 2.8 %shard_map.80 = (f32[128,256]{1,0:T(8,128)S(1)}, bf16[128,256]{1,0:T(8,128)(2,1)S(1)}) custom-call(s32[2]{0:T(128)S(1)} %pad_add_fusion.pos.refs_0_, bf16[128,256]{1,0:T(8,128)(2,1)} %collective-permute-done.3.prior, f32[128,256]{1,0:T(8,128)S(1)} %shard_map.79.near, bf16[128,256]{1,0:T(8,128)(2,1)S(1)} %get-tuple-element.18.q, ...), custom_call_target="tpu_custom_call" | custom-call | flops 134217728 | bytes 1048576 | tf_op jit(solution)/shard_map/pallas_call | solution.py:22
  97.1 2.6 %shard_map.86.refs_1_ = bf16[128,768]{1,0:T(8,128)(2,1)S(1)} custom-call(s32[2]{0:T(128)S(1)} %pad_add_fusion.pos.refs_0_, bf16[128,256]{1,0:T(8,128)(2,1)S(1)} %collective-permute-done.8.after, f32[128,256]{1,0:T(8,128)S(1)} %shard_map.85.near, bf16[128,256]{1,0:T(8,128)(2,1)S(1)} %get-tuple-element.24.k, bf16[128,256]{1,0:T(8,128)(2,1)S(1)} %get-tuple-element.25.v, ...), custom_call_target="tpu_custom_call" | custom-call | flops 134217728 | bytes 1048576 | tf_op jit(solution)/shard_map/pallas_call | solution.py:22
  99.7 3.4 %shard_map.89 = bf16[8,128,256]{2,1,0:T(8,128)(2,1)S(1)} custom-call(s32[2]{0:T(128)S(1)} %pad_add_fusion.pos.refs_0_, bf16[128,768]{1,0:T(8,128)(2,1)S(1)} %shard_map.86.refs_1_, bf16[6,16,128,256]{3,2,1,0:T(8,128)(2,1)} %shard_map.87.refs_2_), custom_call_target="tpu_custom_call" | custom-call | flops 402653184 | bytes 4194304 | tf_op jit(solution)/shard_map/pallas_call | solution.py:22
  103.1 2.1 %collective-permute-start.9 = (bf16[8,128,256]{2,1,0:T(8,128)(2,1)S(1)}, bf16[8,128,256]{2,1,0:T(8,128)(2,1)S(1)}, u32[]{:S(2)}, u32[]{:S(2)}) collective-permute-start(bf16[8,128,256]{2,1,0:T(8,128)(2,1)S(1)} %shard_map.89), channel_id=1, source_target_pairs={{0,16},{16,0},{1,17},{17,1},{2,18},{18,2},{3,19},{19,3},{4,20},{20... | collective-permute-start | bytes 1572872 | tf_op jit(solution)/shard_map/ppermute | solution.py:260
  105.1 3.4 %shard_map.88 = bf16[8,128,256]{2,1,0:T(8,128)(2,1)S(1)} custom-call(s32[2]{0:T(128)S(1)} %pad_add_fusion.pos.refs_0_, bf16[128,768]{1,0:T(8,128)(2,1)S(1)} %shard_map.86.refs_1_, bf16[6,16,128,256]{3,2,1,0:T(8,128)(2,1)} %shard_map.87.refs_2_), custom_call_target="tpu_custom_call" | custom-call | flops 402653184 | bytes 4194304 | tf_op jit(solution)/shard_map/pallas_call | solution.py:22
  108.5 10.2 %collective-permute-done.9 = bf16[8,128,256]{2,1,0:T(8,128)(2,1)S(1)} collective-permute-done((bf16[8,128,256]{2,1,0:T(8,128)(2,1)S(1)}, bf16[8,128,256]{2,1,0:T(8,128)(2,1)S(1)}, u32[]{:S(2)}, u32[]{:S(2)}) %collective-permute-start.9) | collective-permute-done | bytes 524320 | tf_op jit(solution)/shard_map/ppermute | solution.py:260
  119.6 4.1 %all-to-all-start.3 = ((bf16[8,128,256]{2,1,0:T(8,128)(2,1)}), bf16[8,128,256]{2,1,0:T(8,128)(2,1)}, u32[]{:S(2)}, u32[]{:S(2)}) async-start(bf16[8,128,256]{2,1,0:T(8,128)(2,1)} %add_convert_fusion), calls=%async_computation.3 | async-start | bytes 1048576 | tf_op jit(solution)/shard_map/all_to_all | solution.py:264
  123.8 2.7 %shard_map.81 = bf16[16,128,256]{2,1,0:T(8,128)(2,1)} custom-call(s32[2]{0:T(128)S(1)} %pad_add_fusion.pos.refs_0_, bf16[128,256]{1,0:T(8,128)(2,1)S(1)} %get-tuple-element.19.gated, bf16[128,4096]{1,0:T(8,128)(2,1)S(1)} %copy-done.2, bf16[128,4096]{1,0:T(8,128)(2,1)} %collective-permute-done.5.other), custom_call_target="tpu_custom_call" | custom-call | flops 268435456 | bytes 4194304 | tf_op jit(solution)/shard_map/pallas_call | solution.py:22
  126.5 15.3 %all-to-all-done.3.arrived = bf16[8,128,256]{2,1,0:T(8,128)(2,1)} async-done(((bf16[8,128,256]{2,1,0:T(8,128)(2,1)}), bf16[8,128,256]{2,1,0:T(8,128)(2,1)}, u32[]{:S(2)}, u32[]{:S(2)}) %all-to-all-start.3) | async-done | bytes 524320 | tf_op jit(solution)/shard_map/all_to_all | solution.py:264
  141.8 3.7 %all-to-all-start.1 = ((bf16[16,128,256]{2,1,0:T(8,128)(2,1)}), bf16[16,128,256]{2,1,0:T(8,128)(2,1)S(1)}, u32[]{:S(2)}, u32[]{:S(2)}) async-start(bf16[16,128,256]{2,1,0:T(8,128)(2,1)} %shard_map.81), calls=%async_computation.1 | async-start | bytes 2097152 | tf_op jit(solution)/shard_map/all_to_all | solution.py:264
  146.6 2.4 %collective-permute-start.10 = (bf16[128,128]{1,0:T(8,128)(2,1)S(1)}, bf16[128,128]{1,0:T(8,128)(2,1)S(1)}, u32[]{:S(2)}, u32[]{:S(2)}) collective-permute-start(bf16[128,128]{1,0:T(8,128)(2,1)S(1)} %get-tuple-element.29), channel_id=1, source_target_pairs={{0,1},{1,0},{2,3},{3,2},{4,5},{5,4},{6,7},{7,6},{8,9},{9,8},{10,11... | collective-permute-start | bytes 98312 | tf_op jit(solution)/shard_map/ppermute | solution.py:260
  149.0 21.8 %all-to-all-done.1.arrived = bf16[16,128,256]{2,1,0:T(8,128)(2,1)S(1)} async-done(((bf16[16,128,256]{2,1,0:T(8,128)(2,1)}), bf16[16,128,256]{2,1,0:T(8,128)(2,1)S(1)}, u32[]{:S(2)}, u32[]{:S(2)}) %all-to-all-start.1) | async-done | bytes 1048608 | tf_op jit(solution)/shard_map/all_to_all | solution.py:264
  171.5 4.7 %collective-permute-start.6 = (bf16[128,128]{1,0:T(8,128)(2,1)S(1)}, bf16[128,128]{1,0:T(8,128)(2,1)S(1)}, u32[]{:S(2)}, u32[]{:S(2)}) collective-permute-start(bf16[128,128]{1,0:T(8,128)(2,1)S(1)} %get-tuple-element.21), channel_id=1, source_target_pairs={{0,1},{1,0},{2,3},{3,2},{4,5},{5,4},{6,7},{7,6},{8,9},{9,8},{10,11... | collective-permute-start | bytes 98312 | tf_op jit(solution)/shard_map/ppermute | solution.py:260
  (43 shorter events, 14.8 us)
Async XLA Ops:
  0.6 53.9 %copy-start = (bf16[4096,3,128]{2,0,1:T(8,128)(2,1)S(1)}, bf16[4096,3,128]{2,0,1:T(8,128)(2,1)}, u32[]{:S(2)}) copy-start(bf16[4096,3,128]{2,0,1:T(8,128)(2,1)} %param.8) | copy-start | bytes 9437188
  0.6 49.1 %copy-start.3 = (f32[128,128]{1,0:T(8,128)S(1)}, f32[128,128]{1,0:T(8,128)}, u32[]{:S(2)}) copy-start(f32[128,128]{1,0:T(8,128)} %taps.7) | copy-start | bytes 196612
  0.7 51.0 %copy-start.6 = (s32[6144]{0:T(1024)S(1)}, s32[6144]{0:T(1024)}, u32[]{:S(2)}) copy-start(s32[6144]{0:T(1024)} %param.11) | copy-start | bytes 73732
  0.7 53.9 %collective-permute-start.2 = (bf16[3,4096,128]{2,1,0:T(8,128)(2,1)}, bf16[3,4096,128]{2,1,0:T(8,128)(2,1)}, u32[]{:S(2)}, u32[]{:S(2)}) collective-permute-start(bf16[3,4096,128]{2,1,0:T(8,128)(2,1)} %bitcast.3), channel_id=1, source_target_pairs={{0,1},{1,0},{2,3},{3,2},{4,5},{5,4},{6,7},{7,6},{8,9},{9,8},{10,11... | collective-permute-start | bytes 9437192 | tf_op jit(solution)/shard_map/ppermute | solution.py:260
  14.2 4.8 %collective-permute-start = (bf16[256,128]{1,0:T(8,128)(2,1)S(1)}, bf16[256,128]{1,0:T(8,128)(2,1)S(1)}, u32[]{:S(2)}, u32[]{:S(2)}) collective-permute-start(bf16[256,128]{1,0:T(8,128)(2,1)S(1)} %pad_maximum_fusion.1), channel_id=1, source_target_pairs={{0,1},{1,0},{2,3},{3,2},{4,5},{5,4},{6,7},{7,6},{8,9},{9,8},{10,11... | collective-permute-start | bytes 196616 | tf_op jit(solution)/shard_map/ppermute | solution.py:260
  19.8 22.1 %all-to-all-start = ((bf16[8,256,128]{2,1,0:T(8,128)(2,1)}), bf16[8,256,128]{2,1,0:T(8,128)(2,1)}, u32[]{:S(2)}, u32[]{:S(2)}) async-start(bf16[8,256,128]{2,1,0:T(8,128)(2,1)} %broadcast_in_dim.8), calls=%async_computation | async-start | bytes 1048576 | tf_op jit(solution)/shard_map/all_to_all | solution.py:256
  24.0 5.4 %collective-permute-start.7 = (bf16[256,128]{1,0:T(8,128)(2,1)S(1)}, bf16[256,128]{1,0:T(8,128)(2,1)S(1)}, u32[]{:S(2)}, u32[]{:S(2)}) collective-permute-start(bf16[256,128]{1,0:T(8,128)(2,1)S(1)} %pad_maximum_fusion.3), channel_id=1, source_target_pairs={{0,16},{16,0},{1,17},{17,1},{2,18},{18,2},{3,19},{19,3},{4,20},{20... | collective-permute-start | bytes 196616 | tf_op jit(solution)/shard_map/ppermute | solution.py:260
  43.0 33.5 %all-to-all-start.2 = ((bf16[8,512,128]{2,1,0:T(8,128)(2,1)}), bf16[8,512,128]{2,1,0:T(8,128)(2,1)}, u32[]{:S(2)}, u32[]{:S(2)}) async-start(bf16[8,512,128]{2,1,0:T(8,128)(2,1)} %broadcast_in_dim.10), calls=%async_computation.2 | async-start | bytes 2097152 | tf_op jit(solution)/shard_map/all_to_all | solution.py:256
  47.3 24.8 %collective-permute-start.5 = (bf16[128,4096]{1,0:T(8,128)(2,1)}, bf16[128,4096]{1,0:T(8,128)(2,1)}, u32[]{:S(2)}, u32[]{:S(2)}) collective-permute-start(bf16[128,4096]{1,0:T(8,128)(2,1)} %own.3), channel_id=1, source_target_pairs={{0,1},{1,0},{2,3},{3,2},{4,5},{5,4},{6,7},{7,6},{8,9},{9,8},{10,11... | collective-permute-start | bytes 3145736 | tf_op jit(solution)/shard_map/ppermute | solution.py:260
  49.7 39.3 %collective-permute-start.4 = (f32[128,128]{1,0:T(8,128)S(1)}, f32[128,128]{1,0:T(8,128)S(1)}, u32[]{:S(2)}, u32[]{:S(2)}) collective-permute-start(f32[128,128]{1,0:T(8,128)S(1)} %copy-done.3), channel_id=1, source_target_pairs={{0,1},{1,0},{2,3},{3,2},{4,5},{5,4},{6,7},{7,6},{8,9},{9,8},{10,11... | collective-permute-start | bytes 196616 | tf_op jit(solution)/shard_map/ppermute | solution.py:260
  51.8 15.2 %collective-permute-start.1 = (bf16[8,256,128]{2,1,0:T(8,128)(2,1)}, bf16[8,256,128]{2,1,0:T(8,128)(2,1)S(1)}, u32[]{:S(2)}, u32[]{:S(2)}) collective-permute-start(bf16[8,256,128]{2,1,0:T(8,128)(2,1)} %all-to-all-done.part), channel_id=1, source_target_pairs={{0,16},{16,0},{1,17},{17,1},{2,18},{18,2},{3,19},{19,3},{4,20},{20... | collective-permute-start | bytes 1572872 | tf_op jit(solution)/shard_map/ppermute | solution.py:260
  69.6 0.6 copy-start.4
  70.2 24.0 %collective-permute-start.3 = (bf16[128,256]{1,0:T(8,128)(2,1)S(1)}, bf16[128,256]{1,0:T(8,128)(2,1)}, u32[]{:S(2)}, u32[]{:S(2)}) collective-permute-start(bf16[128,256]{1,0:T(8,128)(2,1)S(1)} %get-tuple-element.16), channel_id=1, source_target_pairs={{0,1},{1,32},{32,33},{33,64},{64,65},{65,96},{96,97},{97,128},{128... | collective-permute-start | bytes 196616 | tf_op jit(solution)/shard_map/ppermute | solution.py:251
  76.5 1.2 copy-start.1
  80.4 16.7 %collective-permute-start.8 = (bf16[128,256]{1,0:T(8,128)(2,1)S(1)}, bf16[128,256]{1,0:T(8,128)(2,1)S(1)}, u32[]{:S(2)}, u32[]{:S(2)}) collective-permute-start(bf16[128,256]{1,0:T(8,128)(2,1)S(1)} %get-tuple-element.22), channel_id=1, source_target_pairs={{1,0},{32,1},{33,32},{64,33},{65,64},{96,65},{97,96},{128,97},{129... | collective-permute-start | bytes 196616 | tf_op jit(solution)/shard_map/ppermute | solution.py:251
  82.8 6.3 %copy-start.5 = (bf16[128,256]{1,0:T(8,128)(2,1)S(1)}, bf16[128,256]{1,0:T(8,128)(2,1)}, u32[]{:S(2)}) copy-start(bf16[128,256]{1,0:T(8,128)(2,1)} %copy-done.4) | copy-start | bytes 196612
  103.1 20.7 %copy-start.2 = (bf16[128,4096]{1,0:T(8,128)(2,1)S(1)}, bf16[128,4096]{1,0:T(8,128)(2,1)}, u32[]{:S(2)}) copy-start(bf16[128,4096]{1,0:T(8,128)(2,1)} %own.3) | copy-start | bytes 3145732
  103.1 15.7 %collective-permute-start.9 = (bf16[8,128,256]{2,1,0:T(8,128)(2,1)S(1)}, bf16[8,128,256]{2,1,0:T(8,128)(2,1)S(1)}, u32[]{:S(2)}, u32[]{:S(2)}) collective-permute-start(bf16[8,128,256]{2,1,0:T(8,128)(2,1)S(1)} %shard_map.89), channel_id=1, source_target_pairs={{0,16},{16,0},{1,17},{17,1},{2,18},{18,2},{3,19},{19,3},{4,20},{20... | collective-permute-start | bytes 1572872 | tf_op jit(solution)/shard_map/ppermute | solution.py:260
  119.6 22.1 %all-to-all-start.3 = ((bf16[8,128,256]{2,1,0:T(8,128)(2,1)}), bf16[8,128,256]{2,1,0:T(8,128)(2,1)}, u32[]{:S(2)}, u32[]{:S(2)}) async-start(bf16[8,128,256]{2,1,0:T(8,128)(2,1)} %add_convert_fusion), calls=%async_computation.3 | async-start | bytes 1048576 | tf_op jit(solution)/shard_map/all_to_all | solution.py:264
  141.8 29.0 %all-to-all-start.1 = ((bf16[16,128,256]{2,1,0:T(8,128)(2,1)}), bf16[16,128,256]{2,1,0:T(8,128)(2,1)S(1)}, u32[]{:S(2)}, u32[]{:S(2)}) async-start(bf16[16,128,256]{2,1,0:T(8,128)(2,1)} %shard_map.81), calls=%async_computation.1 | async-start | bytes 2097152 | tf_op jit(solution)/shard_map/all_to_all | solution.py:264
  146.6 29.6 %collective-permute-start.10 = (bf16[128,128]{1,0:T(8,128)(2,1)S(1)}, bf16[128,128]{1,0:T(8,128)(2,1)S(1)}, u32[]{:S(2)}, u32[]{:S(2)}) collective-permute-start(bf16[128,128]{1,0:T(8,128)(2,1)S(1)} %get-tuple-element.29), channel_id=1, source_target_pairs={{0,1},{1,0},{2,3},{3,2},{4,5},{5,4},{6,7},{7,6},{8,9},{9,8},{10,11... | collective-permute-start | bytes 98312 | tf_op jit(solution)/shard_map/ppermute | solution.py:260
  171.5 5.9 %collective-permute-start.6 = (bf16[128,128]{1,0:T(8,128)(2,1)S(1)}, bf16[128,128]{1,0:T(8,128)(2,1)S(1)}, u32[]{:S(2)}, u32[]{:S(2)}) collective-permute-start(bf16[128,128]{1,0:T(8,128)(2,1)S(1)} %get-tuple-element.21), channel_id=1, source_target_pairs={{0,1},{1,0},{2,3},{3,2},{4,5},{5,4},{6,7},{7,6},{8,9},{9,8},{10,11... | collective-permute-start | bytes 98312 | tf_op jit(solution)/shard_map/ppermute | solution.py:260
